TPU v7x, 768 devices: a whole 4x8x12 slice. The times are simulated.
768 devices in a mesh: grp: 24 (over z, y_lo), head: 32 (over y_hi, x, core).
Axes of the slice: x: 4, y: 8 (y_hi: 4, y_lo: 2; y = y_hi * 2 + y_lo), z: 12, core: 2. Of those that a mesh axis runs over, the one named last changes fastest.
Arguments:
- queries: bfloat16 [32, 48, 4096], P('head'), may hold values from -1500 to 1500
- shared_prefix_keys: bfloat16 [32, 3072, 512], P('head', 'grp'), may hold values from -6 to 6
- shared_prefix_values: bfloat16 [32, 3072, 512], P('head', 'grp'), may hold values from -6 to 6
- row_suffix_keys: bfloat16 [32, 48, 16, 512], P('head', 'grp'), may hold values from -6 to 6
- row_suffix_values: bfloat16 [32, 48, 16, 512], P('head', 'grp'), may hold values from -6 to 6
- suffix_lengths: int32 [32, 48], P('head', 'grp'), may hold values from 1 to 16, as said below
- residual: bfloat16 [32, 48, 2048], P('head', 'grp'), may hold values from -4 to 4
- out_weight: bfloat16 [4096, 2048], P('head'), may hold values from -0.5 to 0.5
- norm_gain: float32 [2048], replicated, may hold values from 0.5 to 2
- router_weight: bfloat16 [2048, 64], replicated, may hold values from -0.125 to 0.125
- gate_weights: bfloat16 [64, 2048, 384], P('head'), may hold values from -0.125 to 0.125
- up_weights: bfloat16 [64, 2048, 384], P('head'), may hold values from -0.125 to 0.125
- down_weights: bfloat16 [64, 384, 2048], P('head'), may hold values from -0.3125 to 0.3125
- expert_ids: int32 [32, 48, 8], P('head', 'grp'), may hold values from 0 to 63, all different within a row; in each aligned block of 2 rows (0 to 1, 2 to 3, ..., all dimensions but the last counted through in order) at most 2 rows name the same one
Outputs:
- layer_out: float32 [32, 48, 2048], P('head', 'grp')
Inputs may be any that keep to these rules, and one draw needn't show every extreme that they name: `expert_ids`: each row names 8 different experts; in each aligned block of 2 rows (the rows of one device, prompts then rows in order) no expert is named by more than 2 rows, a bound that some block reaches. `suffix_lengths`: every prompt has a row whose suffix holds 16 tokens.
All inputs are finite; a program needn't handle non-finite values.
Results may differ from a plain program's by a relative error of at most 0.007.
Values may be sent and summed in bfloat16 or wider, within the bound.
No kernel may reach another device: no remote copies, remote signals or barrier semaphores. Data moves between devices by JAX's collectives and lax.ppermute only.
A program may use at most 128 MiB of HBM per device.

v0:
```python
import math

import jax
import jax.numpy as jnp
from jax import lax
from jax.sharding import PartitionSpec as P

QUERY_HEADS = 32
KEY_VALUE_HEADS = 4
HEAD_SIZE = 128
TOPK = 8


masked_score = -1e30
norm_epsilon = 1e-06


def merged(part, axis, combine):
    gathered = jax.tree.map(lambda a: lax.all_gather(a, axis), part)

    def take(source):
        return jax.tree.map(lambda a: lax.dynamic_index_in_dim(a, source, 0, False), gathered)

    return lax.fori_loop(
        1, lax.axis_size(axis), lambda source, state: combine(state, take(source)), take(0)
    )


def join_states(earlier_state, later_state):
    peak_one, mass_one, sum_one = earlier_state
    peak_two, mass_two, sum_two = later_state
    joint_peak = jnp.maximum(peak_one, peak_two)
    keep_first = jnp.exp(peak_one - joint_peak)
    keep_second = jnp.exp(peak_two - joint_peak)
    return (
        joint_peak,
        mass_one * keep_first + mass_two * keep_second,
        sum_one * keep_first[..., None] + sum_two * keep_second[..., None],
    )


def shards(
    queries,
    shared_prefix_keys,
    shared_prefix_values,
    row_suffix_keys,
    row_suffix_values,
    suffix_lengths,
    residual,
    out_weight,
    norm_gain,
    router_weight,
    gate_weights,
    up_weights,
    down_weights,
    expert_ids,
):
    head_count = lax.axis_size("head")
    row_block = lax.axis_index("grp")
    every_row = queries.shape[1]
    prompt_own_rows = residual.shape[1]
    query_group_width = QUERY_HEADS // KEY_VALUE_HEADS
    score_scale = 1.0 / math.sqrt(HEAD_SIZE)
    heads_of_queries = queries[0].reshape(every_row, KEY_VALUE_HEADS, query_group_width, HEAD_SIZE)
    local_keys = shared_prefix_keys[0].reshape(-1, KEY_VALUE_HEADS, HEAD_SIZE)
    local_values = shared_prefix_values[0].reshape(-1, KEY_VALUE_HEADS, HEAD_SIZE)
    scores = (
        jnp.einsum(
            "rkgd,pkd->rkgp", heads_of_queries, local_keys, preferred_element_type=jnp.float32
        )
        * score_scale
    )
    row_peak = jnp.max(scores, -1)
    expo_terms = jnp.exp(scores - row_peak[..., None])
    total_mass = jnp.sum(expo_terms, -1)
    weighted = jnp.einsum(
        "rkgp,pkd->rkgd",
        expo_terms.astype(jnp.bfloat16),
        local_values,
        preferred_element_type=jnp.float32,
    )
    start_row = row_block * prompt_own_rows
    own_queries = lax.dynamic_slice_in_dim(heads_of_queries, start_row, prompt_own_rows, 0)
    suffix_key_rows = row_suffix_keys[0].reshape(prompt_own_rows, -1, KEY_VALUE_HEADS, HEAD_SIZE)
    suffix_value_rows = row_suffix_values[0].reshape(
        prompt_own_rows, -1, KEY_VALUE_HEADS, HEAD_SIZE
    )
    suf_count = suffix_key_rows.shape[1]
    in_suffix = (jnp.arange(suf_count)[None, :] < suffix_lengths[0][:, None])[:, None, None, :]
    suf_scores = (
        jnp.einsum(
            "rkgd,rskd->rkgs", own_queries, suffix_key_rows, preferred_element_type=jnp.float32
        )
        * score_scale
    )
    suf_scores = jnp.where(in_suffix, suf_scores, masked_score)
    suf_peak = jnp.max(suf_scores, -1)
    suf_terms = jnp.where(in_suffix, jnp.exp(suf_scores - suf_peak[..., None]), 0.0)
    suf_mass = jnp.sum(suf_terms, -1)
    suf_weighted = jnp.einsum(
        "rkgs,rskd->rkgd",
        suf_terms.astype(jnp.bfloat16),
        suffix_value_rows,
        preferred_element_type=jnp.float32,
    )
    own_state = (
        lax.dynamic_slice_in_dim(row_peak, start_row, prompt_own_rows, 0),
        lax.dynamic_slice_in_dim(total_mass, start_row, prompt_own_rows, 0),
        lax.dynamic_slice_in_dim(weighted, start_row, prompt_own_rows, 0),
    )
    own_peak, own_mass, own_weighted = join_states(own_state, (suf_peak, suf_mass, suf_weighted))
    row_peak = lax.dynamic_update_slice_in_dim(row_peak, own_peak, start_row, 0).reshape(
        every_row, QUERY_HEADS
    )
    total_mass = lax.dynamic_update_slice_in_dim(total_mass, own_mass, start_row, 0).reshape(
        every_row, QUERY_HEADS
    )
    weighted = lax.dynamic_update_slice_in_dim(weighted, own_weighted, start_row, 0).reshape(
        every_row, QUERY_HEADS, HEAD_SIZE
    )
    all_peak, all_mass, all_weighted = merged((row_peak, total_mass, weighted), "grp", join_states)
    all_attn = all_weighted / all_mass[..., None]
    mine_rows = lax.dynamic_slice_in_dim(all_attn, start_row, prompt_own_rows, 0).astype(
        jnp.bfloat16
    )
    mine = lax.all_to_all(mine_rows[None], "head", split_axis=2, concat_axis=0, tiled=True)
    flat_attn = mine.reshape(head_count * prompt_own_rows, -1)
    projected = lax.psum_scatter(
        jnp.dot(flat_attn, out_weight, preferred_element_type=jnp.float32),
        "head",
        scatter_dimension=0,
        tiled=True,
    )
    hidden_state = residual[0].astype(jnp.float32) + projected
    mean_square = jnp.mean(hidden_state * hidden_state, -1, keepdims=True)
    normed = (hidden_state * lax.rsqrt(mean_square + norm_epsilon) * norm_gain).astype(jnp.bfloat16)
    logits = jnp.dot(normed, router_weight, preferred_element_type=jnp.float32)
    experts_all = router_weight.shape[1]
    capacity = max(2, prompt_own_rows * TOPK * 2 // experts_all)
    chosen_ids = expert_ids[0]
    is_chosen = chosen_ids[..., None] == jnp.arange(experts_all, dtype=jnp.int32)
    chosen_logits = jnp.sum(jnp.where(is_chosen, logits[:, None, :], 0.0), -1)
    chosen_expo = jnp.exp(chosen_logits)
    route_weights = chosen_expo / jnp.sum(chosen_expo, -1, keepdims=True)
    flat_match = is_chosen.reshape(prompt_own_rows * TOPK, experts_all).astype(jnp.int32)
    earlier = jnp.cumsum(flat_match, 0) - flat_match
    slot_index = jnp.sum(earlier * flat_match, -1).reshape(prompt_own_rows, TOPK)
    target_slot = chosen_ids * capacity + slot_index
    place_map = jnp.any(
        target_slot[..., None] == jnp.arange(experts_all * capacity, dtype=jnp.int32), 1
    ).astype(jnp.bfloat16)
    buffer = jnp.einsum("rs,rd->sd", place_map, normed, preferred_element_type=jnp.float32).astype(
        jnp.bfloat16
    )
    buffer = buffer.reshape(head_count, -1, buffer.shape[1])
    arrived = lax.all_to_all(buffer, "head", split_axis=0, concat_axis=0, tiled=True)
    local_experts = gate_weights.shape[0]
    arrived = arrived.reshape(head_count, local_experts, capacity, -1)
    gate_out = jnp.einsum(
        "secd,edf->secf", arrived, gate_weights, preferred_element_type=jnp.float32
    )
    up_out = jnp.einsum("secd,edf->secf", arrived, up_weights, preferred_element_type=jnp.float32)
    inner_act = (jax.nn.silu(gate_out) * up_out).astype(jnp.bfloat16)
    produced = jnp.einsum(
        "secf,efd->secd", inner_act, down_weights, preferred_element_type=jnp.float32
    ).astype(jnp.bfloat16)
    produced = produced.reshape(head_count, local_experts * capacity, -1)
    returned = lax.all_to_all(produced, "head", split_axis=0, concat_axis=0, tiled=True)
    returned = returned.reshape(experts_all * capacity, -1)
    gathered = (
        returned[target_slot.reshape(-1)].reshape(prompt_own_rows, TOPK, -1).astype(jnp.float32)
    )
    routed_sum = jnp.sum(route_weights[..., None] * gathered, 1)
    layer_out = hidden_state + routed_sum
    return layer_out[None]


def solution(mesh):
    return jax.shard_map(
        shards,
        mesh=mesh,
        in_specs=(
            P("head", None, None),
            P("head", "grp", None),
            P("head", "grp", None),
            P("head", "grp", None, None),
            P("head", "grp", None, None),
            P("head", "grp"),
            P("head", "grp", None),
            P("head", None),
            P(),
            P(),
            P("head", None, None),
            P("head", None, None),
            P("head", None, None),
            P("head", "grp", None),
        ),
        out_specs=P("head", "grp", None),
        check_vma=False,
    )
```

profile of v0, /device:TPU:1, one launch (start us, length us, event | category | flops | bytes accessed | tf_op | source)
XLA Modules:
  0.0 942.7 jit_solution(1607729450265558665)
XLA Ops:
  6.5 1.2 copy.149
  7.8 1.3 iota_compare_fusion.3
  9.1 1.4 reshape_squeeze.17
  10.4 1.6 reshape_squeeze.15
  12.0 1.4 fusion.59
  13.4 1.0 fusion.30
  15.7 1.4 copy.148
  17.1 1.4 copy.147
  18.5 1.0 fusion.60
  21.0 0.9 reshape_squeeze.18
  22.0 1.3 fusion.32
  23.2 0.9 copy-done.2
  25.0 1.5 fusion.26
  26.5 2.1 copy.171
  29.0 71.6 %all_gather.10 = f32[24,48,32]{1,2,0:T(8,128)S(1)} all-gather(f32[1,48,32]{1,2,0:T(8,128)S(1)} %bitcast.146), channel_id=1, replica_groups=mesh['grp'=24,'head'=32] {'grp'}, dimensions={0}, use_global_device_ids=true | all-gather | bytes 153600 | tf_op jit(solution)/shard_map/all_gather | solution.py:19
  101.7 51.5 %all_gather.9 = f32[24,48,32]{1,2,0:T(8,128)S(1)} all-gather(f32[1,48,32]{1,2,0:T(8,128)S(1)} %bitcast.145), channel_id=1, replica_groups=mesh['grp'=24,'head'=32] {'grp'}, dimensions={0}, use_global_device_ids=true | all-gather | bytes 153600 | tf_op jit(solution)/shard_map/all_gather | solution.py:19
  154.1 303.7 %all-gather.2.cloned.1.call-done = f32[24,48,32,128]{3,2,1,0:T(8,128)} async-done(((f32[1,48,32,128]{3,2,1,0:T(8,128)}), f32[24,48,32,128]{3,2,1,0:T(8,128)}) %all-gather.2.cloned.1.call-update) | async-done | bytes 18874384 | tf_op jit(solution)/shard_map/all_gather | solution.py:19
  457.8 2.1 slice_bitcast_fusion
  459.9 85.5 %while.19 = (s32[]{:T(128)}, f32[48,32]{1,0:T(8,128)S(1)}, f32[48,32]{1,0:T(8,128)S(1)}, f32[48,32,128]{2,1,0:T(8,128)}, f32[24,48,32]{1,2,0:T(8,128)}, /*index=...) while((s32[]{:T(128)}, f32[48,32]{1,0:T(8,128)S(1)}, ...), condition=%wide.region_5.6_spmd, body=%wide.region_4.5_spmd.sunk | while | flops 599045 | bytes 2470039 | solution.py:24
  460.8 2.8 fusion.71
  464.6 2.8 fusion.71
  468.3 2.8 fusion.71
  472.0 2.8 fusion.71
  475.7 2.8 fusion.71
  479.4 2.8 fusion.71
  483.1 2.8 fusion.71
  486.9 2.8 fusion.71
  490.6 2.8 fusion.71
  494.3 2.8 fusion.71
  498.0 2.8 fusion.71
  501.7 2.8 fusion.71
  505.4 2.8 fusion.71
  509.2 2.8 fusion.71
  512.9 2.8 fusion.71
  516.6 2.8 fusion.71
  520.3 2.8 fusion.71
  524.0 2.8 fusion.71
  527.8 2.8 fusion.71
  531.5 2.8 fusion.71
  535.2 2.8 fusion.71
  538.9 2.8 fusion.71
  542.6 2.8 fusion.71
  545.4 2.5 copy.129
  548.1 1.6 fusion.51
  549.7 11.2 %all-to-all-start = ((bf16[1,2,32,128]{3,1,0,2:T(2,128)(2,1)}), bf16[1,2,32,128]{3,1,0,2:T(2,128)(2,1)S(1)}, u32[]{:S(2)}, u32[]{:S(2)}) async-start(bf16[1,2,32,128]{3,1,0,2:T(2,128)(2,1)} %fusion.51), calls=%async_computation | async-start | bytes 32768 | tf_op jit(solution)/shard_map/all_to_all | solution.py:126
  561.1 9.2 all-to-all-done
  570.2 2.1 fusion.61
  572.7 1.3 dynamic-slice.4
  574.7 290.4 %all-reduce.3.cloned.1.call-done = f32[64,2048]{1,0:T(8,128)} async-done(((f32[64,2048]{1,0:T(8,128)}), f32[64,2048]{1,0:T(8,128)}) %all-reduce.3.cloned.1.call-update) | async-done | bytes 524304
  865.2 1.0 multiply_reduce_fusion
  866.2 2.0 convolution_convert_fusion
  868.2 2.0 reshape.126
  870.2 8.1 all-to-all-start.1
  878.4 18.3 %all-to-all-done.1 = bf16[32,4,2048]{2,1,0:T(4,128)(2,1)} async-done(((bf16[32,4,2048]{2,1,0:T(4,128)(2,1)}), bf16[32,4,2048]{2,1,0:T(4,128)(2,1)}, u32[]{:S(2)}, u32[]{:S(2)}) %all-to-all-start.1) | async-done | bytes 524320 | tf_op jit(solution)/shard_map/all_to_all | solution.py:156
  896.7 1.3 copy.130
  898.8 2.5 fusion.13
  901.3 4.0 fusion.9
  905.4 2.3 copy.131
  907.6 4.9 all-to-all-start.2
  912.5 1.2 fusion.57
  914.1 16.4 %all-to-all-done.2 = bf16[32,4,2048]{2,1,0:T(4,128)(2,1)} async-done(((bf16[32,4,2048]{2,1,0:T(4,128)(2,1)}), bf16[32,4,2048]{2,1,0:T(4,128)(2,1)}, u32[]{:S(2)}, u32[]{:S(2)}) %all-to-all-start.2) | async-done | bytes 524320 | tf_op jit(solution)/shard_map/all_to_all | solution.py:168
  930.6 2.0 reshape.129
  932.5 1.8 gather_fusion
  934.4 1.5 add_bitcast_fusion
  (150 shorter events, 29.3 us)
Async XLA Ops:
  6.5 894.8 %copy-start = (bf16[2,384,2048]{2,1,0:T(8,128)(2,1)S(1)}, bf16[2,384,2048]{2,1,0:T(8,128)(2,1)}, u32[]{:S(2)}) copy-start(bf16[2,384,2048]{2,1,0:T(8,128)(2,1)} %param.28) | copy-start | bytes 9437188
  6.5 451.3 %all-gather.2.cloned.1.call-start = ((), (), s32[]{:S(2)}) async-start(), calls=%async_computation.3 | async-start | bytes 19660800 | tf_op jit(solution)/shard_map/all_gather | solution.py:19
  14.4 0.6 copy-start.5
  19.4 5.6 copy-start.8
  19.4 9.4 copy-start.6
  23.2 0.9 copy-start.2
  100.6 0.7 copy-start.3
  153.2 0.8 copy-start.4
  459.9 101.1 %copy-start.9 = (s32[1,2,8]{2,1,0:T(2,128)S(1)}, s32[1,2,8]{2,1,0:T(2,128)}, u32[]{:S(2)}) copy-start(s32[1,2,8]{2,1,0:T(2,128)} %param.29) | copy-start | bytes 196
  545.4 319.8 %copy-start.7 = (bf16[1,2,2048]{2,1,0:T(2,128)(2,1)S(1)}, bf16[1,2,2048]{2,1,0:T(2,128)(2,1)}, u32[]{:S(2)}) copy-start(bf16[1,2,2048]{2,1,0:T(2,128)(2,1)} %param.22) | copy-start | bytes 24580
  545.4 320.7 %copy-start.10 = (f32[2048]{0:T(1024)S(1)}, f32[2048]{0:T(1024)}, u32[]{:S(2)}) copy-start(f32[2048]{0:T(1024)} %param.24) | copy-start | bytes 24580
  549.7 20.6 %all-to-all-start = ((bf16[1,2,32,128]{3,1,0,2:T(2,128)(2,1)}), bf16[1,2,32,128]{3,1,0,2:T(2,128)(2,1)S(1)}, u32[]{:S(2)}, u32[]{:S(2)}) async-start(bf16[1,2,32,128]{3,1,0,2:T(2,128)(2,1)} %fusion.51), calls=%async_computation | async-start | bytes 32768 | tf_op jit(solution)/shard_map/all_to_all | solution.py:126
  560.9 304.2 %all-reduce.3.cloned.1.call-start = ((), (), s32[]{:S(2)}) async-start(), calls=%async_computation.4 | async-start | bytes 1048576
  870.2 26.5 %all-to-all-start.1 = ((bf16[32,4,2048]{2,1,0:T(4,128)(2,1)}), bf16[32,4,2048]{2,1,0:T(4,128)(2,1)}, u32[]{:S(2)}, u32[]{:S(2)}) async-start(bf16[32,4,2048]{2,1,0:T(4,128)(2,1)} %reshape.126), calls=%async_computation.1 | async-start | bytes 1048576 | tf_op jit(solution)/shard_map/all_to_all | solution.py:156
  898.0 0.8 copy-start.1
  907.6 22.9 %all-to-all-start.2 = ((bf16[32,4,2048]{2,1,0:T(4,128)(2,1)}), bf16[32,4,2048]{2,1,0:T(4,128)(2,1)}, u32[]{:S(2)}, u32[]{:S(2)}) async-start(bf16[32,4,2048]{2,1,0:T(4,128)(2,1)} %copy.131), calls=%async_computation.2 | async-start | bytes 1048576 | tf_op jit(solution)/shard_map/all_to_all | solution.py:168
Sparse Core Ops, SparseCore 0:
  28.8 428.9 all-gather.1
  572.5 292.6 all-reduce.2
where the time goes:
time: 948 us; the launch traced here: 943 us
  waiting for transfers between devices  638 us (67%)
  blocking collectives  123 us (13%)
  other arithmetic  73.7 us (8%)
  local copies, waits for them, and re-layouts  52.2 us (6%)
  starting transfers between devices  24.2 us (3%)
  matrix products  16.9 us (2%)
  between operations  14.3 us (2%)
    all_gather x1, waiting for transfers between devices, merged(): gathered = jax.tree.map(lambda a: lax.all_gather(a, axis), part)  304 us
    unnamed x3, waiting for transfers between devices  290 us
    all_gather x2, blocking collectives, merged(): gathered = jax.tree.map(lambda a: lax.all_gather(a, axis), part)  123 us
    add x23, other arithmetic, join_states(): sum_one * keep_first[..., None] + sum_two * keep_second[..., None]  64.1 us
    dynamic_slice x69, local copies, waits for them, and re-layouts, take(): lax.dynamic_index_in_dim(a, source, 0, False)  20.5 us
  transfers between devices with their start and end apart: 5, of which 5 were waited for; matrix products, arithmetic and copies ran while one was open for 0% of the time, Pallas kernels for 0%

commit v1 on v0

v1 whole, which is shorter than its diff:
```python
import math

import jax
import jax.numpy as jnp
from jax import lax
from jax.sharding import PartitionSpec as P

QUERY_HEADS = 32
KEY_VALUE_HEADS = 4
HEAD_SIZE = 128
TOPK = 8
GROUP = QUERY_HEADS // KEY_VALUE_HEADS

masked_score = -1e30
norm_epsilon = 1e-06
f32 = jnp.float32
bf16 = jnp.bfloat16


def rounded(x):
    return lax.reduce_precision(x, 8, 7)


def two_pieces(x):
    high = rounded(x)
    return high, rounded(x - high)


def exchange(x, axis):
    return lax.all_to_all(x, axis, split_axis=0, concat_axis=0, tiled=True)


def shards(
    queries,
    shared_prefix_keys,
    shared_prefix_values,
    row_suffix_keys,
    row_suffix_values,
    suffix_lengths,
    residual,
    out_weight,
    norm_gain,
    router_weight,
    gate_weights,
    up_weights,
    down_weights,
    expert_ids,
):
    head_count = lax.axis_size("head")
    grp_count = lax.axis_size("grp")
    row_block = lax.axis_index("grp")
    every_row = queries.shape[1]
    own_rows = residual.shape[1]
    width = residual.shape[2]
    score_scale = 1.0 / math.sqrt(HEAD_SIZE)
    q = queries[0].reshape(every_row, KEY_VALUE_HEADS, GROUP, HEAD_SIZE)
    k = shared_prefix_keys[0].reshape(-1, KEY_VALUE_HEADS, HEAD_SIZE)
    v = shared_prefix_values[0].reshape(-1, KEY_VALUE_HEADS, HEAD_SIZE)
    scores = jnp.einsum("rkgd,pkd->rkgp", q, k, preferred_element_type=f32) * score_scale
    m_high, m_low = two_pieces(jnp.max(scores, -1))
    terms = jnp.exp(scores - (m_high + m_low)[..., None])
    s_high, s_low = two_pieces(jnp.sum(terms, -1))
    weighted = jnp.einsum("rkgp,pkd->rkgd", terms.astype(bf16), v, preferred_element_type=f32)
    values = weighted.astype(bf16).reshape(grp_count, own_rows * QUERY_HEADS, HEAD_SIZE)
    stats = jnp.stack([m_high, m_low, s_high, s_low]).astype(bf16)
    stats = stats.reshape(4, grp_count, own_rows * QUERY_HEADS).transpose(1, 0, 2)
    stats = jnp.pad(stats, ((0, 0), (0, 4), (0, HEAD_SIZE - own_rows * QUERY_HEADS)))
    arrived = exchange(jnp.concatenate([values, stats], 1), "grp")

    own_q = lax.dynamic_slice_in_dim(q, row_block * own_rows, own_rows, 0)
    suf_k = row_suffix_keys[0].reshape(own_rows, -1, KEY_VALUE_HEADS, HEAD_SIZE)
    suf_v = row_suffix_values[0].reshape(own_rows, -1, KEY_VALUE_HEADS, HEAD_SIZE)
    inside = (jnp.arange(suf_k.shape[1])[None, :] < suffix_lengths[0][:, None])[:, None, None, :]
    suf_scores = jnp.einsum("rkgd,rskd->rkgs", own_q, suf_k, preferred_element_type=f32)
    suf_scores = jnp.where(inside, suf_scores * score_scale, masked_score)
    suf_m = jnp.max(suf_scores, -1)
    suf_terms = jnp.where(inside, jnp.exp(suf_scores - suf_m[..., None]), 0.0)
    suf_s = jnp.sum(suf_terms, -1)
    suf_o = jnp.einsum(
        "rkgs,rskd->rkgd", suf_terms.astype(bf16), suf_v, preferred_element_type=f32
    )
    suf_m = suf_m.reshape(1, -1)
    suf_s = suf_s.reshape(1, -1)
    suf_o = suf_o.reshape(-1, HEAD_SIZE)

    n = own_rows * QUERY_HEADS
    parts = arrived[:, n : n + 4, :n].astype(f32)
    part_m = parts[:, 0] + parts[:, 1]
    part_s = parts[:, 2] + parts[:, 3]
    top = jnp.maximum(jnp.max(part_m, 0, keepdims=True), suf_m)
    scale = jnp.exp(part_m - top)
    suf_scale = jnp.exp(suf_m - top)
    mass = jnp.sum(scale * part_s, 0) + (suf_scale * suf_s)[0]
    total = jnp.sum(scale[..., None] * arrived[:, :n].astype(f32), 0) + suf_scale[0][:, None] * suf_o
    attn = (total / mass[:, None]).astype(bf16).reshape(own_rows, QUERY_HEADS, HEAD_SIZE)

    ids_row = jnp.pad(expert_ids[0].astype(bf16).reshape(1, 1, -1), ((0, 0), (0, 0), (0, HEAD_SIZE - own_rows * TOPK)))
    ids_row = jnp.broadcast_to(ids_row, (head_count, 1, HEAD_SIZE))
    arrived = exchange(jnp.concatenate([attn.transpose(1, 0, 2), ids_row], 1), "head")
    every_id = arrived[:, own_rows, : own_rows * TOPK].reshape(head_count * own_rows, TOPK)
    flat_attn = arrived[:, :own_rows].reshape(head_count * own_rows, HEAD_SIZE)
    partial = jnp.dot(flat_attn, out_weight, preferred_element_type=f32).astype(bf16)
    partial = exchange(partial.reshape(head_count, own_rows, width), "head")
    hidden = residual[0].astype(f32) + jnp.sum(partial.astype(f32), 0)
    mean_square = jnp.mean(hidden * hidden, -1, keepdims=True)
    normed = (hidden * lax.rsqrt(mean_square + norm_epsilon) * norm_gain).astype(bf16)

    x = exchange(jnp.broadcast_to(normed[None], (head_count, own_rows, width)), "head")
    x = x.reshape(head_count * own_rows, width)
    logits = jnp.dot(x, router_weight, preferred_element_type=f32)
    experts_all = router_weight.shape[1]
    local_experts = gate_weights.shape[0]
    expert_range = jnp.arange(experts_all, dtype=jnp.int32).astype(bf16)
    chosen = jnp.any(every_id[..., None] == expert_range, 1)
    expo = jnp.where(chosen, jnp.exp(logits), 0.0)
    route = expo / jnp.sum(expo, -1, keepdims=True)
    first = lax.axis_index("head") * local_experts
    own_route = lax.dynamic_slice_in_dim(route, first, local_experts, 1)
    gate_out = jnp.einsum("rd,edf->erf", x, gate_weights, preferred_element_type=f32)
    up_out = jnp.einsum("rd,edf->erf", x, up_weights, preferred_element_type=f32)
    act = (jax.nn.silu(gate_out) * up_out).astype(bf16)
    produced = jnp.einsum("erf,efd->erd", act, down_weights, preferred_element_type=f32)
    produced = produced.astype(bf16).astype(f32)
    mixed = jnp.sum(own_route.T[..., None] * produced, 0).astype(bf16)
    returned = exchange(mixed.reshape(head_count, own_rows, width), "head")
    return (hidden + jnp.sum(returned.astype(f32), 0))[None]


def solution(mesh):
    return jax.shard_map(
        shards,
        mesh=mesh,
        in_specs=(
            P("head", None, None),
            P("head", "grp", None),
            P("head", "grp", None),
            P("head", "grp", None, None),
            P("head", "grp", None, None),
            P("head", "grp"),
            P("head", "grp", None),
            P("head", None),
            P(),
            P(),
            P("head", None, None),
            P("head", None, None),
            P("head", None, None),
            P("head", "grp", None),
        ),
        out_specs=P("head", "grp", None),
        check_vma=False,
    )
```

time: 948 us -> 151 us (0.16)
  waiting for transfers between devices: 638 us -> 26.4 us
  blocking collectives: 123 us -> 56.2 us
  other arithmetic: 73.7 us -> 11.4 us
  local copies, waits for them, and re-layouts: 52.2 us -> 19.2 us
  between operations: 14.3 us -> 0.18 us
    all_gather x1 -> x0, waiting for transfers between devices: 304 us -> none  [merged(): gathered = jax.tree.map(lambda a: lax.all_gather(a, axis), part)]
    unnamed x3 -> x0, waiting for transfers between devices: 290 us -> none
    all_gather x2 -> x0, blocking collectives: 123 us -> none  [merged(): gathered = jax.tree.map(lambda a: lax.all_gather(a, axis), part)]
    add x48 -> x3, other arithmetic: 65.6 us -> 1.24 us  [the longest x1 0.62 us: shards(): return (hidden + jnp.sum(returned.astype(f32), 0))[None]]
    all_to_all x0 -> x3, blocking collectives: none -> 56.2 us  [exchange(): return lax.all_to_all(x, axis, split_axis=0, concat_axis=0, tiled=True)]
    dynamic_slice x71 -> x0, local copies, waits for them, and re-layouts: 21.2 us -> none  [the longest x69 20.5 us: take(): lax.dynamic_index_in_dim(a, source, 0, False)]
    all_to_all x3 -> x2, waiting for transfers between devices: 43.9 us -> 26.4 us  [exchange(): return lax.all_to_all(x, axis, split_axis=0, concat_axis=0, tiled=True)]
    all_to_all x3 -> x2, starting transfers between devices: 24.2 us -> 21.4 us  [exchange(): return lax.all_to_all(x, axis, split_axis=0, concat_axis=0, tiled=True)]
  transfers between devices with their start and end apart: 5 -> 2, of which waited for: 5 -> 2; matrix products, arithmetic and copies ran while one was open for 0% -> 4% of each run, Pallas kernels for 0% -> 0%
where the time goes in v1:
time: 151 us; the launch traced here: 150 us
  blocking collectives  56.2 us (37%)
  waiting for transfers between devices  26.4 us (17%)
  starting transfers between devices  21.4 us (14%)
  local copies, waits for them, and re-layouts  19.2 us (13%)
  matrix products  15.2 us (10%)
  other arithmetic  11.4 us (8%)
    all_to_all x3, blocking collectives, exchange(): return lax.all_to_all(x, axis, split_axis=0, concat_axis=0, tiled=True)  56.2 us
    all_to_all x2, waiting for transfers between devices, exchange(): return lax.all_to_all(x, axis, split_axis=0, concat_axis=0, tiled=True)  26.4 us
    all_to_all x2, starting transfers between devices, exchange(): return lax.all_to_all(x, axis, split_axis=0, concat_axis=0, tiled=True)  21.4 us
    dot_general x1, matrix products, shards(): jnp.einsum('erf,efd->erd', act, down_weights, preferred_element_type=f32)  3.78 us
    dot_general x1, matrix products, shards(): jnp.einsum('rd,edf->erf', x, gate_weights, preferred_element_type=f32)  3.21 us
    reduce_sum x2, local copies, waits for them, and re-layouts, shards(): s_high, s_low = two_pieces(jnp.sum(terms, -1))  3.03 us
  transfers between devices with their start and end apart: 2, of which 2 were waited for; matrix products, arithmetic and copies ran while one was open for 4% of the time, Pallas kernels for 0%

profile of v1, /device:TPU:1, one launch (start us, length us, event | category | flops | bytes accessed | tf_op | source)
XLA Modules:
  0.0 149.9 jit_solution(6376651965969771326)
XLA Ops:
  0.0 0.0 copy-start
  0.0 1.7 %reshape_squeeze.15 = bf16[128,4,128]{2,1,0:T(4,128)(2,1)} reshape(bf16[1,128,512]{2,1,0:T(8,128)(2,1)} %param.15) | data formatting | bytes 262144 | tf_op jit(solution)/shard_map/reshape;squeeze | solution.py:57
  1.7 1.1 copy.146
  2.8 2.1 %fusion.55 = (f32[48,4,8]{0,2,1:T(8,128)S(1)}, f32[48,4,8,128]{3,0,2,1:T(8,128)}) fusion(bf16[48,4,8,128]{3,2,1,0:T(8,128)(2,1)S(1)} %bitcast.85, bf16[128,4,128,1]{2,1,0,3:T(4,128)(2,1)} %bitcast.89), kind=kOutput, calls=%fused_computation.93 | convolution fusion | flops 50723328 | bytes 1316864 | tf_op jit(solution)/shard_map/rkgd,pkd->rkgp/dot_general | solution.py:59
  4.9 0.6 reduce-precision_add_fusion
  5.5 0.7 copy.127
  6.2 0.0 copy-start.2
  6.2 1.6 %reshape_squeeze.17 = bf16[128,4,128]{2,1,0:T(4,128)(2,1)} reshape(bf16[1,128,512]{2,1,0:T(8,128)(2,1)} %param.16) | data formatting | bytes 262144 | tf_op jit(solution)/shard_map/reshape;squeeze | solution.py:58
  7.8 2.3 %fusion.16 = (bf16[48,4,8,128]{3,0,2,1:T(8,128)(2,1)S(1)}, f32[48,4,8]{0,2,1:T(8,128)}) fusion(f32[48,4,8,128]{3,0,2,1:T(8,128)} %get-tuple-element.19, f32[48,4,8]{0,2,1:T(8,128)} %reduce-precision_add_fusion), kind=kLoop, calls=%fused_computation.28 | loop fusion | flops 588288 | bytes 1191936 | tf_op jit(solution)/shard_map/convert_element_type | solution.py:63
  10.1 1.2 fusion.4
  11.3 0.0 copy-start.1
  11.3 0.8 copy.126
  12.1 1.6 %reduce_max.32 = f32[1,24,64]{2,1,0:T(8,128)} reshape(f32[48,4,8]{2,1,0:T(4,128)} %copy.127) | data formatting | bytes 12288 | tf_op jit(solution)/shard_map/reduce_max | solution.py:60
  13.7 1.4 copy.128
  15.1 1.6 %reduce_sum.92 = f32[1,24,64]{2,1,0:T(8,128)} reshape(f32[48,4,8]{2,1,0:T(4,128)} %copy.128) | data formatting | bytes 12288 | tf_op jit(solution)/shard_map/reduce_sum | solution.py:62
  16.7 0.7 reduce-precision_convert_fusion
  17.5 1.8 %fusion.17 = bf16[24,72,128]{2,1,0:T(8,128)(2,1)} fusion(bf16[24,4,64]{2,1,0:T(4,128)(2,1)S(1)} %copy.145, bf16[24,64,128]{2,1,0:T(8,128)(2,1)} %bitcast.87), kind=kLoop, calls=%fused_computation.31 | loop fusion | flops 1327104 | bytes 847872 | tf_op jit(solution)/shard_map/concatenate | solution.py:68
  19.3 17.0 %all-to-all-start = ((bf16[24,72,128]{2,1,0:T(8,128)(2,1)}), bf16[24,72,128]{2,1,0:T(8,128)(2,1)}, u32[]{:S(2)}, u32[]{:S(2)}) async-start(bf16[24,72,128]{2,1,0:T(8,128)(2,1)} %fusion.17), calls=%async_computation | async-start | bytes 884736 | tf_op jit(solution)/shard_map/all_to_all | solution.py:30
  36.3 1.4 reshape_squeeze.18
  37.7 0.0 copy-done.2
  37.7 0.1 iota_compare_fusion.1
  37.8 1.5 fusion.56
  39.3 0.1 reshape.251
  39.4 0.1 reshape.252
  39.5 0.7 convert_element_type.95
  40.1 0.1 convert_element_type.96
  40.2 0.8 reshape_squeeze.19
  41.0 0.9 fusion.30
  41.9 0.1 reshape.254
  42.0 13.7 %all-to-all-done = bf16[24,72,128]{2,1,0:T(8,128)(2,1)} async-done(((bf16[24,72,128]{2,1,0:T(8,128)(2,1)}), bf16[24,72,128]{2,1,0:T(8,128)(2,1)}, u32[]{:S(2)}, u32[]{:S(2)}) %all-to-all-start) | async-done | bytes 442400 | tf_op jit(solution)/shard_map/all_to_all | solution.py:30
  55.7 0.8 slice_convert_fusion
  56.6 0.1 reduce_max.35
  56.7 0.1 reduce_sum.96
  56.8 1.3 multiply_reduce_fusion
  58.1 1.0 fusion.13
  59.1 21.5 %all_to_all.25 = bf16[32,3,128]{2,1,0:T(4,128)(2,1)S(1)} all-to-all(bf16[32,3,128]{2,1,0:T(4,128)(2,1)S(1)} %copy.134), channel_id=1, replica_groups=mesh['grp'=24,'head'=32] {'head'}, dimensions={0} | all-to-all | bytes 49152 | tf_op jit(solution)/shard_map/all_to_all | solution.py:30
  80.6 1.3 convolution_convert_fusion.1
  81.8 0.9 reshape.256
  82.7 17.8 %all_to_all.26 = bf16[32,2,2048]{2,1,0:T(2,128)(2,1)S(1)} all-to-all(bf16[32,2,2048]{2,1,0:T(2,128)(2,1)} %reshape.256), channel_id=1, replica_groups=mesh['grp'=24,'head'=32] {'head'}, dimensions={0} | all-to-all | bytes 524288 | tf_op jit(solution)/shard_map/all_to_all | solution.py:30
  100.5 0.2 convert_reduce_fusion.1
  100.8 0.0 copy-done.1
  100.8 0.1 fusion.34
  100.9 0.8 fusion.46
  101.7 0.8 broadcast_in_dim.56
  102.5 4.4 %all-to-all-start.3 = ((bf16[32,2,2048]{2,1,0:T(2,128)(2,1)}), bf16[32,2,2048]{2,1,0:T(2,128)(2,1)}, u32[]{:S(2)}, u32[]{:S(2)}) async-start(bf16[32,2,2048]{2,1,0:T(2,128)(2,1)} %broadcast_in_dim.56), calls=%async_computation.3 | async-start | bytes 524288 | tf_op jit(solution)/shard_map/all_to_all | solution.py:30
  106.9 0.1 slice_reduce_fusion
  107.0 0.1 eq.15
  107.1 0.2 compare_reduce_fusion
  107.2 0.1 copy.135
  107.3 12.7 %all-to-all-done.3 = bf16[32,2,2048]{2,1,0:T(2,128)(2,1)} async-done(((bf16[32,2,2048]{2,1,0:T(2,128)(2,1)}), bf16[32,2,2048]{2,1,0:T(2,128)(2,1)}, u32[]{:S(2)}, u32[]{:S(2)}) %all-to-all-start.3) | async-done | bytes 262176 | tf_op jit(solution)/shard_map/all_to_all | solution.py:30
  120.0 1.0 reshape.261
  121.1 3.2 %convolution_bitcast_fusion.1 = f32[2,64,384]{2,1,0:T(8,128)} fusion(bf16[64,2048,1]{1,0,2:T(8,128)(2,1)S(1)} %reshape.261, bf16[2,2048,384]{2,1,0:T(8,128)(2,1)} %param.24), kind=kOutput, calls=%fused_computation.11 | convolution fusion | flops 201326592 | bytes 3604480 | tf_op jit(solution)/shard_map/rd,edf->erf/dot_general | solution.py:119
  124.3 1.7 %reshape.257 = bf16[64,2048]{1,0:T(8,128)(2,1)} reshape(bf16[32,2,2048]{2,1,0:T(2,128)(2,1)} %all-to-all-done.3) | data formatting | bytes 524288 | tf_op jit(solution)/shard_map/reshape | solution.py:109
  126.0 1.3 fusion.57
  127.3 0.0 copy-done
  127.3 3.8 %fusion.2 = bf16[64,2048]{1,0:T(8,128)(2,1)} fusion(bf16[2,384,2048]{2,1,0:T(8,128)(2,1)S(1)} %copy-done, bf16[64,2048,1]{1,0,2:T(8,128)(2,1)S(1)} %reshape.261, bf16[2,2048,384]{2,1,0:T(8,128)(2,1)} %param.25, f32[2,64]{1,0:T(2,128)S(1)} %fusion.48, f32[2,64,384]{2,1,0:T(8,128)} %convolution_bitcast_fusion.1), kind=kOutput, calls=%fused_computation.4 | convolution fusion | flops 403865600 | bytes 7012864 | tf_op jit(solution)/shard_map/erf,efd->erd/dot_general | solution.py:122
  131.1 1.1 convert_element_type.107
  132.2 16.9 %all_to_all.27 = bf16[32,2,2048]{2,1,0:T(2,128)(2,1)S(1)} all-to-all(bf16[32,2,2048]{2,1,0:T(2,128)(2,1)S(1)} %convert_element_type.107), channel_id=1, replica_groups=mesh['grp'=24,'head'=32] {'head'}, dimensions={0} | all-to-all | bytes 524288 | tf_op jit(solution)/shard_map/all_to_all | solution.py:30
  149.2 0.1 convert_reduce_fusion
  149.3 0.6 bitcast_add_fusion
  (15 shorter events, 0.2 us)
Async XLA Ops:
  0.0 127.3 %copy-start = (bf16[2,384,2048]{2,1,0:T(8,128)(2,1)S(1)}, bf16[2,384,2048]{2,1,0:T(8,128)(2,1)}, u32[]{:S(2)}) copy-start(bf16[2,384,2048]{2,1,0:T(8,128)(2,1)} %param.26) | copy-start | bytes 9437188
  6.2 31.5 %copy-start.2 = (s32[1,2]{1,0:T(1,128)S(1)}, s32[1,2]{1,0:T(1,128)}, u32[]{:S(2)}) copy-start(s32[1,2]{1,0:T(1,128)} %param.19) | copy-start | bytes 28
  11.3 89.5 %copy-start.1 = (bf16[1,2,2048]{2,1,0:T(2,128)(2,1)S(1)}, bf16[1,2,2048]{2,1,0:T(2,128)(2,1)}, u32[]{:S(2)}) copy-start(bf16[1,2,2048]{2,1,0:T(2,128)(2,1)} %param.20) | copy-start | bytes 24580
  19.3 36.4 %all-to-all-start = ((bf16[24,72,128]{2,1,0:T(8,128)(2,1)}), bf16[24,72,128]{2,1,0:T(8,128)(2,1)}, u32[]{:S(2)}, u32[]{:S(2)}) async-start(bf16[24,72,128]{2,1,0:T(8,128)(2,1)} %fusion.17), calls=%async_computation | async-start | bytes 884736 | tf_op jit(solution)/shard_map/all_to_all | solution.py:30
  102.5 17.5 %all-to-all-start.3 = ((bf16[32,2,2048]{2,1,0:T(2,128)(2,1)}), bf16[32,2,2048]{2,1,0:T(2,128)(2,1)}, u32[]{:S(2)}, u32[]{:S(2)}) async-start(bf16[32,2,2048]{2,1,0:T(2,128)(2,1)} %broadcast_in_dim.56), calls=%async_computation.3 | async-start | bytes 524288 | tf_op jit(solution)/shard_map/all_to_all | solution.py:30

commit v2 on v1

v2 whole, which is shorter than its diff:
```python
import math

import jax
import jax.numpy as jnp
from jax import lax
from jax.experimental import pallas as pl
from jax.experimental.pallas import tpu as pltpu
from jax.sharding import PartitionSpec as P

QUERY_HEADS = 32
KEY_VALUE_HEADS = 4
HEAD_SIZE = 128
GROUP = QUERY_HEADS // KEY_VALUE_HEADS
LANES = 128
STAT_ROWS = 16
DEST_ROWS = 8

masked_score = -1e30
norm_epsilon = 1e-06
score_scale = 1.0 / math.sqrt(HEAD_SIZE)
f32 = jnp.float32
bf16 = jnp.bfloat16
INTERPRET = False


def exchange(x, axis):
    return lax.all_to_all(x, axis, split_axis=0, concat_axis=0, tiled=True)


def kernel_call(body, outs, scratch, *args, scalars=0, hbm=()):
    smem = pl.BlockSpec(memory_space=pltpu.SMEM)
    vmem = pl.BlockSpec(memory_space=pltpu.VMEM)
    raw = pl.BlockSpec(memory_space=pl.ANY)
    specs = [smem if i < scalars else raw if i in hbm else vmem for i in range(len(args))]
    return pl.pallas_call(
        body,
        out_shape=outs,
        in_specs=specs,
        out_specs=jax.tree.map(lambda _: vmem, outs),
        scratch_shapes=scratch,
        compiler_params=pltpu.CompilerParams(vmem_limit_bytes=24 << 20),
        interpret=INTERPRET,
    )(*args)


def shape(dims, dtype):
    return jax.ShapeDtypeStruct(dims, dtype)


def head_columns(k):
    return slice(k * HEAD_SIZE, (k + 1) * HEAD_SIZE)


def dot_last(a, b):
    return lax.dot_general(a, b, (((1,), (1,)), ((), ())), preferred_element_type=f32)


def dot_first(a, b):
    return lax.dot_general(a, b, (((0,), (0,)), ((), ())), preferred_element_type=f32)


def prefix_body(block_ref, q_ref, k_ref, v_ref, out_ref, own_ref, q_rows, stats):
    rows = q_ref.shape[0]
    dests = out_ref.shape[0]
    per_dest = rows * GROUP // dests
    stats[...] = jnp.zeros(stats.shape, f32)
    start = pl.multiple_of(block_ref[0] * per_dest, per_dest)
    for k in range(KEY_VALUE_HEADS):
        for j in range(GROUP):
            part = q_ref[:, head_columns(k * GROUP + j)].astype(f32)
            q_rows[k, pl.ds(j, rows, stride=GROUP), :] = part
    for k in range(KEY_VALUE_HEADS):
        own_ref[k * per_dest : (k + 1) * per_dest, :] = q_rows[k, pl.ds(start, per_dest), :]
        q = q_rows[k].astype(bf16)
        scores = dot_last(k_ref[:, head_columns(k)], q) * score_scale
        top = jnp.max(scores, 0, keepdims=True)
        top_high = top.astype(bf16).astype(f32)
        top_low = (top - top_high).astype(bf16).astype(f32)
        terms = jnp.exp(scores - (top_high + top_low))
        mass = jnp.sum(terms, 0, keepdims=True)
        mass_high = mass.astype(bf16).astype(f32)
        width = rows * GROUP
        stats[k : k + 1, 0:width] = top_high
        stats[4 + k : 5 + k, 0:width] = top_low
        stats[8 + k : 9 + k, 0:width] = mass_high
        stats[12 + k : 13 + k, 0:width] = mass - mass_high
        weighted = dot_first(terms.astype(bf16), v_ref[:, head_columns(k)])
        out_ref[:, k * per_dest : (k + 1) * per_dest, :] = weighted.astype(bf16).reshape(
            dests, per_dest, HEAD_SIZE
        )
    held = stats[...]
    first = KEY_VALUE_HEADS * per_dest
    for d in range(dests):
        piece = held[:, d * per_dest : d * per_dest + LANES]
        out_ref[d, first : first + STAT_ROWS, :] = piece.astype(bf16)


def suffix_body(length_ref, own_ref, k_ref, v_ref, out_ref, stat_ref):
    per_dest = own_ref.shape[0] // KEY_VALUE_HEADS
    keys = k_ref.shape[0]
    half = keys // 2
    row = lax.broadcasted_iota(jnp.int32, (keys, per_dest), 0)
    lane = lax.broadcasted_iota(jnp.int32, (keys, per_dest), 1)
    second = row >= half
    limit = jnp.where(second, length_ref[0, 1] + half, length_ref[0, 0])
    inside = (second == (lane >= GROUP)) & (row < limit)
    stat_ref[...] = jnp.zeros(stat_ref.shape, f32)
    for k in range(KEY_VALUE_HEADS):
        q = own_ref[k * per_dest : (k + 1) * per_dest, :].astype(bf16)
        scores = dot_last(k_ref[:, head_columns(k)], q) * score_scale
        scores = jnp.where(inside, scores, masked_score)
        top = jnp.max(scores, 0, keepdims=True)
        terms = jnp.where(inside, jnp.exp(scores - top), 0.0)
        mass = jnp.sum(terms, 0, keepdims=True)
        for r in (k, 4 + k):
            stat_ref[r : r + 1, 0:per_dest] = top
            stat_ref[8 + r : 9 + r, 0:per_dest] = mass
        out_ref[k * per_dest : (k + 1) * per_dest, :] = dot_first(
            terms.astype(bf16), v_ref[:, head_columns(k)]
        )


def merge_body(part_ref, suffix_ref, stat_ref, chosen_ref, out_ref, rows):
    sources = part_ref.shape[0]
    per_dest = suffix_ref.shape[0] // KEY_VALUE_HEADS
    first = KEY_VALUE_HEADS * per_dest
    tops, masses = [stat_ref[0:8]], [stat_ref[8:16]]
    for g in range(sources):
        held = part_ref[g, first : first + STAT_ROWS, :].astype(f32)
        tops.append(held[0:8] + pltpu.roll(held[0:8], 4, 0))
        masses.append(held[8:16] + pltpu.roll(held[8:16], 4, 0))
    top = tops[0]
    for t in tops[1:]:
        top = jnp.maximum(top, t)
    scales = [jnp.exp(t - top) for t in tops]
    total = scales[0] * masses[0]
    for s, m in zip(scales[1:], masses[1:]):
        total = total + s * m
    inverse = 1.0 / total
    scales = [s * inverse for s in scales]
    scales += [jnp.zeros((8, LANES), f32)] * (-len(scales) % 16)
    table = jnp.concatenate(scales, 0)
    turned = jnp.concatenate(
        [table[i : i + LANES].T[0:per_dest] for i in range(0, table.shape[0], LANES)], 1
    )
    rows[...] = jnp.zeros(rows.shape, f32)
    for k in range(KEY_VALUE_HEADS):
        mine = slice(k * per_dest, (k + 1) * per_dest)
        mixed = turned[:, k : k + 1] * suffix_ref[mine, :]
        for g in range(sources):
            at = (g + 1) * 8 + k
            mixed = mixed + turned[:, at : at + 1] * part_ref[g, mine, :].astype(f32)
        for i in range(per_dest // GROUP):
            at = k * GROUP * DEST_ROWS + i
            rows[pl.ds(at, GROUP, stride=DEST_ROWS), :] = mixed[i * GROUP : (i + 1) * GROUP]
    for i in range(per_dest // GROUP):
        line = jnp.broadcast_to(chosen_ref[i : i + 1, :], (QUERY_HEADS, LANES))
        rows[pl.ds(2 + i, QUERY_HEADS, stride=DEST_ROWS), :] = line
    out_ref[...] = rows[...].astype(bf16)


def project_body(attn_ref, weight_ref, out_ref, chosen_ref, rows, lines):
    count = attn_ref.shape[0] // DEST_ROWS
    blocks = weight_ref.shape[1] // LANES
    rows[...] = attn_ref[...].astype(f32)
    attn = jnp.concatenate([rows[pl.ds(i, count, stride=DEST_ROWS), :] for i in range(2)], 0)
    for i in range(2):
        chosen_ref[i * count : (i + 1) * count, :] = rows[pl.ds(2 + i, count, stride=DEST_ROWS), :]
    made = jnp.dot(attn.astype(bf16), weight_ref[...], preferred_element_type=f32)
    spread_rows(made, lines, count, blocks)
    out_ref[...] = lines[...].astype(bf16)


def spread_rows(made, lines, count, blocks):
    for i in range(2):
        for c in range(blocks):
            lines[pl.ds(i * blocks + c, count, stride=2 * blocks), :] = made[
                i * count : (i + 1) * count, c * LANES : (c + 1) * LANES
            ]


def norm_body(part_ref, residual_ref, gain_ref, hidden_ref, out_ref, lines):
    sources, size, _ = part_ref.shape
    blocks = size // 2
    for c in range(blocks):
        piece = residual_ref[:, c * LANES : (c + 1) * LANES].astype(f32)
        lines[pl.ds(c, 2, stride=blocks), :] = piece
    hidden = lines[...]
    for s in range(sources):
        hidden = hidden + part_ref[s].astype(f32)
    hidden_ref[...] = hidden
    halves = []
    for i in range(2):
        half = hidden[i * blocks : (i + 1) * blocks]
        mean_square = jnp.sum(half * half, keepdims=True) / (blocks * LANES)
        halves.append(half * lax.rsqrt(mean_square + norm_epsilon) * gain_ref[...])
    normed = jnp.concatenate(halves, 0).astype(bf16)
    for s in range(sources):
        out_ref[s] = normed


def expert_body(
    first_ref, x_ref, chosen_ref, router_ref, gate_hbm, up_hbm, down_hbm, out_ref,
    lines, x_rows, gate, up, down, sems,
):
    experts = gate.shape[0]
    copies = []
    for e in range(experts):
        for n, (source, target) in enumerate(((gate_hbm, gate), (up_hbm, up), (down_hbm, down))):
            copy = pltpu.make_async_copy(source.at[e], target.at[e], sems.at[3 * e + n])
            copy.start()
            copies.append(copy)
    count, size, _ = x_ref.shape
    blocks = size // 2
    lines[...] = x_ref[...].reshape(count * size, LANES).astype(f32)
    for i in range(2):
        for c in range(blocks):
            x_rows[i * count : (i + 1) * count, c * LANES : (c + 1) * LANES] = lines[
                pl.ds(i * blocks + c, count, stride=size), :
            ].astype(bf16)
    x = x_rows[...]
    logits = jnp.dot(x, router_ref[...], preferred_element_type=f32)
    expo = jnp.where(chosen_ref[:, 0 : logits.shape[1]] > 0.5, jnp.exp(logits), 0.0)
    lane = lax.broadcasted_iota(jnp.int32, logits.shape, 1)
    mass = jnp.sum(expo, 1, keepdims=True)
    mixed = jnp.zeros((2 * count, down.shape[2]), f32)
    for e in range(experts):
        copies[3 * e].wait()
        gate_out = jnp.dot(x, gate[e], preferred_element_type=f32)
        copies[3 * e + 1].wait()
        up_out = jnp.dot(x, up[e], preferred_element_type=f32)
        act = (gate_out / (1.0 + jnp.exp(-gate_out)) * up_out).astype(bf16)
        copies[3 * e + 2].wait()
        made = jnp.dot(act, down[e], preferred_element_type=f32).astype(bf16).astype(f32)
        mine = jnp.sum(jnp.where(lane == first_ref[0] + e, expo, 0.0), 1, keepdims=True)
        mixed = mixed + (mine / mass) * made
    spread_rows(mixed, lines, count, blocks)
    out_ref[...] = lines[...].astype(bf16).reshape(count, size, LANES)


def final_body(part_ref, hidden_ref, out_ref, lines):
    sources, size, _ = part_ref.shape
    blocks = size // 2
    total = part_ref[0].astype(f32)
    for s in range(1, sources):
        total = total + part_ref[s].astype(f32)
    lines[...] = hidden_ref[...] + total
    for c in range(blocks):
        out_ref[:, c * LANES : (c + 1) * LANES] = lines[pl.ds(c, 2, stride=blocks), :]


def prefix_attention(block, q, k, v, dests):
    rows = q.shape[0]
    per_dest = rows * GROUP // dests
    send = KEY_VALUE_HEADS * per_dest + STAT_ROWS
    padded = (rows * GROUP // LANES + 1) * LANES
    return kernel_call(
        prefix_body,
        (shape((dests, send, HEAD_SIZE), bf16), shape((KEY_VALUE_HEADS * per_dest, HEAD_SIZE), f32)),
        [
            pltpu.VMEM((KEY_VALUE_HEADS, rows * GROUP, HEAD_SIZE), f32),
            pltpu.VMEM((STAT_ROWS, padded), f32),
        ],
        block, q, k, v, scalars=1,
    )


def suffix_attention(lengths, own, k, v):
    return kernel_call(
        suffix_body,
        (shape(own.shape, f32), shape((STAT_ROWS, LANES), f32)),
        [], lengths, own, k, v, scalars=1,
    )


def merge_parts(parts, suffix, stats, chosen):
    dims = (QUERY_HEADS * DEST_ROWS, HEAD_SIZE)
    return kernel_call(
        merge_body, shape(dims, bf16), [pltpu.VMEM(dims, f32)], parts, suffix, stats, chosen
    )


def project(attn, weight):
    count = attn.shape[0] // DEST_ROWS
    dims = (count * 2 * weight.shape[1] // LANES, LANES)
    return kernel_call(
        project_body,
        (shape(dims, bf16), shape((2 * count, LANES), f32)),
        [pltpu.VMEM(attn.shape, f32), pltpu.VMEM(dims, f32)],
        attn, weight,
    )


def normalize(parts, residual, gain):
    return kernel_call(
        norm_body,
        (shape(parts.shape[1:], f32), shape(parts.shape, bf16)),
        [pltpu.VMEM(parts.shape[1:], f32)],
        parts, residual, gain,
    )


def run_experts(first, x, chosen, router, gate, up, down):
    count, size, _ = x.shape
    return kernel_call(
        expert_body,
        shape(x.shape, bf16),
        [
            pltpu.VMEM((count * size, LANES), f32),
            pltpu.VMEM((2 * count, size // 2 * LANES), bf16),
            pltpu.VMEM(gate.shape, bf16),
            pltpu.VMEM(up.shape, bf16),
            pltpu.VMEM(down.shape, bf16),
            pltpu.SemaphoreType.DMA((3 * gate.shape[0],)),
        ],
        first, x, chosen, router, gate, up, down, scalars=1, hbm=(4, 5, 6),
    )


def add_parts(parts, hidden):
    size = parts.shape[1]
    return kernel_call(
        final_body,
        shape((2, size // 2 * LANES), f32),
        [pltpu.VMEM((size, LANES), f32)],
        parts, hidden,
    )


def chosen_lines(ids):
    mask = jnp.any(ids[..., None] == jnp.arange(LANES, dtype=jnp.int32), 1)
    return mask.astype(f32)


def shards(
    queries,
    shared_prefix_keys,
    shared_prefix_values,
    row_suffix_keys,
    row_suffix_values,
    suffix_lengths,
    residual,
    out_weight,
    norm_gain,
    router_weight,
    gate_weights,
    up_weights,
    down_weights,
    expert_ids,
):
    heads = lax.axis_size("head")
    dests = lax.axis_size("grp")
    block = lax.axis_index("grp").astype(jnp.int32).reshape(1)
    send, own = prefix_attention(
        block, queries[0], shared_prefix_keys[0], shared_prefix_values[0], dests
    )
    arrived = exchange(send, "grp")
    chosen = chosen_lines(expert_ids[0])
    suffix, stats = suffix_attention(
        suffix_lengths,
        own,
        row_suffix_keys.reshape(-1, row_suffix_keys.shape[-1]),
        row_suffix_values.reshape(-1, row_suffix_values.shape[-1]),
    )
    attn = merge_parts(arrived, suffix, stats, chosen)
    attn = exchange(attn.reshape(heads, DEST_ROWS, HEAD_SIZE), "head")
    parts, chosen = project(attn.reshape(heads * DEST_ROWS, HEAD_SIZE), out_weight)
    parts = exchange(parts.reshape(heads, -1, LANES), "head")
    hidden, normed = normalize(parts, residual[0], norm_gain.reshape(-1, LANES))
    x = exchange(normed, "head")
    first = (lax.axis_index("head") * gate_weights.shape[0]).astype(jnp.int32).reshape(1)
    made = run_experts(first, x, chosen, router_weight, gate_weights, up_weights, down_weights)
    return add_parts(exchange(made, "head"), hidden)[None]


def solution(mesh):
    return jax.shard_map(
        shards,
        mesh=mesh,
        in_specs=(
            P("head", None, None),
            P("head", "grp", None),
            P("head", "grp", None),
            P("head", "grp", None, None),
            P("head", "grp", None, None),
            P("head", "grp"),
            P("head", "grp", None),
            P("head", None),
            P(),
            P(),
            P("head", None, None),
            P("head", None, None),
            P("head", None, None),
            P("head", "grp", None),
        ),
        out_specs=P("head", "grp", None),
        check_vma=False,
    )
```

time: 151 us -> 131 us (0.87)
  matrix products: 15.2 us -> 0 us
  other arithmetic: 11.4 us -> 0.77 us
  Pallas kernels: 0 us -> 9.02 us
  local copies, waits for them, and re-layouts: 19.2 us -> 15.8 us
  waiting for transfers between devices: 26.4 us -> 28.8 us
    dot_general x8 -> x0, matrix products: 15.2 us -> none  [the longest x1 3.78 us: shards(): jnp.einsum('erf,efd->erd', act, down_weights, preferred_element_type=f32)]
    unnamed x8 -> x31, local copies, waits for them, and re-layouts: 1.08 us -> 15.8 us
    pallas_call x0 -> x7, Pallas kernels: none -> 9.02 us  [kernel_call(): pl.pallas_call(body, out_shape=outs, in_specs=specs, out_specs=jax.tree.m...]
    another operation x4 -> x0, local copies, waits for them, and re-layouts: 5.48 us -> none  [the longest x1 1.74 us: shards(): k = shared_prefix_keys[0].reshape(-1, KEY_VALUE_HEADS, HEAD_SIZE)]
    reshape x6 -> x0, local copies, waits for them, and re-layouts: 3.92 us -> none  [the longest x2 2.79 us: shards(): x = x.reshape(head_count * own_rows, width)]
    convert_element_type x4 -> x1, other arithmetic: 3.75 us -> 0.01 us  [chosen_lines(): return mask.astype(f32)]
    reduce_sum x3 -> x0, local copies, waits for them, and re-layouts: 3.12 us -> none  [the longest x2 3.03 us: shards(): s_high, s_low = two_pieces(jnp.sum(terms, -1))]
    reduce_sum x6 -> x0, other arithmetic: 2.7 us -> none  [the longest x1 1.27 us: shards(): jnp.sum(scale[..., None] * arrived[:, :n].astype(f32), 0)]
  transfers between devices with their start and end apart: 2 -> 2, of which waited for: 2 -> 2; matrix products, arithmetic and copies ran while one was open for 4% -> 2% of each run, Pallas kernels for 0% -> 1%
where the time goes in v2:
time: 131 us; the launch traced here: 130 us
  blocking collectives  55.1 us (42%)
  waiting for transfers between devices  28.8 us (22%)
  starting transfers between devices  20.7 us (16%)
  local copies, waits for them, and re-layouts  15.8 us (12%)
  Pallas kernels  9.02 us (7%)
    all_to_all x3, blocking collectives, exchange(): return lax.all_to_all(x, axis, split_axis=0, concat_axis=0, tiled=True)  55.1 us
    all_to_all x2, waiting for transfers between devices, exchange(): return lax.all_to_all(x, axis, split_axis=0, concat_axis=0, tiled=True)  28.8 us
    all_to_all x2, starting transfers between devices, exchange(): return lax.all_to_all(x, axis, split_axis=0, concat_axis=0, tiled=True)  20.7 us
    unnamed x31, local copies, waits for them, and re-layouts  15.8 us
    pallas_call x7, Pallas kernels, kernel_call(): pl.pallas_call(body, out_shape=outs, in_specs=specs, out_specs=jax.tree.m...  9.02 us
  transfers between devices with their start and end apart: 2, of which 2 were waited for; matrix products, arithmetic and copies ran while one was open for 2% of the time, Pallas kernels for 1%

profile of v2, /device:TPU:1, one launch (start us, length us, event | category | flops | bytes accessed | tf_op | source)
XLA Modules:
  0.0 130.3 jit_solution(10980133551209441501)
XLA Ops:
  0.0 0.0 copy-start
  0.0 0.0 copy-start.6
  0.0 1.1 copy-done.6
  1.1 0.0 copy-start.8
  1.2 0.9 copy-done.8
  2.1 0.0 copy-start.9
  2.1 0.9 copy-done.9
  3.0 1.1 shard_map.136
  4.1 0.0 copy-start.5
  4.1 0.8 copy-done.5
  4.9 17.0 %all-to-all-start = ((bf16[24,80,128]{2,1,0:T(8,128)(2,1)}), bf16[24,80,128]{2,1,0:T(8,128)(2,1)}, u32[]{:S(2)}, u32[]{:S(2)}) async-start(bf16[24,80,128]{2,1,0:T(8,128)(2,1)} %copy-done.5), calls=%async_computation | async-start | bytes 983040 | tf_op jit(solution)/shard_map/all_to_all | solution.py:27
  21.9 0.8 fusion
  22.7 0.0 copy-start.10
  22.7 0.7 copy-done.10
  23.4 0.0 copy-start.11
  23.4 0.8 copy-done.11
  24.2 0.0 copy-start.14
  24.2 0.7 copy-done.14
  24.8 0.9 shard_map.137
  25.7 17.3 %all-to-all-done.part_ref = bf16[24,80,128]{2,1,0:T(8,128)(2,1)} async-done(((bf16[24,80,128]{2,1,0:T(8,128)(2,1)}), bf16[24,80,128]{2,1,0:T(8,128)(2,1)}, u32[]{:S(2)}, u32[]{:S(2)}) %all-to-all-start) | async-done | bytes 491552 | tf_op jit(solution)/shard_map/all_to_all | solution.py:27
  43.0 1.6 %shard_map.138 = bf16[256,128]{1,0:T(8,128)(2,1)S(1)} custom-call(bf16[24,80,128]{2,1,0:T(8,128)(2,1)} %all-to-all-done.part_ref, f32[64,128]{1,0:T(8,128)S(1)} %get-tuple-element.15.suffix_ref, f32[16,128]{1,0:T(8,128)S(1)} %get-tuple-element.16.stat_ref, f32[2,128]{1,0:T(2,128)S(1)} %convert_element_type.3.chosen_ref), custom_call_target="tpu_custom_call" | custom-call | tf_op jit(solution)/shard_map/pallas_call | solution.py:35
  44.5 21.6 %all_to_all.25 = bf16[32,8,128]{2,1,0:T(8,128)(2,1)S(1)} all-to-all(bf16[32,8,128]{2,1,0:T(8,128)(2,1)S(1)} %bitcast.15), channel_id=1, replica_groups=mesh['grp'=24,'head'=32] {'head'}, dimensions={0} | all-to-all | bytes 131072 | tf_op jit(solution)/shard_map/all_to_all | solution.py:27
  66.2 0.0 copy-start.4
  66.2 1.0 copy-done.4
  67.2 0.5 shard_map.139
  67.7 16.6 %all_to_all.26.part_ref = bf16[32,32,128]{2,1,0:T(8,128)(2,1)S(1)} all-to-all(bf16[32,32,128]{2,1,0:T(8,128)(2,1)S(1)} %bitcast.17), channel_id=1, replica_groups=mesh['grp'=24,'head'=32] {'head'}, dimensions={0} | all-to-all | bytes 524288 | tf_op jit(solution)/shard_map/all_to_all | solution.py:27
  84.3 0.0 copy-start.12
  84.4 0.7 copy-done.12
  85.0 0.0 copy-start.13
  85.0 0.7 copy-done.13
  85.7 0.2 shard_map.140
  85.9 0.0 copy-start.7
  85.9 0.7 copy-done.7
  86.6 3.7 %all-to-all-start.3 = ((bf16[32,32,128]{2,1,0:T(8,128)(2,1)}), bf16[32,32,128]{2,1,0:T(8,128)(2,1)S(1)}, u32[]{:S(2)}, u32[]{:S(2)}) async-start(bf16[32,32,128]{2,1,0:T(8,128)(2,1)} %copy-done.7), calls=%async_computation.3 | async-start | bytes 524288 | tf_op jit(solution)/shard_map/all_to_all | solution.py:27
  90.3 2.0 %copy.16.router_ref = bf16[2048,64]{1,0:T(8,128)(2,1)} copy(bf16[2048,64]{0,1:T(8,128)(2,1)} %param.23) | data formatting | bytes 524288 | tf_op args[9]
  92.3 11.5 %all-to-all-done.3.x_ref = bf16[32,32,128]{2,1,0:T(8,128)(2,1)S(1)} async-done(((bf16[32,32,128]{2,1,0:T(8,128)(2,1)}), bf16[32,32,128]{2,1,0:T(8,128)(2,1)S(1)}, u32[]{:S(2)}, u32[]{:S(2)}) %all-to-all-start.3) | async-done | bytes 262176 | tf_op jit(solution)/shard_map/all_to_all | solution.py:27
  103.8 0.0 copy-done
  103.8 0.0 copy-start.1
  103.8 1.9 %copy-done.1 = bf16[2,2048,384]{2,1,0:T(8,128)(2,1)S(1)} copy-done((bf16[2,2048,384]{2,1,0:T(8,128)(2,1)S(1)}, bf16[2,2048,384]{2,1,0:T(8,128)(2,1)}, u32[]{:S(2)}) %copy-start.1) | copy-done | bytes 3145752
  105.7 0.0 copy-start.2
  105.7 1.9 %copy-done.2 = bf16[2,384,2048]{2,1,0:T(8,128)(2,1)S(1)} copy-done((bf16[2,384,2048]{2,1,0:T(8,128)(2,1)S(1)}, bf16[2,384,2048]{2,1,0:T(8,128)(2,1)}, u32[]{:S(2)}) %copy-start.2) | copy-done | bytes 3145752
  107.6 0.0 copy-start.3
  107.6 1.0 copy-done.3
  108.6 4.2 %shard_map.141 = bf16[32,32,128]{2,1,0:T(8,128)(2,1)S(1)} custom-call(s32[1]{0:T(128)} %bitcast.first_ref, bf16[32,32,128]{2,1,0:T(8,128)(2,1)S(1)} %all-to-all-done.3.x_ref, f32[64,128]{1,0:T(8,128)S(1)} %get-tuple-element.19.chosen_ref, bf16[2048,64]{1,0:T(8,128)(2,1)S(1)} %copy-done.3, bf16[2,2048,384]{2,1,0:T(8,128)(2,1)S(1)} %copy-done, ...), custom_call_target="tpu_custom_call" | custom-call | tf_op jit(solution)/shard_map/pallas_call | solution.py:35
  112.8 16.9 %all_to_all.27.part_ref = bf16[32,32,128]{2,1,0:T(8,128)(2,1)S(1)} all-to-all(bf16[32,32,128]{2,1,0:T(8,128)(2,1)S(1)} %shard_map.141), channel_id=1, replica_groups=mesh['grp'=24,'head'=32] {'head'}, dimensions={0} | all-to-all | bytes 524288 | tf_op jit(solution)/shard_map/all_to_all | solution.py:27
  129.6 0.7 shard_map.142
  (1 shorter events, 0.0 us)
Async XLA Ops:
  0.0 103.8 %copy-start = (bf16[2,2048,384]{2,1,0:T(8,128)(2,1)S(1)}, bf16[2,2048,384]{2,1,0:T(8,128)(2,1)}, u32[]{:S(2)}) copy-start(bf16[2,2048,384]{2,1,0:T(8,128)(2,1)} %gate_hbm.1) | copy-start | bytes 9437188
  0.0 1.1 copy-start.6
  1.1 0.9 copy-start.8
  2.1 0.9 copy-start.9
  4.1 0.8 copy-start.5
  4.9 38.1 %all-to-all-start = ((bf16[24,80,128]{2,1,0:T(8,128)(2,1)}), bf16[24,80,128]{2,1,0:T(8,128)(2,1)}, u32[]{:S(2)}, u32[]{:S(2)}) async-start(bf16[24,80,128]{2,1,0:T(8,128)(2,1)} %copy-done.5), calls=%async_computation | async-start | bytes 983040 | tf_op jit(solution)/shard_map/all_to_all | solution.py:27
  22.7 0.8 copy-start.10
  23.4 0.8 copy-start.11
  24.2 0.7 copy-start.14
  66.2 1.0 copy-start.4
  84.3 0.7 copy-start.12
  85.0 0.7 copy-start.13
  85.9 0.7 copy-start.7
  86.6 17.1 %all-to-all-start.3 = ((bf16[32,32,128]{2,1,0:T(8,128)(2,1)}), bf16[32,32,128]{2,1,0:T(8,128)(2,1)S(1)}, u32[]{:S(2)}, u32[]{:S(2)}) async-start(bf16[32,32,128]{2,1,0:T(8,128)(2,1)} %copy-done.7), calls=%async_computation.3 | async-start | bytes 524288 | tf_op jit(solution)/shard_map/all_to_all | solution.py:27
  103.8 1.9 %copy-start.1 = (bf16[2,2048,384]{2,1,0:T(8,128)(2,1)S(1)}, bf16[2,2048,384]{2,1,0:T(8,128)(2,1)}, u32[]{:S(2)}) copy-start(bf16[2,2048,384]{2,1,0:T(8,128)(2,1)} %up_hbm.1) | copy-start | bytes 9437188
  105.7 1.9 %copy-start.2 = (bf16[2,384,2048]{2,1,0:T(8,128)(2,1)S(1)}, bf16[2,384,2048]{2,1,0:T(8,128)(2,1)}, u32[]{:S(2)}) copy-start(bf16[2,384,2048]{2,1,0:T(8,128)(2,1)} %down_hbm.1) | copy-start | bytes 9437188
  107.6 1.0 copy-start.3

commit v3 on v2

--- a/solution.py
+++ b/solution.py
@@ -27,18 +27,22 @@
     return lax.all_to_all(x, axis, split_axis=0, concat_axis=0, tiled=True)
 
 
-def kernel_call(body, outs, scratch, *args, scalars=0, hbm=()):
+def kernel_call(body, outs, scratch, *args, scalars=0, hbm=(), hbm_outs=()):
     smem = pl.BlockSpec(memory_space=pltpu.SMEM)
     vmem = pl.BlockSpec(memory_space=pltpu.VMEM)
-    raw = pl.BlockSpec(memory_space=pl.ANY)
+    raw = pl.BlockSpec(memory_space=pltpu.HBM)
     specs = [smem if i < scalars else raw if i in hbm else vmem for i in range(len(args))]
+    args = [
+        pltpu.with_memory_space_constraint(a, pltpu.HBM) if i in hbm else a
+        for i, a in enumerate(args)
+    ]
     return pl.pallas_call(
         body,
         out_shape=outs,
         in_specs=specs,
-        out_specs=jax.tree.map(lambda _: vmem, outs),
+        out_specs=tuple(raw if i in hbm_outs else vmem for i in range(len(outs))),
         scratch_shapes=scratch,
-        compiler_params=pltpu.CompilerParams(vmem_limit_bytes=24 << 20),
+        compiler_params=pltpu.CompilerParams(vmem_limit_bytes=16 << 20),
         interpret=INTERPRET,
     )(*args)
 
@@ -59,43 +63,89 @@
     return lax.dot_general(a, b, (((0,), (0,)), ((), ())), preferred_element_type=f32)
 
 
-def prefix_body(block_ref, q_ref, k_ref, v_ref, out_ref, own_ref, q_rows, stats):
-    rows = q_ref.shape[0]
-    dests = out_ref.shape[0]
+def start_copy(source, target, sem):
+    copy = pltpu.make_async_copy(source, target, sem)
+    copy.start()
+    return copy
+
+
+def prefix_body(
+    block_ref, expert_ref, q_hbm, k_hbm, v_hbm, out_hbm, own_ref, mark_ref,
+    q_in, k_in, v_in, q_rows, stats, made, in_sems, out_sems,
+):
+    rows = q_hbm.shape[0]
+    dests = out_hbm.shape[0]
     per_dest = rows * GROUP // dests
+    width = rows * GROUP
+    wide = GROUP * HEAD_SIZE
+    arrivals = []
+    for k in range(KEY_VALUE_HEADS):
+        q_columns = slice(k * wide, (k + 1) * wide)
+        pairs = (
+            (q_hbm.at[:, q_columns], q_in.at[k]),
+            (k_hbm.at[:, head_columns(k)], k_in.at[k]),
+            (v_hbm.at[:, head_columns(k)], v_in.at[k]),
+        )
+        arrivals.append([start_copy(a, b, in_sems.at[3 * k + n]) for n, (a, b) in enumerate(pairs)])
     stats[...] = jnp.zeros(stats.shape, f32)
+    lane = lax.broadcasted_iota(jnp.int32, mark_ref.shape, 1)
+    row = lax.broadcasted_iota(jnp.int32, mark_ref.shape, 0)
+    mark_ref[...] = (lane == expert_ref[0] + row).astype(f32)
     start = pl.multiple_of(block_ref[0] * per_dest, per_dest)
+    departures = []
     for k in range(KEY_VALUE_HEADS):
+        for copy in arrivals[k]:
+            copy.wait()
         for j in range(GROUP):
-            part = q_ref[:, head_columns(k * GROUP + j)].astype(f32)
-            q_rows[k, pl.ds(j, rows, stride=GROUP), :] = part
-    for k in range(KEY_VALUE_HEADS):
-        own_ref[k * per_dest : (k + 1) * per_dest, :] = q_rows[k, pl.ds(start, per_dest), :]
-        q = q_rows[k].astype(bf16)
-        scores = dot_last(k_ref[:, head_columns(k)], q) * score_scale
+            q_rows[k, pl.ds(j, rows, stride=GROUP), :] = q_in[k, :, head_columns(j)].astype(f32)
+        mine = slice(k * per_dest, (k + 1) * per_dest)
+        own_ref[mine, :] = q_rows[k, pl.ds(start, per_dest), :]
+        scores = dot_last(k_in[k], q_rows[k].astype(bf16)) * score_scale
         top = jnp.max(scores, 0, keepdims=True)
         top_high = top.astype(bf16).astype(f32)
         top_low = (top - top_high).astype(bf16).astype(f32)
         terms = jnp.exp(scores - (top_high + top_low))
         mass = jnp.sum(terms, 0, keepdims=True)
         mass_high = mass.astype(bf16).astype(f32)
-        width = rows * GROUP
         stats[k : k + 1, 0:width] = top_high
         stats[4 + k : 5 + k, 0:width] = top_low
         stats[8 + k : 9 + k, 0:width] = mass_high
         stats[12 + k : 13 + k, 0:width] = mass - mass_high
-        weighted = dot_first(terms.astype(bf16), v_ref[:, head_columns(k)])
-        out_ref[:, k * per_dest : (k + 1) * per_dest, :] = weighted.astype(bf16).reshape(
-            dests, per_dest, HEAD_SIZE
-        )
+        weighted = dot_first(terms.astype(bf16), v_in[k])
+        made[:, mine, :] = weighted.astype(bf16).reshape(dests, per_dest, HEAD_SIZE)
+        departures.append(start_copy(made.at[:, mine, :], out_hbm.at[:, mine, :], out_sems.at[k]))
     held = stats[...]
-    first = KEY_VALUE_HEADS * per_dest
+    last = slice(KEY_VALUE_HEADS * per_dest, KEY_VALUE_HEADS * per_dest + STAT_ROWS)
     for d in range(dests):
-        piece = held[:, d * per_dest : d * per_dest + LANES]
-        out_ref[d, first : first + STAT_ROWS, :] = piece.astype(bf16)
-
-
-def suffix_body(length_ref, own_ref, k_ref, v_ref, out_ref, stat_ref):
+        made[d, last, :] = held[:, d * per_dest : d * per_dest + LANES].astype(bf16)
+    departures.append(
+        start_copy(made.at[:, last, :], out_hbm.at[:, last, :], out_sems.at[KEY_VALUE_HEADS])
+    )
+    for copy in departures:
+        copy.wait()
+
+
+def window_body(
+    length_ref, own_ref, k_hbm, v_hbm, residual_hbm, gain_hbm, out_ref, stat_ref, lines_ref,
+    gain_ref, k_ref, v_ref, residual_ref, sems,
+):
+    pairs = (
+        (k_hbm, k_ref),
+        (v_hbm, v_ref),
+        (residual_hbm, residual_ref),
+        (gain_hbm, gain_ref),
+    )
+    copies = [start_copy(a, b, sems.at[n]) for n, (a, b) in enumerate(pairs)]
+    for copy in copies:
+        copy.wait()
+    blocks = lines_ref.shape[0] // 2
+    for c in range(blocks):
+        piece = residual_ref[:, c * LANES : (c + 1) * LANES].astype(f32)
+        lines_ref[pl.ds(c, 2, stride=blocks), :] = piece
+    suffix_attention(length_ref, own_ref, k_ref, v_ref, out_ref, stat_ref)
+
+
+def suffix_attention(length_ref, own_ref, k_ref, v_ref, out_ref, stat_ref):
     per_dest = own_ref.shape[0] // KEY_VALUE_HEADS
     keys = k_ref.shape[0]
     half = keys // 2
@@ -120,7 +170,12 @@
         )
 
 
-def merge_body(part_ref, suffix_ref, stat_ref, chosen_ref, out_ref, rows):
+def merge_body(
+    part_ref, suffix_ref, stat_ref, chosen_ref, weight_hbm, router_hbm, up_hbm,
+    out_ref, weight_ref, router_ref, up_ref, rows, sems,
+):
+    pairs = ((weight_hbm, weight_ref), (router_hbm, router_ref), (up_hbm, up_ref))
+    copies = [start_copy(a, b, sems.at[n]) for n, (a, b) in enumerate(pairs)]
     sources = part_ref.shape[0]
     per_dest = suffix_ref.shape[0] // KEY_VALUE_HEADS
     first = KEY_VALUE_HEADS * per_dest
@@ -157,6 +212,8 @@
         line = jnp.broadcast_to(chosen_ref[i : i + 1, :], (QUERY_HEADS, LANES))
         rows[pl.ds(2 + i, QUERY_HEADS, stride=DEST_ROWS), :] = line
     out_ref[...] = rows[...].astype(bf16)
+    for copy in copies:
+        copy.wait()
 
 
 def project_body(attn_ref, weight_ref, out_ref, chosen_ref, rows, lines):
@@ -179,13 +236,10 @@
             ]
 
 
-def norm_body(part_ref, residual_ref, gain_ref, hidden_ref, out_ref, lines):
+def norm_body(part_ref, residual_ref, gain_ref, hidden_ref, out_ref):
     sources, size, _ = part_ref.shape
     blocks = size // 2
-    for c in range(blocks):
-        piece = residual_ref[:, c * LANES : (c + 1) * LANES].astype(f32)
-        lines[pl.ds(c, 2, stride=blocks), :] = piece
-    hidden = lines[...]
+    hidden = residual_ref[...]
     for s in range(sources):
         hidden = hidden + part_ref[s].astype(f32)
     hidden_ref[...] = hidden
@@ -200,16 +254,11 @@
 
 
 def expert_body(
-    first_ref, x_ref, chosen_ref, router_ref, gate_hbm, up_hbm, down_hbm, out_ref,
-    lines, x_rows, gate, up, down, sems,
+    x_ref, chosen_ref, mark_ref, router_ref, gate, up, down_hbm, out_ref,
+    lines, x_rows, down, sems,
 ):
     experts = gate.shape[0]
-    copies = []
-    for e in range(experts):
-        for n, (source, target) in enumerate(((gate_hbm, gate), (up_hbm, up), (down_hbm, down))):
-            copy = pltpu.make_async_copy(source.at[e], target.at[e], sems.at[3 * e + n])
-            copy.start()
-            copies.append(copy)
+    copies = [start_copy(down_hbm.at[e], down.at[e], sems.at[e]) for e in range(experts)]
     count, size, _ = x_ref.shape
     blocks = size // 2
     lines[...] = x_ref[...].reshape(count * size, LANES).astype(f32)
@@ -219,20 +268,18 @@
                 pl.ds(i * blocks + c, count, stride=size), :
             ].astype(bf16)
     x = x_rows[...]
-    logits = jnp.dot(x, router_ref[...], preferred_element_type=f32)
+    logits = dot_last(x, router_ref[...])
     expo = jnp.where(chosen_ref[:, 0 : logits.shape[1]] > 0.5, jnp.exp(logits), 0.0)
-    lane = lax.broadcasted_iota(jnp.int32, logits.shape, 1)
     mass = jnp.sum(expo, 1, keepdims=True)
     mixed = jnp.zeros((2 * count, down.shape[2]), f32)
     for e in range(experts):
-        copies[3 * e].wait()
         gate_out = jnp.dot(x, gate[e], preferred_element_type=f32)
-        copies[3 * e + 1].wait()
         up_out = jnp.dot(x, up[e], preferred_element_type=f32)
         act = (gate_out / (1.0 + jnp.exp(-gate_out)) * up_out).astype(bf16)
-        copies[3 * e + 2].wait()
+        copies[e].wait()
         made = jnp.dot(act, down[e], preferred_element_type=f32).astype(bf16).astype(f32)
-        mine = jnp.sum(jnp.where(lane == first_ref[0] + e, expo, 0.0), 1, keepdims=True)
+        mark = mark_ref[e : e + 1, 0 : expo.shape[1]] > 0.5
+        mine = jnp.sum(jnp.where(mark, expo, 0.0), 1, keepdims=True)
         mixed = mixed + (mine / mass) * made
     spread_rows(mixed, lines, count, blocks)
     out_ref[...] = lines[...].astype(bf16).reshape(count, size, LANES)
@@ -249,34 +296,55 @@
         out_ref[:, c * LANES : (c + 1) * LANES] = lines[pl.ds(c, 2, stride=blocks), :]
 
 
-def prefix_attention(block, q, k, v, dests):
+def prefix_attention(block, expert, q, k, v, dests):
     rows = q.shape[0]
     per_dest = rows * GROUP // dests
-    send = KEY_VALUE_HEADS * per_dest + STAT_ROWS
+    send = (dests, KEY_VALUE_HEADS * per_dest + STAT_ROWS, HEAD_SIZE)
     padded = (rows * GROUP // LANES + 1) * LANES
-    return kernel_call(
+    made, own, marks = kernel_call(
         prefix_body,
-        (shape((dests, send, HEAD_SIZE), bf16), shape((KEY_VALUE_HEADS * per_dest, HEAD_SIZE), f32)),
+        (
+            pltpu.HBM(send, bf16),
+            shape((KEY_VALUE_HEADS * per_dest, HEAD_SIZE), f32),
+            shape((8, LANES), f32),
+        ),
         [
+            pltpu.VMEM((KEY_VALUE_HEADS, rows, GROUP * HEAD_SIZE), bf16),
+            pltpu.VMEM((KEY_VALUE_HEADS, k.shape[0], HEAD_SIZE), bf16),
+            pltpu.VMEM((KEY_VALUE_HEADS, k.shape[0], HEAD_SIZE), bf16),
             pltpu.VMEM((KEY_VALUE_HEADS, rows * GROUP, HEAD_SIZE), f32),
             pltpu.VMEM((STAT_ROWS, padded), f32),
+            pltpu.VMEM(send, bf16),
+            pltpu.SemaphoreType.DMA((3 * KEY_VALUE_HEADS,)),
+            pltpu.SemaphoreType.DMA((KEY_VALUE_HEADS + 1,)),
         ],
-        block, q, k, v, scalars=1,
-    )
-
-
-def suffix_attention(lengths, own, k, v):
-    return kernel_call(
-        suffix_body,
-        (shape(own.shape, f32), shape((STAT_ROWS, LANES), f32)),
-        [], lengths, own, k, v, scalars=1,
-    )
-
-
-def merge_parts(parts, suffix, stats, chosen):
+        block, expert, q, k, v, scalars=2, hbm=(2, 3, 4), hbm_outs=(0,),
+    )
+    return made, own, marks
+
+
+def fill_window(lengths, own, k, v, residual, gain):
+    return kernel_call(
+        window_body,
+        (
+            shape(own.shape, f32),
+            shape((STAT_ROWS, LANES), f32),
+            shape((residual.size // LANES, LANES), f32),
+            shape(gain.shape, f32),
+        ),
+        [pltpu.VMEM(a.shape, bf16) for a in (k, v, residual)]
+        + [pltpu.SemaphoreType.DMA((4,))],
+        lengths, own, k, v, residual, gain, scalars=1, hbm=(2, 3, 4, 5),
+    )
+
+
+def merge_parts(parts, suffix, stats, chosen, *weights):
     dims = (QUERY_HEADS * DEST_ROWS, HEAD_SIZE)
     return kernel_call(
-        merge_body, shape(dims, bf16), [pltpu.VMEM(dims, f32)], parts, suffix, stats, chosen
+        merge_body,
+        (shape(dims, bf16), *(shape(w.shape, bf16) for w in weights)),
+        [pltpu.VMEM(dims, f32), pltpu.SemaphoreType.DMA((len(weights),))],
+        parts, suffix, stats, chosen, *weights, hbm=range(4, 4 + len(weights)),
     )
 
 
@@ -295,36 +363,34 @@
     return kernel_call(
         norm_body,
         (shape(parts.shape[1:], f32), shape(parts.shape, bf16)),
-        [pltpu.VMEM(parts.shape[1:], f32)],
+        [],
         parts, residual, gain,
     )
 
 
-def run_experts(first, x, chosen, router, gate, up, down):
+def run_experts(x, chosen, marks, router, gate, up, down):
     count, size, _ = x.shape
     return kernel_call(
         expert_body,
-        shape(x.shape, bf16),
+        (shape(x.shape, bf16),),
         [
             pltpu.VMEM((count * size, LANES), f32),
             pltpu.VMEM((2 * count, size // 2 * LANES), bf16),
-            pltpu.VMEM(gate.shape, bf16),
-            pltpu.VMEM(up.shape, bf16),
             pltpu.VMEM(down.shape, bf16),
-            pltpu.SemaphoreType.DMA((3 * gate.shape[0],)),
+            pltpu.SemaphoreType.DMA((down.shape[0],)),
         ],
-        first, x, chosen, router, gate, up, down, scalars=1, hbm=(4, 5, 6),
-    )
+        x, chosen, marks, router, gate, up, down, hbm=(6,),
+    )[0]
 
 
 def add_parts(parts, hidden):
     size = parts.shape[1]
     return kernel_call(
         final_body,
-        shape((2, size // 2 * LANES), f32),
+        (shape((2, size // 2 * LANES), f32),),
         [pltpu.VMEM((size, LANES), f32)],
         parts, hidden,
-    )
+    )[0]
 
 
 def chosen_lines(ids):
@@ -351,25 +417,29 @@
     heads = lax.axis_size("head")
     dests = lax.axis_size("grp")
     block = lax.axis_index("grp").astype(jnp.int32).reshape(1)
-    send, own = prefix_attention(
-        block, queries[0], shared_prefix_keys[0], shared_prefix_values[0], dests
+    expert = (lax.axis_index("head") * gate_weights.shape[0]).astype(jnp.int32).reshape(1)
+    send, own, marks = prefix_attention(
+        block, expert, queries[0], shared_prefix_keys[0], shared_prefix_values[0], dests
     )
     arrived = exchange(send, "grp")
     chosen = chosen_lines(expert_ids[0])
-    suffix, stats = suffix_attention(
+    suffix, stats, residual_lines, gain = fill_window(
         suffix_lengths,
         own,
         row_suffix_keys.reshape(-1, row_suffix_keys.shape[-1]),
         row_suffix_values.reshape(-1, row_suffix_values.shape[-1]),
-    )
-    attn = merge_parts(arrived, suffix, stats, chosen)
+        residual[0],
+        norm_gain.reshape(-1, LANES),
+    )
+    attn, weight, router, up = merge_parts(
+        arrived, suffix, stats, chosen, out_weight, router_weight.T, up_weights
+    )
     attn = exchange(attn.reshape(heads, DEST_ROWS, HEAD_SIZE), "head")
-    parts, chosen = project(attn.reshape(heads * DEST_ROWS, HEAD_SIZE), out_weight)
+    parts, chosen = project(attn.reshape(heads * DEST_ROWS, HEAD_SIZE), weight)
     parts = exchange(parts.reshape(heads, -1, LANES), "head")
-    hidden, normed = normalize(parts, residual[0], norm_gain.reshape(-1, LANES))
+    hidden, normed = normalize(parts, residual_lines, gain)
     x = exchange(normed, "head")
-    first = (lax.axis_index("head") * gate_weights.shape[0]).astype(jnp.int32).reshape(1)
-    made = run_experts(first, x, chosen, router_weight, gate_weights, up_weights, down_weights)
+    made = run_experts(x, chosen, marks, router, gate_weights, up, down_weights)
     return add_parts(exchange(made, "head"), hidden)[None]
 
 

time: 131 us -> 120 us (0.916)
  blocking collectives: 55.1 us -> 71.6 us
  local copies, waits for them, and re-layouts: 15.8 us -> 0.65 us
  waiting for transfers between devices: 28.8 us -> 17.9 us
  starting transfers between devices: 20.7 us -> 16.9 us
  Pallas kernels: 9.02 us -> 12.1 us
    all_to_all x3 -> x4, blocking collectives: 55.1 us -> 71.6 us  [exchange(): return lax.all_to_all(x, axis, split_axis=0, concat_axis=0, tiled=True)]
    unnamed x31 -> x4, local copies, waits for them, and re-layouts: 15.8 us -> 0.65 us
    all_to_all x2 -> x1, waiting for transfers between devices: 28.8 us -> 17.9 us  [exchange(): return lax.all_to_all(x, axis, split_axis=0, concat_axis=0, tiled=True)]
    all_to_all x2 -> x1, starting transfers between devices: 20.7 us -> 16.9 us  [exchange(): return lax.all_to_all(x, axis, split_axis=0, concat_axis=0, tiled=True)]
    pallas_call x7, Pallas kernels: 9.02 us -> 12.1 us  [kernel_call(): pl.pallas_call(body, out_shape=outs, in_specs=specs, out_specs=tuple((raw...]
  transfers between devices with their start and end apart: 2 -> 1, of which waited for: 2 -> 1; matrix products, arithmetic and copies ran while one was open for 2% -> 1% of each run, Pallas kernels for 1% -> 1%
where the time goes in v3:
time: 120 us
  blocking collectives  71.6 us (60%)
  waiting for transfers between devices  17.9 us (15%)
  starting transfers between devices  16.9 us (14%)
  Pallas kernels  12.1 us (10%)
    all_to_all x4, blocking collectives, exchange(): return lax.all_to_all(x, axis, split_axis=0, concat_axis=0, tiled=True)  71.6 us
    all_to_all x1, waiting for transfers between devices, exchange(): return lax.all_to_all(x, axis, split_axis=0, concat_axis=0, tiled=True)  17.9 us
    all_to_all x1, starting transfers between devices, exchange(): return lax.all_to_all(x, axis, split_axis=0, concat_axis=0, tiled=True)  16.9 us
    pallas_call x7, Pallas kernels, kernel_call(): pl.pallas_call(body, out_shape=outs, in_specs=specs, out_specs=tuple((raw...  12.1 us
  transfers between devices with their start and end apart: 1, of which 1 were waited for; matrix products, arithmetic and copies ran while one was open for 1% of the time, Pallas kernels for 1%

profile of v3, /device:TPU:1, one launch (start us, length us, event | category | flops | bytes accessed | tf_op | source)
XLA Modules:
  0.0 120.0 jit_solution(5485263173490400663)
XLA Ops:
  0.0 3.7 %shard_map.136 = (bf16[24,80,128]{2,1,0:T(8,128)(2,1)}, f32[64,128]{1,0:T(8,128)S(1)}, f32[8,128]{1,0:T(8,128)S(1)}) custom-call(s32[1]{0:T(128)} %bitcast.block_ref, s32[1]{0:T(128)} %bitcast.1.expert_ref, bf16[48,4096]{1,0:T(8,128)(2,1)} %bitcast.18, bf16[128,512]{1,0:T(8,128)(2,1)} %bitcast.20, bf16[128,512]{1,0:T(8,128)(2,1)} %bitcast.21), custom_call_target="tpu_custom_call" | custom-call | tf_op jit(solution)/shard_map/pallas_call | solution.py:39
  3.7 16.9 %all-to-all-start = ((bf16[24,80,128]{2,1,0:T(8,128)(2,1)}), bf16[24,80,128]{2,1,0:T(8,128)(2,1)S(1)}, u32[]{:S(2)}, u32[]{:S(2)}) async-start(bf16[24,80,128]{2,1,0:T(8,128)(2,1)} %get-tuple-element.20), calls=%async_computation | async-start | bytes 983040 | tf_op jit(solution)/shard_map/all_to_all | solution.py:27
  20.7 0.8 fusion
  21.4 0.0 copy-start.1
  21.4 0.6 copy-done.1
  22.1 1.7 %shard_map.137 = (f32[64,128]{1,0:T(8,128)S(1)}, f32[16,128]{1,0:T(8,128)S(1)}, f32[32,128]{1,0:T(8,128)S(1)}, f32[16,128]{1,0:T(8,128)S(1)}) custom-call(s32[1,2]{1,0:T(1,128)S(1)} %copy-done.1, f32[64,128]{1,0:T(8,128)S(1)} %get-tuple-element.21.own_ref, bf16[32,512]{1,0:T(8,128)(2,1)} %bitcast.22, bf16[32,512]{1,0:T(8,128)(2,1)} %bitcast.23, ...), custom_call_target="tpu_custom_call" | custom-call | tf_op jit(solution)/shard_map/pallas_call | solution.py:39
  23.8 17.9 %all-to-all-done.part_ref = bf16[24,80,128]{2,1,0:T(8,128)(2,1)S(1)} async-done(((bf16[24,80,128]{2,1,0:T(8,128)(2,1)}), bf16[24,80,128]{2,1,0:T(8,128)(2,1)S(1)}, u32[]{:S(2)}, u32[]{:S(2)}) %all-to-all-start) | async-done | bytes 491552 | tf_op jit(solution)/shard_map/all_to_all | solution.py:27
  41.7 0.0 copy-start
  41.7 2.3 %shard_map.138 = (bf16[256,128]{1,0:T(8,128)(2,1)S(1)}, bf16[128,2048]{1,0:T(8,128)(2,1)S(1)}, bf16[64,2048]{1,0:T(8,128)(2,1)S(1)}, bf16[2,2048,384]{2,1,0:T(8,128)(2,1)S(1)}) custom-call(bf16[24,80,128]{2,1,0:T(8,128)(2,1)S(1)} %all-to-all-done.part_ref, f32[64,128]{1,0:T(8,128)S(1)} %get-tuple-element.22.suffix_ref, ...), custom_call_target="tpu_custom_call" | custom-call | tf_op jit(solution)/shard_map/pallas_call | solution.py:39
  44.0 21.7 %all_to_all.25 = bf16[32,8,128]{2,1,0:T(8,128)(2,1)S(1)} all-to-all(bf16[32,8,128]{2,1,0:T(8,128)(2,1)S(1)} %bitcast.17), channel_id=1, replica_groups=mesh['grp'=24,'head'=32] {'head'}, dimensions={0} | all-to-all | bytes 131072 | tf_op jit(solution)/shard_map/all_to_all | solution.py:27
  65.7 0.5 shard_map.139
  66.1 16.6 %all_to_all.26.part_ref = bf16[32,32,128]{2,1,0:T(8,128)(2,1)S(1)} all-to-all(bf16[32,32,128]{2,1,0:T(8,128)(2,1)S(1)} %bitcast.16), channel_id=1, replica_groups=mesh['grp'=24,'head'=32] {'head'}, dimensions={0} | all-to-all | bytes 524288 | tf_op jit(solution)/shard_map/all_to_all | solution.py:27
  82.8 0.2 shard_map.140
  83.0 16.9 %all_to_all.27.x_ref = bf16[32,32,128]{2,1,0:T(8,128)(2,1)S(1)} all-to-all(bf16[32,32,128]{2,1,0:T(8,128)(2,1)S(1)} %get-tuple-element.29), channel_id=1, replica_groups=mesh['grp'=24,'head'=32] {'head'}, dimensions={0} | all-to-all | bytes 524288 | tf_op jit(solution)/shard_map/all_to_all | solution.py:27
  99.9 0.0 copy-done
  99.9 3.1 %shard_map.141 = bf16[32,32,128]{2,1,0:T(8,128)(2,1)S(1)} custom-call(bf16[32,32,128]{2,1,0:T(8,128)(2,1)S(1)} %all_to_all.27.x_ref, f32[64,128]{1,0:T(8,128)S(1)} %get-tuple-element.30.chosen_ref, f32[8,128]{1,0:T(8,128)S(1)} %get-tuple-element.31.mark_ref, bf16[64,2048]{1,0:T(8,128)(2,1)S(1)} %get-tuple-element.32.router_ref, ...), custom_call_target="tpu_custom_call" | custom-call | tf_op jit(solution)/shard_map/pallas_call | solution.py:39
  103.0 16.4 %all_to_all.28.part_ref = bf16[32,32,128]{2,1,0:T(8,128)(2,1)S(1)} all-to-all(bf16[32,32,128]{2,1,0:T(8,128)(2,1)S(1)} %shard_map.141), channel_id=1, replica_groups=mesh['grp'=24,'head'=32] {'head'}, dimensions={0} | all-to-all | bytes 524288 | tf_op jit(solution)/shard_map/all_to_all | solution.py:27
  119.4 0.7 shard_map.142
  (1 shorter events, 0.0 us)
Async XLA Ops:
  3.7 38.0 %all-to-all-start = ((bf16[24,80,128]{2,1,0:T(8,128)(2,1)}), bf16[24,80,128]{2,1,0:T(8,128)(2,1)S(1)}, u32[]{:S(2)}, u32[]{:S(2)}) async-start(bf16[24,80,128]{2,1,0:T(8,128)(2,1)} %get-tuple-element.20), calls=%async_computation | async-start | bytes 983040 | tf_op jit(solution)/shard_map/all_to_all | solution.py:27
  21.4 0.7 copy-start.1
  41.7 58.2 %copy-start = (bf16[2,2048,384]{2,1,0:T(8,128)(2,1)S(1)}, bf16[2,2048,384]{2,1,0:T(8,128)(2,1)}, u32[]{:S(2)}) copy-start(bf16[2,2048,384]{2,1,0:T(8,128)(2,1)} %gate.1) | copy-start | bytes 9437188

commit v4 on v3

v4 whole, which is shorter than its diff:
```python
import math

import jax
import jax.numpy as jnp
from jax import lax
from jax.experimental import pallas as pl
from jax.experimental.pallas import tpu as pltpu
from jax.sharding import PartitionSpec as P


QUERY_HEADS = 32
KEY_VALUE_HEADS = 4
HEAD_SIZE = 128
GROUP = QUERY_HEADS // KEY_VALUE_HEADS
LANES = 128
STAT_ROWS = 8
DEST_ROWS = 16
SPREAD = 4
EXTRA_ROWS = 8

masked_score = -1e30
norm_epsilon = 1e-06
score_scale = 1.0 / math.sqrt(HEAD_SIZE)
f32 = jnp.float32
bf16 = jnp.bfloat16
INTERPRET = False


def exchange(x, axis, groups=None):
    return lax.all_to_all(
        x, axis, split_axis=0, concat_axis=0, tiled=True, axis_index_groups=groups
    )


def kernel_call(body, outs, scratch, *args, scalars=0, hbm=(), hbm_outs=()):
    smem = pl.BlockSpec(memory_space=pltpu.SMEM)
    vmem = pl.BlockSpec(memory_space=pltpu.VMEM)
    raw = pl.BlockSpec(memory_space=pltpu.HBM)
    specs = [smem if i < scalars else raw if i in hbm else vmem for i in range(len(args))]
    args = [
        pltpu.with_memory_space_constraint(a, pltpu.HBM) if i in hbm else a
        for i, a in enumerate(args)
    ]
    return pl.pallas_call(
        body,
        out_shape=outs,
        in_specs=specs,
        out_specs=tuple(raw if i in hbm_outs else vmem for i in range(len(outs))),
        scratch_shapes=scratch,
        compiler_params=pltpu.CompilerParams(vmem_limit_bytes=16 << 20),
        interpret=INTERPRET,
    )(*args)


def shape(dims, dtype):
    return jax.ShapeDtypeStruct(dims, dtype)


def head_columns(k):
    return slice(k * HEAD_SIZE, (k + 1) * HEAD_SIZE)


def dot_last(a, b):
    return lax.dot_general(a, b, (((1,), (1,)), ((), ())), preferred_element_type=f32)


def dot_first(a, b):
    return lax.dot_general(a, b, (((0,), (0,)), ((), ())), preferred_element_type=f32)


def start_copy(source, target, sem):
    copy = pltpu.make_async_copy(source, target, sem)
    copy.start()
    return copy


def prefix_body(
    block_ref, expert_ref, q_hbm, k_hbm, v_hbm, out_hbm, own_ref, mark_ref,
    q_in, k_in, v_in, q_rows, stats, rests, made, in_sems, out_sems,
):
    rows = q_hbm.shape[0]
    dests = out_hbm.shape[0]
    per_dest = rows * GROUP // dests
    width = rows * GROUP
    wide = GROUP * HEAD_SIZE
    keys = start_copy(k_hbm, k_in, in_sems.at[KEY_VALUE_HEADS])
    arrivals = [
        start_copy(q_hbm.at[:, k * wide : (k + 1) * wide], q_in.at[k], in_sems.at[k])
        for k in range(KEY_VALUE_HEADS)
    ]
    values = start_copy(v_hbm, v_in, in_sems.at[KEY_VALUE_HEADS + 1])
    stats[...] = jnp.zeros(stats.shape, f32)
    rests[...] = jnp.zeros(rests.shape, f32)
    lane = lax.broadcasted_iota(jnp.int32, mark_ref.shape, 1)
    row = lax.broadcasted_iota(jnp.int32, mark_ref.shape, 0)
    mark_ref[...] = (lane == expert_ref[0] + row).astype(f32)
    start = pl.multiple_of(block_ref[0] * per_dest, per_dest)
    departures = []
    for k in range(KEY_VALUE_HEADS):
        arrivals[k].wait()
        if k == 0:
            keys.wait()
        for j in range(GROUP):
            q_rows[k, pl.ds(j, rows, stride=GROUP), :] = q_in[k, :, head_columns(j)].astype(f32)
        mine = slice(k * per_dest, (k + 1) * per_dest)
        own_ref[mine, :] = q_rows[k, pl.ds(start, per_dest), :]
        scores = dot_last(k_in[:, head_columns(k)], q_rows[k].astype(bf16)) * score_scale
        top = jnp.max(scores, 0, keepdims=True)
        top_high = top.astype(bf16).astype(f32)
        top_low = (top - top_high).astype(bf16).astype(f32)
        terms = jnp.exp(scores - (top_high + top_low))
        mass = jnp.sum(terms, 0, keepdims=True)
        mass_high = mass.astype(bf16).astype(f32)
        stats[k : k + 1, 0:width] = top_high
        stats[4 + k : 5 + k, 0:width] = mass_high
        rests[k : k + 1, 0:width] = top_low
        rests[4 + k : 5 + k, 0:width] = mass - mass_high
        if k == 0:
            values.wait()
        weighted = dot_first(terms.astype(bf16), v_in[:, head_columns(k)])
        made[:, mine, :] = weighted.astype(bf16).reshape(dests, per_dest, HEAD_SIZE)
        departures.append(start_copy(made.at[:, mine, :], out_hbm.at[:, mine, :], out_sems.at[k]))
    held = stats[...]
    rest = pltpu.roll(rests[...], per_dest, 1)
    low = lax.broadcasted_iota(jnp.int32, (STAT_ROWS, LANES), 1) < per_dest
    last = slice(KEY_VALUE_HEADS * per_dest, KEY_VALUE_HEADS * per_dest + STAT_ROWS)
    for d in range(dests):
        at = slice(d * per_dest, d * per_dest + LANES)
        made[d, last, :] = jnp.where(low, held[:, at], rest[:, at]).astype(bf16)
    departures.append(
        start_copy(made.at[:, last, :], out_hbm.at[:, last, :], out_sems.at[KEY_VALUE_HEADS])
    )
    for copy in departures:
        copy.wait()


def pack_body(place_ref, weight_hbm, residual_hbm, *refs):
    outs, (weight, residual, extra, extras, sems) = refs[:SPREAD], refs[SPREAD:]
    depth, width = weight.shape[0], outs[0].shape[1]
    load = start_copy(weight_hbm, weight, sems.at[0])
    small = start_copy(residual_hbm, residual, sems.at[1])
    small.wait()
    copies = []
    starts = []
    for s in range(SPREAD):
        start = pl.multiple_of(((place_ref[0] + s) & (SPREAD - 1)) * width, width)
        starts.append(start)
        extra[...] = jnp.zeros(extra.shape, f32)
        extra[0:2, :] = residual[:, pl.ds(start, width)].astype(f32)
        extras[s] = extra[...].astype(bf16)
        copies.append(
            start_copy(extras.at[s], outs[s].at[depth : depth + EXTRA_ROWS, :], sems.at[2 + s])
        )
    load.wait()
    for s in range(SPREAD):
        piece = weight.at[:, pl.ds(starts[s], width)]
        copies.append(start_copy(piece, outs[s].at[0:depth, :], sems.at[2 + SPREAD + s]))
    for copy in copies:
        copy.wait()


def window_body(length_ref, own_ref, k_hbm, v_hbm, out_ref, stat_ref, k_ref, v_ref, sems):
    pairs = ((k_hbm, k_ref), (v_hbm, v_ref))
    copies = [start_copy(a, b, sems.at[n]) for n, (a, b) in enumerate(pairs)]
    for copy in copies:
        copy.wait()
    suffix_attention(length_ref, own_ref, k_ref, v_ref, out_ref, stat_ref)


def suffix_attention(length_ref, own_ref, k_ref, v_ref, out_ref, stat_ref):
    per_dest = own_ref.shape[0] // KEY_VALUE_HEADS
    keys = k_ref.shape[0]
    half = keys // 2
    row = lax.broadcasted_iota(jnp.int32, (keys, per_dest), 0)
    lane = lax.broadcasted_iota(jnp.int32, (keys, per_dest), 1)
    second = row >= half
    limit = jnp.where(second, length_ref[0, 1] + half, length_ref[0, 0])
    inside = (second == (lane >= GROUP)) & (row < limit)
    stat_ref[...] = jnp.zeros(stat_ref.shape, f32)
    for k in range(KEY_VALUE_HEADS):
        q = own_ref[k * per_dest : (k + 1) * per_dest, :].astype(bf16)
        scores = dot_last(k_ref[:, head_columns(k)], q) * score_scale
        scores = jnp.where(inside, scores, masked_score)
        top = jnp.max(scores, 0, keepdims=True)
        terms = jnp.where(inside, jnp.exp(scores - top), 0.0)
        mass = jnp.sum(terms, 0, keepdims=True)
        stat_ref[k : k + 1, 0:per_dest] = top
        stat_ref[4 + k : 5 + k, 0:per_dest] = mass
        out_ref[k * per_dest : (k + 1) * per_dest, :] = dot_first(
            terms.astype(bf16), v_ref[:, head_columns(k)]
        )


def merge_body(
    part_ref, suffix_ref, stat_ref, chosen_ref, router_hbm, up_hbm,
    out_ref, router_ref, up_ref, rows, heads, sems,
):
    pairs = ((router_hbm, router_ref), (up_hbm, up_ref))
    copies = [start_copy(a, b, sems.at[n]) for n, (a, b) in enumerate(pairs)]
    sources = part_ref.shape[0]
    per_dest = suffix_ref.shape[0] // KEY_VALUE_HEADS
    first = KEY_VALUE_HEADS * per_dest
    held = [stat_ref[...]]
    for g in range(sources):
        both = part_ref[g, first : first + STAT_ROWS, :].astype(f32)
        held.append(both + pltpu.roll(both, LANES - per_dest, 1))
    top = held[0]
    for t in held[1:]:
        top = jnp.maximum(top, t)
    scales = [jnp.exp(t - top) for t in held]
    masses = [pltpu.roll(t, 4, 0) for t in held]
    total = scales[0] * masses[0]
    for s, m in zip(scales[1:], masses[1:]):
        total = total + s * m
    inverse = 1.0 / total
    scales = [s * inverse for s in scales]
    scales += [jnp.zeros((8, LANES), f32)] * (-len(scales) % 16)
    table = jnp.concatenate(scales, 0)
    turned = jnp.concatenate(
        [table[i : i + LANES].T[0:per_dest] for i in range(0, table.shape[0], LANES)], 1
    )
    rows[...] = jnp.zeros(rows.shape, f32)
    for k in range(KEY_VALUE_HEADS):
        mine = slice(k * per_dest, (k + 1) * per_dest)
        mixed = turned[:, k : k + 1] * suffix_ref[mine, :]
        for g in range(sources):
            at = (g + 1) * 8 + k
            mixed = mixed + turned[:, at : at + 1] * part_ref[g, mine, :].astype(f32)
        for i in range(2):
            heads[i * QUERY_HEADS + k * GROUP : i * QUERY_HEADS + (k + 1) * GROUP, :] = mixed[
                i * GROUP : (i + 1) * GROUP
            ]
    near = QUERY_HEADS // SPREAD
    for y in range(SPREAD):
        for s in range(SPREAD):
            source = (y - s) % SPREAD * near
            for i in range(2):
                at = y * near * DEST_ROWS + i * SPREAD + s
                rows[pl.ds(at, near, stride=DEST_ROWS), :] = heads[
                    i * QUERY_HEADS + source : i * QUERY_HEADS + source + near, :
                ]
    for i in range(2):
        line = jnp.broadcast_to(chosen_ref[i : i + 1, :], (QUERY_HEADS, LANES))
        rows[pl.ds(2 * SPREAD + i, QUERY_HEADS, stride=DEST_ROWS), :] = line
    out_ref[...] = rows[...].astype(bf16)
    for copy in copies:
        copy.wait()


def project_body(place_ref, attn_ref, *refs):
    pieces, (out_ref, chosen_ref, residual_ref, rows, lines) = refs[:SPREAD], refs[SPREAD:]
    count = attn_ref.shape[0] // DEST_ROWS
    depth = pieces[0].shape[0] - EXTRA_ROWS
    near = count // SPREAD
    blocks = pieces[0].shape[1] // LANES
    rows[...] = attn_ref[...].astype(f32)
    for i in range(2):
        line = rows[pl.ds(2 * SPREAD + i, count, stride=DEST_ROWS), :]
        chosen_ref[i * count : (i + 1) * count, :] = line
    made = jnp.zeros((2 * count, blocks * LANES), f32)
    for s in range(SPREAD):
        attn = [rows[pl.ds(i * SPREAD + s, count, stride=DEST_ROWS), :] for i in range(2)]
        attn = jnp.concatenate(attn, 0).astype(bf16)
        made = made + jnp.dot(attn, pieces[s][0:depth, :], preferred_element_type=f32)
        extra = pieces[s][depth : depth + EXTRA_ROWS, :].astype(f32)
        source = (place_ref[0] + SPREAD - s) & (SPREAD - 1)
        for i in range(2):
            for c in range(blocks):
                residual_ref[pl.ds(c * 2 * SPREAD + i * SPREAD + source, 1), :] = extra[
                    i : i + 1, c * LANES : (c + 1) * LANES
                ]
    for c in range(blocks):
        lines[c] = made[:, c * LANES : (c + 1) * LANES]
    for n in range(near):
        parts = [lines[c, pl.ds(n, 2 * SPREAD, stride=near), :] for c in range(blocks)]
        out_ref[n] = jnp.concatenate(parts, 0).astype(bf16)


def spread_rows(made, lines, count, blocks):
    for i in range(2):
        for c in range(blocks):
            lines[pl.ds(i * blocks + c, count, stride=2 * blocks), :] = made[
                i * count : (i + 1) * count, c * LANES : (c + 1) * LANES
            ]


def sum_body(part_ref, residual_ref, out_ref):
    hidden = residual_ref[...]
    for n in range(part_ref.shape[0]):
        hidden = hidden + part_ref[n].astype(f32)
    hidden = hidden.astype(bf16)
    for h in range(out_ref.shape[0]):
        out_ref[h] = hidden


def expert_body(
    first_ref, x_ref, chosen_ref, mark_ref, gain_ref, router_ref, gate, up, down_hbm,
    out_ref, hidden_ref, lines, x_rows, down, sems,
):
    experts = gate.shape[0]
    copies = [start_copy(down_hbm.at[e], down.at[e], sems.at[e]) for e in range(experts)]
    count, size, _ = x_ref.shape
    near = count // SPREAD
    pairs = 2 * SPREAD
    blocks = size // pairs
    own = first_ref[0] // experts
    far = own // near
    lines[...] = x_ref[...].astype(f32).reshape(lines.shape)
    for y in range(SPREAD):
        for c in range(blocks):
            for n in range(near):
                at = (y * near + n) * size + c * pairs
                x_rows[y * blocks + c, pl.ds(n, pairs, stride=near), :] = lines[at : at + pairs, :]
            for i in range(2):
                at = (y * near + own - far * near) * size + c * pairs + i * SPREAD + far
                to = (i * SPREAD + y) * blocks + c
                hidden_ref[to : to + 1, :] = lines[pl.ds(at, 1), :]
    hidden = jnp.concatenate([x_rows[c] for c in range(SPREAD * blocks)], 1)
    mean_square = jnp.sum(hidden * hidden, 1, keepdims=True) / hidden.shape[1]
    x = (hidden * lax.rsqrt(mean_square + norm_epsilon) * gain_ref[...]).astype(bf16)
    logits = dot_last(x, router_ref[...])
    expo = jnp.where(chosen_ref[:, 0 : logits.shape[1]] > 0.5, jnp.exp(logits), 0.0)
    mass = jnp.sum(expo, 1, keepdims=True)
    mixed = jnp.zeros((2 * count, down.shape[2]), f32)
    for e in range(experts):
        gate_out = jnp.dot(x, gate[e], preferred_element_type=f32)
        up_out = jnp.dot(x, up[e], preferred_element_type=f32)
        act = (gate_out / (1.0 + jnp.exp(-gate_out)) * up_out).astype(bf16)
        copies[e].wait()
        made = jnp.dot(act, down[e], preferred_element_type=f32).astype(bf16).astype(f32)
        mark = mark_ref[e : e + 1, 0 : expo.shape[1]] > 0.5
        mine = jnp.sum(jnp.where(mark, expo, 0.0), 1, keepdims=True)
        mixed = mixed + (mine / mass) * made
    spread_rows(mixed, lines, count, size // 2)
    out_ref[...] = lines[...].astype(bf16).reshape(count, size, LANES)


def final_body(part_ref, hidden_ref, out_ref, lines):
    sources, size, _ = part_ref.shape
    blocks = size // 2
    total = part_ref[0].astype(f32)
    for s in range(1, sources):
        total = total + part_ref[s].astype(f32)
    lines[...] = hidden_ref[...] + total
    for c in range(blocks):
        out_ref[:, c * LANES : (c + 1) * LANES] = lines[pl.ds(c, 2, stride=blocks), :]


def prefix_attention(block, expert, q, k, v, dests):
    rows = q.shape[0]
    per_dest = rows * GROUP // dests
    send = (dests, KEY_VALUE_HEADS * per_dest + STAT_ROWS, HEAD_SIZE)
    padded = (rows * GROUP // LANES + 1) * LANES
    made, own, marks = kernel_call(
        prefix_body,
        (
            pltpu.HBM(send, bf16),
            shape((KEY_VALUE_HEADS * per_dest, HEAD_SIZE), f32),
            shape((8, LANES), f32),
        ),
        [
            pltpu.VMEM((KEY_VALUE_HEADS, rows, GROUP * HEAD_SIZE), bf16),
            pltpu.VMEM(k.shape, bf16),
            pltpu.VMEM(v.shape, bf16),
            pltpu.VMEM((KEY_VALUE_HEADS, rows * GROUP, HEAD_SIZE), f32),
            pltpu.VMEM((STAT_ROWS, padded), f32),
            pltpu.VMEM((STAT_ROWS, padded), f32),
            pltpu.VMEM(send, bf16),
            pltpu.SemaphoreType.DMA((KEY_VALUE_HEADS + 2,)),
            pltpu.SemaphoreType.DMA((KEY_VALUE_HEADS + 1,)),
        ],
        block, expert, q, k, v, scalars=2, hbm=(2, 3, 4), hbm_outs=(0,),
    )
    return made, own, marks


def pack_weights(place, weight, residual):
    width = weight.shape[1] // SPREAD
    dims = (weight.shape[0] + EXTRA_ROWS, width)
    return kernel_call(
        pack_body,
        tuple(pltpu.HBM(dims, bf16) for _ in range(SPREAD)),
        [
            pltpu.VMEM(weight.shape, bf16),
            pltpu.VMEM(residual.shape, bf16),
            pltpu.VMEM((EXTRA_ROWS, width), f32),
            pltpu.VMEM((SPREAD, EXTRA_ROWS, width), bf16),
            pltpu.SemaphoreType.DMA((2 + 2 * SPREAD,)),
        ],
        place, weight, residual, scalars=1, hbm=(1, 2), hbm_outs=range(SPREAD),
    )


def fill_window(lengths, own, k, v):
    return kernel_call(
        window_body,
        (shape(own.shape, f32), shape((STAT_ROWS, LANES), f32)),
        [pltpu.VMEM(k.shape, bf16), pltpu.VMEM(v.shape, bf16), pltpu.SemaphoreType.DMA((2,))],
        lengths, own, k, v, scalars=1, hbm=(2, 3),
    )


def merge_parts(parts, suffix, stats, chosen, *weights):
    dims = (QUERY_HEADS * DEST_ROWS, HEAD_SIZE)
    return kernel_call(
        merge_body,
        (shape(dims, bf16), *(shape(w.shape, bf16) for w in weights)),
        [
            pltpu.VMEM(dims, f32),
            pltpu.VMEM((2 * QUERY_HEADS, HEAD_SIZE), f32),
            pltpu.SemaphoreType.DMA((len(weights),)),
        ],
        parts, suffix, stats, chosen, *weights, hbm=range(4, 4 + len(weights)),
    )


def project(place, attn, pieces):
    count = attn.shape[0] // DEST_ROWS
    near, blocks = count // SPREAD, pieces[0].shape[1] // LANES
    size = 2 * SPREAD * blocks
    return kernel_call(
        project_body,
        (
            shape((near, size, LANES), bf16),
            shape((2 * count, LANES), f32),
            shape((size, LANES), f32),
        ),
        [pltpu.VMEM(attn.shape, f32), pltpu.VMEM((blocks, 2 * count, LANES), f32)],
        place, attn, *pieces, scalars=1,
    )


def sum_parts(parts, residual, heads):
    return kernel_call(
        sum_body, (shape((heads, *parts.shape[1:]), bf16),), [], parts, residual
    )[0]


def run_experts(first, x, chosen, marks, gain, router, gate, up, down):
    count, size, _ = x.shape
    return kernel_call(
        expert_body,
        (shape(x.shape, bf16), shape((size, LANES), f32)),
        [
            pltpu.VMEM((count * size, LANES), f32),
            pltpu.VMEM((size // 2, 2 * count, LANES), f32),
            pltpu.VMEM(down.shape, bf16),
            pltpu.SemaphoreType.DMA((down.shape[0],)),
        ],
        first, x, chosen, marks, gain, router, gate, up, down, scalars=1, hbm=(8,),
    )


def add_parts(parts, hidden):
    size = parts.shape[1]
    return kernel_call(
        final_body,
        (shape((2, size // 2 * LANES), f32),),
        [pltpu.VMEM((size, LANES), f32)],
        parts, hidden,
    )[0]


def chosen_lines(ids):
    mask = jnp.any(ids[..., None] == jnp.arange(LANES, dtype=jnp.int32), 1)
    return mask.astype(f32)


def layer(
    queries,
    shared_prefix_keys,
    shared_prefix_values,
    row_suffix_keys,
    row_suffix_values,
    suffix_lengths,
    residual,
    out_weight,
    norm_gain,
    router_weight,
    gate_weights,
    up_weights,
    down_weights,
    expert_ids,
):
    heads = lax.axis_size("head")
    dests = lax.axis_size("grp")
    block = lax.axis_index("grp").astype(jnp.int32).reshape(1)
    expert = (lax.axis_index("head") * gate_weights.shape[0]).astype(jnp.int32).reshape(1)
    send, own, marks = prefix_attention(
        block, expert, queries[0], shared_prefix_keys[0], shared_prefix_values[0], dests
    )
    arrived = exchange(send, "grp")
    near = heads // SPREAD
    place = (lax.axis_index("head") // near).astype(jnp.int32).reshape(1)
    pieces = list(pack_weights(place, out_weight, residual[0]))
    for s in range(1, SPREAD):
        ring = [(h, (h + s * near) % heads) for h in range(heads)]
        pieces[s] = lax.ppermute(pieces[s], "head", ring)
    suffix, stats = fill_window(
        suffix_lengths,
        own,
        row_suffix_keys.reshape(-1, row_suffix_keys.shape[-1]),
        row_suffix_values.reshape(-1, row_suffix_values.shape[-1]),
    )
    chosen = chosen_lines(expert_ids[0])
    attn, router, up = merge_parts(
        arrived, suffix, stats, chosen, router_weight.T, up_weights
    )
    attn = exchange(attn.reshape(heads, DEST_ROWS, HEAD_SIZE), "head")
    parts, chosen, residual_lines = project(
        place, attn.reshape(heads * DEST_ROWS, HEAD_SIZE), pieces
    )
    groups = [[y * near + n for n in range(near)] for y in range(SPREAD)]
    parts = exchange(parts, "head", groups)
    x = exchange(sum_parts(parts, residual_lines, heads), "head")
    made, hidden = run_experts(
        expert, x, chosen, marks, norm_gain[None], router, gate_weights, up, down_weights
    )
    return add_parts(exchange(made, "head"), hidden)[None]


def solution(mesh):
    return jax.shard_map(
        layer,
        mesh=mesh,
        in_specs=(
            P("head", None, None),
            P("head", "grp", None),
            P("head", "grp", None),
            P("head", "grp", None, None),
            P("head", "grp", None, None),
            P("head", "grp"),
            P("head", "grp", None),
            P("head", None),
            P(),
            P(),
            P("head", None, None),
            P("head", None, None),
            P("head", None, None),
            P("head", "grp", None),
        ),
        out_specs=P("head", "grp", None),
        check_vma=False,
    )
```

time: 120 us -> 141 us (1.18)
  starting transfers between devices: 16.9 us -> 43.5 us
  blocking collectives: 71.6 us -> 46.1 us
  local copies, waits for them, and re-layouts: 0.65 us -> 12.2 us
  waiting for transfers between devices: 17.9 us -> 24.2 us
  Pallas kernels: 12.1 us -> 13.9 us
    all_to_all x4 -> x3, blocking collectives: 71.6 us -> 46.1 us  [exchange(): lax.all_to_all(x, axis, split_axis=0, concat_axis=0, tiled=True, axis_ind...]
    ppermute x0 -> x3, starting transfers between devices: none -> 14.6 us  [layer(): pieces[s] = lax.ppermute(pieces[s], 'head', ring)]
    all_to_all x1 -> x2, starting transfers between devices: 16.9 us -> 28.9 us  [exchange(): lax.all_to_all(x, axis, split_axis=0, concat_axis=0, tiled=True, axis_ind...]
    unnamed x4 -> x30, local copies, waits for them, and re-layouts: 0.65 us -> 12.2 us
    ppermute x0 -> x3, waiting for transfers between devices: none -> 7.93 us  [layer(): pieces[s] = lax.ppermute(pieces[s], 'head', ring)]
    pallas_call x7 -> x8, Pallas kernels: 12.1 us -> 13.9 us  [kernel_call(): pl.pallas_call(body, out_shape=outs, in_specs=specs, out_specs=tuple((raw...]
    all_to_all x1 -> x2, waiting for transfers between devices: 17.9 us -> 16.3 us  [exchange(): lax.all_to_all(x, axis, split_axis=0, concat_axis=0, tiled=True, axis_ind...]
  transfers between devices with their start and end apart: 1 -> 5, of which waited for: 1 -> 3; matrix products, arithmetic and copies ran while one was open for 1% -> 1% of each run, Pallas kernels for 1% -> 3%
where the time goes in v4:
time: 141 us
  blocking collectives  46.1 us (33%)
  starting transfers between devices  43.5 us (31%)
  waiting for transfers between devices  24.2 us (17%)
  Pallas kernels  13.9 us (10%)
  local copies, waits for them, and re-layouts  12.2 us (9%)
    all_to_all x3, blocking collectives, exchange(): lax.all_to_all(x, axis, split_axis=0, concat_axis=0, tiled=True, axis_ind...  46.1 us
    all_to_all x2, starting transfers between devices, exchange(): lax.all_to_all(x, axis, split_axis=0, concat_axis=0, tiled=True, axis_ind...  28.9 us
    all_to_all x2, waiting for transfers between devices, exchange(): lax.all_to_all(x, axis, split_axis=0, concat_axis=0, tiled=True, axis_ind...  16.3 us
    ppermute x3, starting transfers between devices, layer(): pieces[s] = lax.ppermute(pieces[s], 'head', ring)  14.6 us
    pallas_call x8, Pallas kernels, kernel_call(): pl.pallas_call(body, out_shape=outs, in_specs=specs, out_specs=tuple((raw...  13.9 us
    unnamed x30, local copies, waits for them, and re-layouts  12.2 us
    ppermute x3, waiting for transfers between devices, layer(): pieces[s] = lax.ppermute(pieces[s], 'head', ring)  7.93 us
  transfers between devices with their start and end apart: 5, of which 3 were waited for; matrix products, arithmetic and copies ran while one was open for 1% of the time, Pallas kernels for 3%

profile of v4, /device:TPU:1, one launch (start us, length us, event | category | flops | bytes accessed | tf_op | source)
XLA Modules:
  0.0 140.7 jit_solution(10056025396090165963)
XLA Ops:
  0.0 3.7 %shard_map.136 = (bf16[24,72,128]{2,1,0:T(8,128)(2,1)}, f32[64,128]{1,0:T(8,128)S(1)}, f32[8,128]{1,0:T(8,128)S(1)}) custom-call(s32[1]{0:T(128)} %bitcast.2.block_ref, s32[1]{0:T(128)} %bitcast.expert_ref.first_ref, bf16[48,4096]{1,0:T(8,128)(2,1)} %bitcast.18, bf16[128,512]{1,0:T(8,128)(2,1)} %bitcast.20, bf16[128,512]{1,0:T(8,128)(2,1)} %bitcast.21), custom_call_target="tpu_custom_call" | custom-call | tf_op jit(solution)/shard_map/pallas_call | solution.py:44
  3.7 16.9 %all-to-all-start = ((bf16[24,72,128]{2,1,0:T(8,128)(2,1)}), bf16[24,72,128]{2,1,0:T(8,128)(2,1)S(1)}, u32[]{:S(2)}, u32[]{:S(2)}) async-start(bf16[24,72,128]{2,1,0:T(8,128)(2,1)} %get-tuple-element.22), calls=%async_computation | async-start | bytes 884736 | tf_op jit(solution)/shard_map/all_to_all | solution.py:30
  20.7 0.8 fusion
  21.4 0.0 copy-start.14
  21.4 0.6 copy-done.14
  22.1 1.7 %shard_map.137 = (f32[64,128]{1,0:T(8,128)S(1)}, f32[8,128]{1,0:T(8,128)S(1)}) custom-call(s32[1,2]{1,0:T(1,128)S(1)} %copy-done.14, f32[64,128]{1,0:T(8,128)S(1)} %get-tuple-element.23.own_ref, bf16[32,512]{1,0:T(8,128)(2,1)} %bitcast.22, bf16[32,512]{1,0:T(8,128)(2,1)} %bitcast.23), custom_call_target="tpu_custom_call" | custom-call | tf_op jit(solution)/shard_map/pallas_call | solution.py:44
  23.8 16.3 %all-to-all-done.part_ref = bf16[24,72,128]{2,1,0:T(8,128)(2,1)S(1)} async-done(((bf16[24,72,128]{2,1,0:T(8,128)(2,1)}), bf16[24,72,128]{2,1,0:T(8,128)(2,1)S(1)}, u32[]{:S(2)}, u32[]{:S(2)}) %all-to-all-start) | async-done | bytes 442400 | tf_op jit(solution)/shard_map/all_to_all | solution.py:30
  40.0 0.0 copy-start.3
  40.0 0.8 copy-done.3
  40.8 0.0 copy-start.4
  40.8 1.0 copy-done.4
  41.8 0.0 copy-start
  41.8 0.0 copy-start.13
  41.8 2.1 %shard_map.138 = (bf16[512,128]{1,0:T(8,128)(2,1)S(1)}, bf16[64,2048]{1,0:T(8,128)(2,1)S(1)}, bf16[2,2048,384]{2,1,0:T(8,128)(2,1)S(1)}) custom-call(bf16[24,72,128]{2,1,0:T(8,128)(2,1)S(1)} %copy-done.4, f32[64,128]{1,0:T(8,128)S(1)} %get-tuple-element.24.suffix_ref, f32[8,128]{1,0:T(8,128)S(1)} %get-tuple-element.25.stat_ref, ...), custom_call_target="tpu_custom_call" | custom-call | tf_op jit(solution)/shard_map/pallas_call | solution.py:44
  43.9 0.0 copy-start.1
  44.0 1.6 %copy-done.1 = bf16[2,2048,384]{2,1,0:T(8,128)(2,1)} copy-done((bf16[2,2048,384]{2,1,0:T(8,128)(2,1)}, bf16[2,2048,384]{2,1,0:T(8,128)(2,1)S(1)}, u32[]{:S(2)}) %copy-start.1) | copy-done | bytes 3145752
  45.6 0.0 copy-start.12
  45.6 0.7 copy-done.12
  46.2 12.0 %all-to-all-start.1 = ((bf16[32,16,128]{2,1,0:T(8,128)(2,1)}), bf16[32,16,128]{2,1,0:T(8,128)(2,1)S(1)}, u32[]{:S(2)}, u32[]{:S(2)}) async-start(bf16[32,16,128]{2,1,0:T(8,128)(2,1)} %bitcast.16), calls=%async_computation.1 | async-start | bytes 262144 | tf_op jit(solution)/shard_map/all_to_all | solution.py:30
  58.2 2.0 %shard_map.139 = (bf16[136,512]{1,0:T(8,128)(2,1)}, bf16[136,512]{1,0:T(8,128)(2,1)}, bf16[136,512]{1,0:T(8,128)(2,1)}, bf16[136,512]{1,0:T(8,128)(2,1)}) custom-call(s32[1]{0:T(128)} %bitcast.1.place_ref, bf16[128,2048]{1,0:T(8,128)(2,1)} %weight_hbm.1, bf16[2,2048]{1,0:T(2,128)(2,1)} %bitcast.24), custom_call_target="tpu_custom_call" | custom-call | tf_op jit(solution)/shard_map/pallas_call | solution.py:44
  60.2 4.2 %collective-permute-start = (bf16[136,512]{1,0:T(8,128)(2,1)}, bf16[136,512]{1,0:T(8,128)(2,1)S(1)}, u32[]{:S(2)}, u32[]{:S(2)}) collective-permute-start(bf16[136,512]{1,0:T(8,128)(2,1)} %get-tuple-element.28), channel_id=1, source_target_pairs={{0,8},{1,9},{2,10},{3,11},{4,12},{5,13},{6,14},{7,15},{8,16},{9,17... | collective-permute-start | bytes 417800 | tf_op jit(solution)/shard_map/ppermute | solution.py:498
  64.3 5.2 %collective-permute-start.1 = (bf16[136,512]{1,0:T(8,128)(2,1)}, bf16[136,512]{1,0:T(8,128)(2,1)S(1)}, u32[]{:S(2)}, u32[]{:S(2)}) collective-permute-start(bf16[136,512]{1,0:T(8,128)(2,1)} %get-tuple-element.29), channel_id=1, source_target_pairs={{0,16},{1,17},{2,18},{3,19},{4,20},{5,21},{6,22},{7,23},{8,24},{9,... | collective-permute-start | bytes 417800 | tf_op jit(solution)/shard_map/ppermute | solution.py:498
  69.6 5.2 %collective-permute-start.2 = (bf16[136,512]{1,0:T(8,128)(2,1)}, bf16[136,512]{1,0:T(8,128)(2,1)S(1)}, u32[]{:S(2)}, u32[]{:S(2)}) collective-permute-start(bf16[136,512]{1,0:T(8,128)(2,1)} %get-tuple-element.30), channel_id=1, source_target_pairs={{0,24},{1,25},{2,26},{3,27},{4,28},{5,29},{6,30},{7,31},{8,0},{9,1... | collective-permute-start | bytes 417800 | tf_op jit(solution)/shard_map/ppermute | solution.py:498
  74.8 0.0 collective-permute-done.refs_1_
  74.8 0.0 copy-start.6
  74.8 0.6 copy-done.6
  75.4 2.8 %collective-permute-done.1.refs_2_ = bf16[136,512]{1,0:T(8,128)(2,1)S(1)} collective-permute-done((bf16[136,512]{1,0:T(8,128)(2,1)}, bf16[136,512]{1,0:T(8,128)(2,1)S(1)}, u32[]{:S(2)}, u32[]{:S(2)}) %collective-permute-start.1) | collective-permute-done | bytes 139296 | tf_op jit(solution)/shard_map/ppermute | solution.py:498
  78.3 0.0 copy-start.8
  78.3 0.7 copy-done.8
  78.9 5.1 %collective-permute-done.2.refs_3_ = bf16[136,512]{1,0:T(8,128)(2,1)S(1)} collective-permute-done((bf16[136,512]{1,0:T(8,128)(2,1)}, bf16[136,512]{1,0:T(8,128)(2,1)S(1)}, u32[]{:S(2)}, u32[]{:S(2)}) %collective-permute-start.2) | collective-permute-done | bytes 139296 | tf_op jit(solution)/shard_map/ppermute | solution.py:498
  84.0 0.0 copy-start.10
  84.0 0.6 copy-done.10
  84.7 0.0 all-to-all-done.1
  84.7 0.0 copy-start.5
  84.7 0.9 copy-done.5
  85.6 0.0 copy-start.7
  85.6 0.9 copy-done.7
  86.5 0.0 copy-start.9
  86.5 0.9 copy-done.9
  87.4 0.0 copy-start.11
  87.4 0.9 copy-done.11
  88.3 0.3 shard_map.140
  88.6 9.6 %all_to_all.25.part_ref = bf16[8,32,128]{2,1,0:T(8,128)(2,1)S(1)} all-to-all(bf16[8,32,128]{2,1,0:T(8,128)(2,1)S(1)} %get-tuple-element.31), channel_id=1, replica_groups={{0,1,2,3,4,5,6,7},{8,9,10,11,12,13,14,15},{16,17,18,19,20,21,22,23},{24..., dimensions={0} | all-to-all | bytes 131072 | tf_op jit(solution)/shard_map/all_to_all | solution.py:30
  98.2 20.6 %all_to_all.26.x_ref = bf16[32,32,128]{2,1,0:T(8,128)(2,1)S(1)} all-to-all(bf16[32,32,128]{2,1,0:T(8,128)(2,1)S(1)} %shard_map.141), channel_id=1, replica_groups=mesh['grp'=24,'head'=32] {'head'}, dimensions={0} | all-to-all | bytes 524288 | tf_op jit(solution)/shard_map/all_to_all | solution.py:30
  118.9 0.0 copy-done
  118.9 0.0 copy-done.13
  118.9 0.0 copy-start.2
  118.9 1.9 %copy-done.2 = bf16[2,2048,384]{2,1,0:T(8,128)(2,1)S(1)} copy-done((bf16[2,2048,384]{2,1,0:T(8,128)(2,1)S(1)}, bf16[2,2048,384]{2,1,0:T(8,128)(2,1)}, u32[]{:S(2)}) %copy-start.2) | copy-done | bytes 3145752
  120.8 3.5 %shard_map.142 = (bf16[32,32,128]{2,1,0:T(8,128)(2,1)S(1)}, f32[32,128]{1,0:T(8,128)S(1)}) custom-call(s32[1]{0:T(128)} %bitcast.expert_ref.first_ref, bf16[32,32,128]{2,1,0:T(8,128)(2,1)S(1)} %all_to_all.26.x_ref, f32[64,128]{1,0:T(8,128)S(1)} %get-tuple-element.33.chosen_ref, f32[8,128]{1,0:T(8,128)S(1)} %get-tuple-element.34.mark_ref, ...), custom_call_target="tpu_custom_call" | custom-call | tf_op jit(solution)/shard_map/pallas_call | solution.py:44
  124.3 15.8 %all_to_all.27.part_ref = bf16[32,32,128]{2,1,0:T(8,128)(2,1)S(1)} all-to-all(bf16[32,32,128]{2,1,0:T(8,128)(2,1)S(1)} %get-tuple-element.37), channel_id=1, replica_groups=mesh['grp'=24,'head'=32] {'head'}, dimensions={0} | all-to-all | bytes 524288 | tf_op jit(solution)/shard_map/all_to_all | solution.py:30
  140.1 0.7 shard_map.143
  (2 shorter events, 0.0 us)
Async XLA Ops:
  3.7 36.3 %all-to-all-start = ((bf16[24,72,128]{2,1,0:T(8,128)(2,1)}), bf16[24,72,128]{2,1,0:T(8,128)(2,1)S(1)}, u32[]{:S(2)}, u32[]{:S(2)}) async-start(bf16[24,72,128]{2,1,0:T(8,128)(2,1)} %get-tuple-element.22), calls=%async_computation | async-start | bytes 884736 | tf_op jit(solution)/shard_map/all_to_all | solution.py:30
  21.4 0.7 copy-start.14
  40.0 0.8 copy-start.3
  40.8 1.0 copy-start.4
  41.8 77.1 %copy-start = (bf16[2,2048,384]{2,1,0:T(8,128)(2,1)S(1)}, bf16[2,2048,384]{2,1,0:T(8,128)(2,1)}, u32[]{:S(2)}) copy-start(bf16[2,2048,384]{2,1,0:T(8,128)(2,1)} %gate.1) | copy-start | bytes 9437188
  41.8 77.1 %copy-start.13 = (f32[2048]{0:T(1024)S(1)}, f32[2048]{0:T(1024)}, u32[]{:S(2)}) copy-start(f32[2048]{0:T(1024)} %param.22) | copy-start | bytes 24580
  43.9 1.6 %copy-start.1 = (bf16[2,2048,384]{2,1,0:T(8,128)(2,1)}, bf16[2,2048,384]{2,1,0:T(8,128)(2,1)S(1)}, u32[]{:S(2)}) copy-start(bf16[2,2048,384]{2,1,0:T(8,128)(2,1)S(1)} %get-tuple-element.36.up) | copy-start | bytes 9437188
  45.6 0.7 copy-start.12
  46.2 38.5 %all-to-all-start.1 = ((bf16[32,16,128]{2,1,0:T(8,128)(2,1)}), bf16[32,16,128]{2,1,0:T(8,128)(2,1)S(1)}, u32[]{:S(2)}, u32[]{:S(2)}) async-start(bf16[32,16,128]{2,1,0:T(8,128)(2,1)} %bitcast.16), calls=%async_computation.1 | async-start | bytes 262144 | tf_op jit(solution)/shard_map/all_to_all | solution.py:30
  60.2 14.6 %collective-permute-start = (bf16[136,512]{1,0:T(8,128)(2,1)}, bf16[136,512]{1,0:T(8,128)(2,1)S(1)}, u32[]{:S(2)}, u32[]{:S(2)}) collective-permute-start(bf16[136,512]{1,0:T(8,128)(2,1)} %get-tuple-element.28), channel_id=1, source_target_pairs={{0,8},{1,9},{2,10},{3,11},{4,12},{5,13},{6,14},{7,15},{8,16},{9,17... | collective-permute-start | bytes 417800 | tf_op jit(solution)/shard_map/ppermute | solution.py:498
  64.3 13.9 %collective-permute-start.1 = (bf16[136,512]{1,0:T(8,128)(2,1)}, bf16[136,512]{1,0:T(8,128)(2,1)S(1)}, u32[]{:S(2)}, u32[]{:S(2)}) collective-permute-start(bf16[136,512]{1,0:T(8,128)(2,1)} %get-tuple-element.29), channel_id=1, source_target_pairs={{0,16},{1,17},{2,18},{3,19},{4,20},{5,21},{6,22},{7,23},{8,24},{9,... | collective-permute-start | bytes 417800 | tf_op jit(solution)/shard_map/ppermute | solution.py:498
  69.6 14.4 %collective-permute-start.2 = (bf16[136,512]{1,0:T(8,128)(2,1)}, bf16[136,512]{1,0:T(8,128)(2,1)S(1)}, u32[]{:S(2)}, u32[]{:S(2)}) collective-permute-start(bf16[136,512]{1,0:T(8,128)(2,1)} %get-tuple-element.30), channel_id=1, source_target_pairs={{0,24},{1,25},{2,26},{3,27},{4,28},{5,29},{6,30},{7,31},{8,0},{9,1... | collective-permute-start | bytes 417800 | tf_op jit(solution)/shard_map/ppermute | solution.py:498
  74.8 0.7 copy-start.6
  78.3 0.7 copy-start.8
  84.0 0.7 copy-start.10
  84.7 0.9 copy-start.5
  85.6 0.9 copy-start.7
  86.5 0.9 copy-start.9
  87.4 0.9 copy-start.11
  118.9 1.9 %copy-start.2 = (bf16[2,2048,384]{2,1,0:T(8,128)(2,1)S(1)}, bf16[2,2048,384]{2,1,0:T(8,128)(2,1)}, u32[]{:S(2)}) copy-start(bf16[2,2048,384]{2,1,0:T(8,128)(2,1)} %copy-done.1) | copy-start | bytes 9437188

commit v5 on v4

--- a/solution.py
+++ b/solution.py
@@ -16,6 +16,7 @@
 STAT_ROWS = 8
 DEST_ROWS = 16
 SPREAD = 4
+EXPERTS_HERE = 2
 EXTRA_ROWS = 8
 
 masked_score = -1e30
@@ -32,11 +33,10 @@
     )
 
 
-def kernel_call(body, outs, scratch, *args, scalars=0, hbm=(), hbm_outs=()):
-    smem = pl.BlockSpec(memory_space=pltpu.SMEM)
+def kernel_call(body, outs, scratch, *args, hbm=(), hbm_outs=()):
     vmem = pl.BlockSpec(memory_space=pltpu.VMEM)
     raw = pl.BlockSpec(memory_space=pltpu.HBM)
-    specs = [smem if i < scalars else raw if i in hbm else vmem for i in range(len(args))]
+    specs = [raw if i in hbm else vmem for i in range(len(args))]
     args = [
         pltpu.with_memory_space_constraint(a, pltpu.HBM) if i in hbm else a
         for i, a in enumerate(args)
@@ -75,7 +75,7 @@
 
 
 def prefix_body(
-    block_ref, expert_ref, q_hbm, k_hbm, v_hbm, out_hbm, own_ref, mark_ref,
+    q_hbm, k_hbm, v_hbm, out_hbm, own_ref, mark_ref,
     q_in, k_in, v_in, q_rows, stats, rests, made, in_sems, out_sems,
 ):
     rows = q_hbm.shape[0]
@@ -93,8 +93,9 @@
     rests[...] = jnp.zeros(rests.shape, f32)
     lane = lax.broadcasted_iota(jnp.int32, mark_ref.shape, 1)
     row = lax.broadcasted_iota(jnp.int32, mark_ref.shape, 0)
-    mark_ref[...] = (lane == expert_ref[0] + row).astype(f32)
-    start = pl.multiple_of(block_ref[0] * per_dest, per_dest)
+    first = lax.axis_index("head") * EXPERTS_HERE
+    mark_ref[...] = (lane == first + row).astype(f32)
+    start = pl.multiple_of(lax.axis_index("grp") * per_dest, per_dest)
     departures = []
     for k in range(KEY_VALUE_HEADS):
         arrivals[k].wait()
@@ -134,16 +135,21 @@
         copy.wait()
 
 
-def pack_body(place_ref, weight_hbm, residual_hbm, *refs):
+def place_of(heads):
+    return lax.axis_index("head") // (heads // SPREAD)
+
+
+def pack_body(weight_hbm, residual_hbm, *refs):
     outs, (weight, residual, extra, extras, sems) = refs[:SPREAD], refs[SPREAD:]
     depth, width = weight.shape[0], outs[0].shape[1]
+    place = place_of(QUERY_HEADS)
     load = start_copy(weight_hbm, weight, sems.at[0])
     small = start_copy(residual_hbm, residual, sems.at[1])
     small.wait()
     copies = []
     starts = []
     for s in range(SPREAD):
-        start = pl.multiple_of(((place_ref[0] + s) & (SPREAD - 1)) * width, width)
+        start = pl.multiple_of(((place + s) & (SPREAD - 1)) * width, width)
         starts.append(start)
         extra[...] = jnp.zeros(extra.shape, f32)
         extra[0:2, :] = residual[:, pl.ds(start, width)].astype(f32)
@@ -159,8 +165,10 @@
         copy.wait()
 
 
-def window_body(length_ref, own_ref, k_hbm, v_hbm, out_ref, stat_ref, k_ref, v_ref, sems):
-    pairs = ((k_hbm, k_ref), (v_hbm, v_ref))
+def window_body(
+    own_ref, length_hbm, k_hbm, v_hbm, out_ref, stat_ref, length_ref, k_ref, v_ref, sems
+):
+    pairs = ((length_hbm, length_ref), (k_hbm, k_ref), (v_hbm, v_ref))
     copies = [start_copy(a, b, sems.at[n]) for n, (a, b) in enumerate(pairs)]
     for copy in copies:
         copy.wait()
@@ -174,7 +182,7 @@
     row = lax.broadcasted_iota(jnp.int32, (keys, per_dest), 0)
     lane = lax.broadcasted_iota(jnp.int32, (keys, per_dest), 1)
     second = row >= half
-    limit = jnp.where(second, length_ref[0, 1] + half, length_ref[0, 0])
+    limit = jnp.where(second, length_ref[:, 1:2] + half, length_ref[:, 0:1])
     inside = (second == (lane >= GROUP)) & (row < limit)
     stat_ref[...] = jnp.zeros(stat_ref.shape, f32)
     for k in range(KEY_VALUE_HEADS):
@@ -192,11 +200,18 @@
 
 
 def merge_body(
-    part_ref, suffix_ref, stat_ref, chosen_ref, router_hbm, up_hbm,
-    out_ref, router_ref, up_ref, rows, heads, sems,
+    suffix_ref, stat_ref, part_hbm, id_hbm, router_hbm, up_hbm,
+    out_ref, router_ref, up_ref, part_ref, id_ref, rows, heads, sems,
 ):
-    pairs = ((router_hbm, router_ref), (up_hbm, up_ref))
+    pairs = (
+        (part_hbm, part_ref),
+        (id_hbm, id_ref),
+        (router_hbm, router_ref),
+        (up_hbm, up_ref),
+    )
     copies = [start_copy(a, b, sems.at[n]) for n, (a, b) in enumerate(pairs)]
+    rows[...] = jnp.zeros(rows.shape, f32)
+    copies[0].wait()
     sources = part_ref.shape[0]
     per_dest = suffix_ref.shape[0] // KEY_VALUE_HEADS
     first = KEY_VALUE_HEADS * per_dest
@@ -219,7 +234,6 @@
     turned = jnp.concatenate(
         [table[i : i + LANES].T[0:per_dest] for i in range(0, table.shape[0], LANES)], 1
     )
-    rows[...] = jnp.zeros(rows.shape, f32)
     for k in range(KEY_VALUE_HEADS):
         mine = slice(k * per_dest, (k + 1) * per_dest)
         mixed = turned[:, k : k + 1] * suffix_ref[mine, :]
@@ -239,15 +253,20 @@
                 rows[pl.ds(at, near, stride=DEST_ROWS), :] = heads[
                     i * QUERY_HEADS + source : i * QUERY_HEADS + source + near, :
                 ]
+    copies[1].wait()
+    lane = lax.broadcasted_iota(jnp.int32, (QUERY_HEADS, LANES), 1)
     for i in range(2):
-        line = jnp.broadcast_to(chosen_ref[i : i + 1, :], (QUERY_HEADS, LANES))
+        chosen = lane == id_ref[i : i + 1, 0:1]
+        for n in range(1, id_ref.shape[1]):
+            chosen = chosen | (lane == id_ref[i : i + 1, n : n + 1])
+        line = chosen.astype(f32)
         rows[pl.ds(2 * SPREAD + i, QUERY_HEADS, stride=DEST_ROWS), :] = line
     out_ref[...] = rows[...].astype(bf16)
-    for copy in copies:
+    for copy in copies[2:]:
         copy.wait()
 
 
-def project_body(place_ref, attn_ref, *refs):
+def project_body(attn_ref, *refs):
     pieces, (out_ref, chosen_ref, residual_ref, rows, lines) = refs[:SPREAD], refs[SPREAD:]
     count = attn_ref.shape[0] // DEST_ROWS
     depth = pieces[0].shape[0] - EXTRA_ROWS
@@ -263,7 +282,7 @@
         attn = jnp.concatenate(attn, 0).astype(bf16)
         made = made + jnp.dot(attn, pieces[s][0:depth, :], preferred_element_type=f32)
         extra = pieces[s][depth : depth + EXTRA_ROWS, :].astype(f32)
-        source = (place_ref[0] + SPREAD - s) & (SPREAD - 1)
+        source = (place_of(count) + SPREAD - s) & (SPREAD - 1)
         for i in range(2):
             for c in range(blocks):
                 residual_ref[pl.ds(c * 2 * SPREAD + i * SPREAD + source, 1), :] = extra[
@@ -294,7 +313,7 @@
 
 
 def expert_body(
-    first_ref, x_ref, chosen_ref, mark_ref, gain_ref, router_ref, gate, up, down_hbm,
+    x_ref, chosen_ref, mark_ref, gain_ref, router_ref, gate, up, down_hbm,
     out_ref, hidden_ref, lines, x_rows, down, sems,
 ):
     experts = gate.shape[0]
@@ -303,7 +322,7 @@
     near = count // SPREAD
     pairs = 2 * SPREAD
     blocks = size // pairs
-    own = first_ref[0] // experts
+    own = lax.axis_index("head")
     far = own // near
     lines[...] = x_ref[...].astype(f32).reshape(lines.shape)
     for y in range(SPREAD):
@@ -346,7 +365,7 @@
         out_ref[:, c * LANES : (c + 1) * LANES] = lines[pl.ds(c, 2, stride=blocks), :]
 
 
-def prefix_attention(block, expert, q, k, v, dests):
+def prefix_attention(q, k, v, dests):
     rows = q.shape[0]
     per_dest = rows * GROUP // dests
     send = (dests, KEY_VALUE_HEADS * per_dest + STAT_ROWS, HEAD_SIZE)
@@ -369,12 +388,12 @@
             pltpu.SemaphoreType.DMA((KEY_VALUE_HEADS + 2,)),
             pltpu.SemaphoreType.DMA((KEY_VALUE_HEADS + 1,)),
         ],
-        block, expert, q, k, v, scalars=2, hbm=(2, 3, 4), hbm_outs=(0,),
+        q, k, v, hbm=(0, 1, 2), hbm_outs=(0,),
     )
     return made, own, marks
 
 
-def pack_weights(place, weight, residual):
+def pack_weights(weight, residual):
     width = weight.shape[1] // SPREAD
     dims = (weight.shape[0] + EXTRA_ROWS, width)
     return kernel_call(
@@ -387,7 +406,7 @@
             pltpu.VMEM((SPREAD, EXTRA_ROWS, width), bf16),
             pltpu.SemaphoreType.DMA((2 + 2 * SPREAD,)),
         ],
-        place, weight, residual, scalars=1, hbm=(1, 2), hbm_outs=range(SPREAD),
+        weight, residual, hbm=(0, 1), hbm_outs=range(SPREAD),
     )
 
 
@@ -395,26 +414,33 @@
     return kernel_call(
         window_body,
         (shape(own.shape, f32), shape((STAT_ROWS, LANES), f32)),
-        [pltpu.VMEM(k.shape, bf16), pltpu.VMEM(v.shape, bf16), pltpu.SemaphoreType.DMA((2,))],
-        lengths, own, k, v, scalars=1, hbm=(2, 3),
-    )
-
-
-def merge_parts(parts, suffix, stats, chosen, *weights):
+        [
+            pltpu.VMEM(lengths.shape, jnp.int32),
+            pltpu.VMEM(k.shape, bf16),
+            pltpu.VMEM(v.shape, bf16),
+            pltpu.SemaphoreType.DMA((3,)),
+        ],
+        own, lengths, k, v, hbm=(1, 2, 3),
+    )
+
+
+def merge_parts(suffix, stats, parts, ids, *weights):
     dims = (QUERY_HEADS * DEST_ROWS, HEAD_SIZE)
     return kernel_call(
         merge_body,
         (shape(dims, bf16), *(shape(w.shape, bf16) for w in weights)),
         [
+            pltpu.VMEM(parts.shape, bf16),
+            pltpu.VMEM(ids.shape, jnp.int32),
             pltpu.VMEM(dims, f32),
             pltpu.VMEM((2 * QUERY_HEADS, HEAD_SIZE), f32),
-            pltpu.SemaphoreType.DMA((len(weights),)),
+            pltpu.SemaphoreType.DMA((2 + len(weights),)),
         ],
-        parts, suffix, stats, chosen, *weights, hbm=range(4, 4 + len(weights)),
-    )
-
-
-def project(place, attn, pieces):
+        suffix, stats, parts, ids, *weights, hbm=range(2, 4 + len(weights)),
+    )
+
+
+def project(attn, pieces):
     count = attn.shape[0] // DEST_ROWS
     near, blocks = count // SPREAD, pieces[0].shape[1] // LANES
     size = 2 * SPREAD * blocks
@@ -426,7 +452,7 @@
             shape((size, LANES), f32),
         ),
         [pltpu.VMEM(attn.shape, f32), pltpu.VMEM((blocks, 2 * count, LANES), f32)],
-        place, attn, *pieces, scalars=1,
+        attn, *pieces,
     )
 
 
@@ -436,7 +462,7 @@
     )[0]
 
 
-def run_experts(first, x, chosen, marks, gain, router, gate, up, down):
+def run_experts(x, chosen, marks, gain, router, gate, up, down):
     count, size, _ = x.shape
     return kernel_call(
         expert_body,
@@ -447,7 +473,7 @@
             pltpu.VMEM(down.shape, bf16),
             pltpu.SemaphoreType.DMA((down.shape[0],)),
         ],
-        first, x, chosen, marks, gain, router, gate, up, down, scalars=1, hbm=(8,),
+        x, chosen, marks, gain, router, gate, up, down, hbm=(7,),
     )
 
 
@@ -459,11 +485,6 @@
         [pltpu.VMEM((size, LANES), f32)],
         parts, hidden,
     )[0]
-
-
-def chosen_lines(ids):
-    mask = jnp.any(ids[..., None] == jnp.arange(LANES, dtype=jnp.int32), 1)
-    return mask.astype(f32)
 
 
 def layer(
@@ -484,37 +505,34 @@
 ):
     heads = lax.axis_size("head")
     dests = lax.axis_size("grp")
-    block = lax.axis_index("grp").astype(jnp.int32).reshape(1)
-    expert = (lax.axis_index("head") * gate_weights.shape[0]).astype(jnp.int32).reshape(1)
     send, own, marks = prefix_attention(
-        block, expert, queries[0], shared_prefix_keys[0], shared_prefix_values[0], dests
+        queries[0], shared_prefix_keys[0], shared_prefix_values[0], dests
     )
     arrived = exchange(send, "grp")
     near = heads // SPREAD
-    place = (lax.axis_index("head") // near).astype(jnp.int32).reshape(1)
-    pieces = list(pack_weights(place, out_weight, residual[0]))
+    pieces = list(pack_weights(out_weight, residual[0]))
     for s in range(1, SPREAD):
         ring = [(h, (h + s * near) % heads) for h in range(heads)]
         pieces[s] = lax.ppermute(pieces[s], "head", ring)
+        pieces[s] = pltpu.with_memory_space_constraint(pieces[s], pltpu.HBM)
     suffix, stats = fill_window(
         suffix_lengths,
         own,
         row_suffix_keys.reshape(-1, row_suffix_keys.shape[-1]),
         row_suffix_values.reshape(-1, row_suffix_values.shape[-1]),
     )
-    chosen = chosen_lines(expert_ids[0])
     attn, router, up = merge_parts(
-        arrived, suffix, stats, chosen, router_weight.T, up_weights
+        suffix, stats, arrived, expert_ids[0], router_weight.T, up_weights
     )
     attn = exchange(attn.reshape(heads, DEST_ROWS, HEAD_SIZE), "head")
     parts, chosen, residual_lines = project(
-        place, attn.reshape(heads * DEST_ROWS, HEAD_SIZE), pieces
+        attn.reshape(heads * DEST_ROWS, HEAD_SIZE), pieces
     )
     groups = [[y * near + n for n in range(near)] for y in range(SPREAD)]
     parts = exchange(parts, "head", groups)
     x = exchange(sum_parts(parts, residual_lines, heads), "head")
     made, hidden = run_experts(
-        expert, x, chosen, marks, norm_gain[None], router, gate_weights, up, down_weights
+        x, chosen, marks, norm_gain[None], router, gate_weights, up, down_weights
     )
     return add_parts(exchange(made, "head"), hidden)[None]
 

time: 141 us -> 138 us (0.979)
  local copies, waits for them, and re-layouts: 12.2 us -> 6.51 us
  waiting for transfers between devices: 24.2 us -> 26.9 us
    unnamed x30 -> x18, local copies, waits for them, and re-layouts: 12.2 us -> 6.51 us
    all_to_all x2, waiting for transfers between devices: 16.3 us -> 18.2 us  [exchange(): lax.all_to_all(x, axis, split_axis=0, concat_axis=0, tiled=True, axis_ind...]
  transfers between devices with their start and end apart: 5 -> 5, of which waited for: 3 -> 3; matrix products, arithmetic and copies ran while one was open for 1% -> 0% of each run, Pallas kernels for 3% -> 2%
where the time goes in v5:
time: 138 us
  blocking collectives  46.1 us (33%)
  starting transfers between devices  43.5 us (32%)
  waiting for transfers between devices  26.9 us (19%)
  Pallas kernels  14.6 us (11%)
  local copies, waits for them, and re-layouts  6.51 us (5%)
    all_to_all x3, blocking collectives, exchange(): lax.all_to_all(x, axis, split_axis=0, concat_axis=0, tiled=True, axis_ind...  46.1 us
    all_to_all x2, starting transfers between devices, exchange(): lax.all_to_all(x, axis, split_axis=0, concat_axis=0, tiled=True, axis_ind...  28.9 us
    all_to_all x2, waiting for transfers between devices, exchange(): lax.all_to_all(x, axis, split_axis=0, concat_axis=0, tiled=True, axis_ind...  18.2 us
    pallas_call x8, Pallas kernels, kernel_call(): pl.pallas_call(body, out_shape=outs, in_specs=specs, out_specs=tuple((raw...  14.6 us
    ppermute x3, starting transfers between devices, layer(): pieces[s] = lax.ppermute(pieces[s], 'head', ring)  14.6 us
    ppermute x3, waiting for transfers between devices, layer(): pieces[s] = lax.ppermute(pieces[s], 'head', ring)  8.7 us
    unnamed x18, local copies, waits for them, and re-layouts  6.51 us
  transfers between devices with their start and end apart: 5, of which 3 were waited for; matrix products, arithmetic and copies ran while one was open for 0% of the time, Pallas kernels for 2%

profile of v5, /device:TPU:1, one launch (start us, length us, event | category | flops | bytes accessed | tf_op | source)
XLA Modules:
  0.0 137.7 jit_solution(14474833824009904704)
XLA Ops:
  0.0 3.7 %shard_map.136 = (bf16[24,72,128]{2,1,0:T(8,128)(2,1)}, f32[64,128]{1,0:T(8,128)S(1)}, f32[8,128]{1,0:T(8,128)S(1)}) custom-call(bf16[48,4096]{1,0:T(8,128)(2,1)} %bitcast.15, bf16[128,512]{1,0:T(8,128)(2,1)} %bitcast.17, bf16[128,512]{1,0:T(8,128)(2,1)} %bitcast.18), custom_call_target="tpu_custom_call" | custom-call | tf_op jit(solution)/shard_map/pallas_call | solution.py:44
  3.7 16.9 %all-to-all-start = ((bf16[24,72,128]{2,1,0:T(8,128)(2,1)}), bf16[24,72,128]{2,1,0:T(8,128)(2,1)S(1)}, u32[]{:S(2)}, u32[]{:S(2)}) async-start(bf16[24,72,128]{2,1,0:T(8,128)(2,1)} %get-tuple-element.25), calls=%async_computation | async-start | bytes 884736 | tf_op jit(solution)/shard_map/all_to_all | solution.py:31
  20.7 1.1 shard_map.137
  21.8 18.2 %all-to-all-done.part_hbm = bf16[24,72,128]{2,1,0:T(8,128)(2,1)S(1)} async-done(((bf16[24,72,128]{2,1,0:T(8,128)(2,1)}), bf16[24,72,128]{2,1,0:T(8,128)(2,1)S(1)}, u32[]{:S(2)}, u32[]{:S(2)}) %all-to-all-start) | async-done | bytes 442400 | tf_op jit(solution)/shard_map/all_to_all | solution.py:31
  40.0 0.0 copy-start.6
  40.0 0.8 copy-done.6
  40.8 0.0 copy-start
  40.8 0.0 copy-start.5
  40.8 2.3 %shard_map.138 = (bf16[512,128]{1,0:T(8,128)(2,1)S(1)}, bf16[64,2048]{1,0:T(8,128)(2,1)S(1)}, bf16[2,2048,384]{2,1,0:T(8,128)(2,1)S(1)}) custom-call(f32[64,128]{1,0:T(8,128)S(1)} %get-tuple-element.23.suffix_ref, f32[8,128]{1,0:T(8,128)S(1)} %get-tuple-element.24.stat_ref, bf16[24,72,128]{2,1,0:T(8,128)(2,1)} %copy-done.6, s32[2,8]{1,0:T(2,128)} %bitcast.22, ...), custom_call_target="tpu_custom_call" | custom-call | tf_op jit(solution)/shard_map/pallas_call | solution.py:44
  43.1 0.0 copy-start.1
  43.1 1.6 %copy-done.1 = bf16[2,2048,384]{2,1,0:T(8,128)(2,1)} copy-done((bf16[2,2048,384]{2,1,0:T(8,128)(2,1)}, bf16[2,2048,384]{2,1,0:T(8,128)(2,1)S(1)}, u32[]{:S(2)}) %copy-start.1) | copy-done | bytes 3145752
  44.8 0.0 copy-start.4
  44.8 0.6 copy-done.4
  45.4 12.0 %all-to-all-start.1 = ((bf16[32,16,128]{2,1,0:T(8,128)(2,1)}), bf16[32,16,128]{2,1,0:T(8,128)(2,1)S(1)}, u32[]{:S(2)}, u32[]{:S(2)}) async-start(bf16[32,16,128]{2,1,0:T(8,128)(2,1)} %bitcast.13), calls=%async_computation.1 | async-start | bytes 262144 | tf_op jit(solution)/shard_map/all_to_all | solution.py:31
  57.4 1.9 %shard_map.139 = (bf16[136,512]{1,0:T(8,128)(2,1)}, bf16[136,512]{1,0:T(8,128)(2,1)}, bf16[136,512]{1,0:T(8,128)(2,1)}, bf16[136,512]{1,0:T(8,128)(2,1)}) custom-call(bf16[128,2048]{1,0:T(8,128)(2,1)} %weight_hbm.1, bf16[2,2048]{1,0:T(2,128)(2,1)} %bitcast.21), custom_call_target="tpu_custom_call" | custom-call | tf_op jit(solution)/shard_map/pallas_call | solution.py:44
  59.3 4.2 %collective-permute-start = (bf16[136,512]{1,0:T(8,128)(2,1)}, bf16[136,512]{1,0:T(8,128)(2,1)S(1)}, u32[]{:S(2)}, u32[]{:S(2)}) collective-permute-start(bf16[136,512]{1,0:T(8,128)(2,1)} %get-tuple-element.28), channel_id=1, source_target_pairs={{0,8},{1,9},{2,10},{3,11},{4,12},{5,13},{6,14},{7,15},{8,16},{9,17... | collective-permute-start | bytes 417800 | tf_op jit(solution)/shard_map/ppermute | solution.py:516
  63.5 5.2 %collective-permute-start.1 = (bf16[136,512]{1,0:T(8,128)(2,1)}, bf16[136,512]{1,0:T(8,128)(2,1)S(1)}, u32[]{:S(2)}, u32[]{:S(2)}) collective-permute-start(bf16[136,512]{1,0:T(8,128)(2,1)} %get-tuple-element.29), channel_id=1, source_target_pairs={{0,16},{1,17},{2,18},{3,19},{4,20},{5,21},{6,22},{7,23},{8,24},{9,... | collective-permute-start | bytes 417800 | tf_op jit(solution)/shard_map/ppermute | solution.py:516
  68.7 5.2 %collective-permute-start.2 = (bf16[136,512]{1,0:T(8,128)(2,1)}, bf16[136,512]{1,0:T(8,128)(2,1)}, u32[]{:S(2)}, u32[]{:S(2)}) collective-permute-start(bf16[136,512]{1,0:T(8,128)(2,1)} %get-tuple-element.30), channel_id=1, source_target_pairs={{0,24},{1,25},{2,26},{3,27},{4,28},{5,29},{6,30},{7,31},{8,0},{9,1... | collective-permute-start | bytes 417800 | tf_op jit(solution)/shard_map/ppermute | solution.py:516
  73.9 0.0 collective-permute-done.refs_1_
  73.9 0.0 copy-start.7
  73.9 3.5 %collective-permute-done.1.refs_2_ = bf16[136,512]{1,0:T(8,128)(2,1)S(1)} collective-permute-done((bf16[136,512]{1,0:T(8,128)(2,1)}, bf16[136,512]{1,0:T(8,128)(2,1)S(1)}, u32[]{:S(2)}, u32[]{:S(2)}) %collective-permute-start.1) | collective-permute-done | bytes 139296 | tf_op jit(solution)/shard_map/ppermute | solution.py:516
  77.4 0.0 copy-done.7
  77.4 0.0 copy-start.8
  77.4 0.6 copy-done.8
  78.1 5.2 %collective-permute-done.2.refs_3_ = bf16[136,512]{1,0:T(8,128)(2,1)} collective-permute-done((bf16[136,512]{1,0:T(8,128)(2,1)}, bf16[136,512]{1,0:T(8,128)(2,1)}, u32[]{:S(2)}, u32[]{:S(2)}) %collective-permute-start.2) | collective-permute-done | bytes 139296 | tf_op jit(solution)/shard_map/ppermute | solution.py:516
  83.3 0.0 all-to-all-done.1
  83.3 0.0 copy-start.3
  83.3 0.9 copy-done.3
  84.2 1.3 shard_map.140
  85.5 9.6 %all_to_all.25.part_ref = bf16[8,32,128]{2,1,0:T(8,128)(2,1)S(1)} all-to-all(bf16[8,32,128]{2,1,0:T(8,128)(2,1)S(1)} %get-tuple-element.31), channel_id=1, replica_groups={{0,1,2,3,4,5,6,7},{8,9,10,11,12,13,14,15},{16,17,18,19,20,21,22,23},{24..., dimensions={0} | all-to-all | bytes 131072 | tf_op jit(solution)/shard_map/all_to_all | solution.py:31
  95.2 20.6 %all_to_all.26.x_ref = bf16[32,32,128]{2,1,0:T(8,128)(2,1)S(1)} all-to-all(bf16[32,32,128]{2,1,0:T(8,128)(2,1)S(1)} %shard_map.141), channel_id=1, replica_groups=mesh['grp'=24,'head'=32] {'head'}, dimensions={0} | all-to-all | bytes 524288 | tf_op jit(solution)/shard_map/all_to_all | solution.py:31
  115.8 0.0 copy-done
  115.8 0.0 copy-done.5
  115.8 0.0 copy-start.2
  115.8 1.9 %copy-done.2 = bf16[2,2048,384]{2,1,0:T(8,128)(2,1)S(1)} copy-done((bf16[2,2048,384]{2,1,0:T(8,128)(2,1)S(1)}, bf16[2,2048,384]{2,1,0:T(8,128)(2,1)}, u32[]{:S(2)}) %copy-start.2) | copy-done | bytes 3145752
  117.7 3.5 %shard_map.142 = (bf16[32,32,128]{2,1,0:T(8,128)(2,1)S(1)}, f32[32,128]{1,0:T(8,128)S(1)}) custom-call(bf16[32,32,128]{2,1,0:T(8,128)(2,1)S(1)} %all_to_all.26.x_ref, f32[64,128]{1,0:T(8,128)S(1)} %get-tuple-element.33.chosen_ref, f32[8,128]{1,0:T(8,128)S(1)} %get-tuple-element.34.mark_ref, f32[1,2048]{1,0:T(1,128)S(1)} %bitcast.14, ...), custom_call_target="tpu_custom_call" | custom-call | tf_op jit(solution)/shard_map/pallas_call | solution.py:44
  121.2 15.8 %all_to_all.27.part_ref = bf16[32,32,128]{2,1,0:T(8,128)(2,1)S(1)} all-to-all(bf16[32,32,128]{2,1,0:T(8,128)(2,1)S(1)} %get-tuple-element.37), channel_id=1, replica_groups=mesh['grp'=24,'head'=32] {'head'}, dimensions={0} | all-to-all | bytes 524288 | tf_op jit(solution)/shard_map/all_to_all | solution.py:31
  137.0 0.7 shard_map.143
  (1 shorter events, 0.0 us)
Async XLA Ops:
  3.7 36.3 %all-to-all-start = ((bf16[24,72,128]{2,1,0:T(8,128)(2,1)}), bf16[24,72,128]{2,1,0:T(8,128)(2,1)S(1)}, u32[]{:S(2)}, u32[]{:S(2)}) async-start(bf16[24,72,128]{2,1,0:T(8,128)(2,1)} %get-tuple-element.25), calls=%async_computation | async-start | bytes 884736 | tf_op jit(solution)/shard_map/all_to_all | solution.py:31
  40.0 0.8 copy-start.6
  40.8 75.0 %copy-start = (bf16[2,2048,384]{2,1,0:T(8,128)(2,1)S(1)}, bf16[2,2048,384]{2,1,0:T(8,128)(2,1)}, u32[]{:S(2)}) copy-start(bf16[2,2048,384]{2,1,0:T(8,128)(2,1)} %gate.1) | copy-start | bytes 9437188
  40.8 75.0 %copy-start.5 = (f32[2048]{0:T(1024)S(1)}, f32[2048]{0:T(1024)}, u32[]{:S(2)}) copy-start(f32[2048]{0:T(1024)} %param.22) | copy-start | bytes 24580
  43.1 1.7 %copy-start.1 = (bf16[2,2048,384]{2,1,0:T(8,128)(2,1)}, bf16[2,2048,384]{2,1,0:T(8,128)(2,1)S(1)}, u32[]{:S(2)}) copy-start(bf16[2,2048,384]{2,1,0:T(8,128)(2,1)S(1)} %get-tuple-element.36.up) | copy-start | bytes 9437188
  44.8 0.6 copy-start.4
  45.4 37.9 %all-to-all-start.1 = ((bf16[32,16,128]{2,1,0:T(8,128)(2,1)}), bf16[32,16,128]{2,1,0:T(8,128)(2,1)S(1)}, u32[]{:S(2)}, u32[]{:S(2)}) async-start(bf16[32,16,128]{2,1,0:T(8,128)(2,1)} %bitcast.13), calls=%async_computation.1 | async-start | bytes 262144 | tf_op jit(solution)/shard_map/all_to_all | solution.py:31
  59.3 14.6 %collective-permute-start = (bf16[136,512]{1,0:T(8,128)(2,1)}, bf16[136,512]{1,0:T(8,128)(2,1)S(1)}, u32[]{:S(2)}, u32[]{:S(2)}) collective-permute-start(bf16[136,512]{1,0:T(8,128)(2,1)} %get-tuple-element.28), channel_id=1, source_target_pairs={{0,8},{1,9},{2,10},{3,11},{4,12},{5,13},{6,14},{7,15},{8,16},{9,17... | collective-permute-start | bytes 417800 | tf_op jit(solution)/shard_map/ppermute | solution.py:516
  63.5 13.9 %collective-permute-start.1 = (bf16[136,512]{1,0:T(8,128)(2,1)}, bf16[136,512]{1,0:T(8,128)(2,1)S(1)}, u32[]{:S(2)}, u32[]{:S(2)}) collective-permute-start(bf16[136,512]{1,0:T(8,128)(2,1)} %get-tuple-element.29), channel_id=1, source_target_pairs={{0,16},{1,17},{2,18},{3,19},{4,20},{5,21},{6,22},{7,23},{8,24},{9,... | collective-permute-start | bytes 417800 | tf_op jit(solution)/shard_map/ppermute | solution.py:516
  68.7 14.5 %collective-permute-start.2 = (bf16[136,512]{1,0:T(8,128)(2,1)}, bf16[136,512]{1,0:T(8,128)(2,1)}, u32[]{:S(2)}, u32[]{:S(2)}) collective-permute-start(bf16[136,512]{1,0:T(8,128)(2,1)} %get-tuple-element.30), channel_id=1, source_target_pairs={{0,24},{1,25},{2,26},{3,27},{4,28},{5,29},{6,30},{7,31},{8,0},{9,1... | collective-permute-start | bytes 417800 | tf_op jit(solution)/shard_map/ppermute | solution.py:516
  73.9 3.5 %copy-start.7 = (bf16[136,512]{1,0:T(8,128)(2,1)}, bf16[136,512]{1,0:T(8,128)(2,1)S(1)}, u32[]{:S(2)}) copy-start(bf16[136,512]{1,0:T(8,128)(2,1)S(1)} %collective-permute-done.refs_1_) | copy-start | bytes 417796
  77.4 0.6 copy-start.8
  83.3 0.9 copy-start.3
  115.8 1.9 %copy-start.2 = (bf16[2,2048,384]{2,1,0:T(8,128)(2,1)S(1)}, bf16[2,2048,384]{2,1,0:T(8,128)(2,1)}, u32[]{:S(2)}) copy-start(bf16[2,2048,384]{2,1,0:T(8,128)(2,1)} %copy-done.1) | copy-start | bytes 9437188

commit v6 on v5

--- a/solution.py
+++ b/solution.py
@@ -140,27 +140,26 @@
 
 
 def pack_body(weight_hbm, residual_hbm, *refs):
-    outs, (weight, residual, extra, extras, sems) = refs[:SPREAD], refs[SPREAD:]
-    depth, width = weight.shape[0], outs[0].shape[1]
+    outs, (residual, extra, extras, sems) = refs[:SPREAD], refs[SPREAD:]
+    depth, width = weight_hbm.shape[0], outs[0].shape[1]
     place = place_of(QUERY_HEADS)
-    load = start_copy(weight_hbm, weight, sems.at[0])
-    small = start_copy(residual_hbm, residual, sems.at[1])
+    small = start_copy(residual_hbm, residual, sems.at[0])
+    starts = [
+        pl.multiple_of(((place + s) & (SPREAD - 1)) * width, width) for s in range(SPREAD)
+    ]
+    copies = [
+        start_copy(
+            weight_hbm.at[:, pl.ds(start, width)], outs[s].at[0:depth, :], sems.at[1 + s]
+        )
+        for s, start in enumerate(starts)
+    ]
+    extra[...] = jnp.zeros(extra.shape, f32)
     small.wait()
-    copies = []
-    starts = []
-    for s in range(SPREAD):
-        start = pl.multiple_of(((place + s) & (SPREAD - 1)) * width, width)
-        starts.append(start)
-        extra[...] = jnp.zeros(extra.shape, f32)
+    for s, start in enumerate(starts):
         extra[0:2, :] = residual[:, pl.ds(start, width)].astype(f32)
         extras[s] = extra[...].astype(bf16)
-        copies.append(
-            start_copy(extras.at[s], outs[s].at[depth : depth + EXTRA_ROWS, :], sems.at[2 + s])
-        )
-    load.wait()
-    for s in range(SPREAD):
-        piece = weight.at[:, pl.ds(starts[s], width)]
-        copies.append(start_copy(piece, outs[s].at[0:depth, :], sems.at[2 + SPREAD + s]))
+        target = outs[s].at[depth : depth + EXTRA_ROWS, :]
+        copies.append(start_copy(extras.at[s], target, sems.at[1 + SPREAD + s]))
     for copy in copies:
         copy.wait()
 
@@ -199,24 +198,18 @@
         )
 
 
-def merge_body(
-    suffix_ref, stat_ref, part_hbm, id_hbm, router_hbm, up_hbm,
-    out_ref, router_ref, up_ref, part_ref, id_ref, rows, heads, sems,
-):
-    pairs = (
-        (part_hbm, part_ref),
-        (id_hbm, id_ref),
-        (router_hbm, router_ref),
-        (up_hbm, up_ref),
-    )
+def merge_body(part_ref, suffix_ref, stat_ref, *refs):
+    count = (len(refs) - 6) // 2
+    sources, (out_ref, *targets) = refs[: 1 + count], refs[1 + count : 2 + 2 * count]
+    id_ref, rows, heads, sems = refs[2 + 2 * count :]
+    pairs = list(zip(sources, (id_ref, *targets)))
     copies = [start_copy(a, b, sems.at[n]) for n, (a, b) in enumerate(pairs)]
     rows[...] = jnp.zeros(rows.shape, f32)
-    copies[0].wait()
-    sources = part_ref.shape[0]
+    part_count = part_ref.shape[0]
     per_dest = suffix_ref.shape[0] // KEY_VALUE_HEADS
     first = KEY_VALUE_HEADS * per_dest
     held = [stat_ref[...]]
-    for g in range(sources):
+    for g in range(part_count):
         both = part_ref[g, first : first + STAT_ROWS, :].astype(f32)
         held.append(both + pltpu.roll(both, LANES - per_dest, 1))
     top = held[0]
@@ -237,7 +230,7 @@
     for k in range(KEY_VALUE_HEADS):
         mine = slice(k * per_dest, (k + 1) * per_dest)
         mixed = turned[:, k : k + 1] * suffix_ref[mine, :]
-        for g in range(sources):
+        for g in range(part_count):
             at = (g + 1) * 8 + k
             mixed = mixed + turned[:, at : at + 1] * part_ref[g, mine, :].astype(f32)
         for i in range(2):
@@ -253,7 +246,7 @@
                 rows[pl.ds(at, near, stride=DEST_ROWS), :] = heads[
                     i * QUERY_HEADS + source : i * QUERY_HEADS + source + near, :
                 ]
-    copies[1].wait()
+    copies[0].wait()
     lane = lax.broadcasted_iota(jnp.int32, (QUERY_HEADS, LANES), 1)
     for i in range(2):
         chosen = lane == id_ref[i : i + 1, 0:1]
@@ -262,7 +255,7 @@
         line = chosen.astype(f32)
         rows[pl.ds(2 * SPREAD + i, QUERY_HEADS, stride=DEST_ROWS), :] = line
     out_ref[...] = rows[...].astype(bf16)
-    for copy in copies[2:]:
+    for copy in copies[1:]:
         copy.wait()
 
 
@@ -400,11 +393,10 @@
         pack_body,
         tuple(pltpu.HBM(dims, bf16) for _ in range(SPREAD)),
         [
-            pltpu.VMEM(weight.shape, bf16),
             pltpu.VMEM(residual.shape, bf16),
             pltpu.VMEM((EXTRA_ROWS, width), f32),
             pltpu.VMEM((SPREAD, EXTRA_ROWS, width), bf16),
-            pltpu.SemaphoreType.DMA((2 + 2 * SPREAD,)),
+            pltpu.SemaphoreType.DMA((1 + 2 * SPREAD,)),
         ],
         weight, residual, hbm=(0, 1), hbm_outs=range(SPREAD),
     )
@@ -424,19 +416,18 @@
     )
 
 
-def merge_parts(suffix, stats, parts, ids, *weights):
+def merge_parts(parts, suffix, stats, ids, *weights):
     dims = (QUERY_HEADS * DEST_ROWS, HEAD_SIZE)
     return kernel_call(
         merge_body,
         (shape(dims, bf16), *(shape(w.shape, bf16) for w in weights)),
         [
-            pltpu.VMEM(parts.shape, bf16),
             pltpu.VMEM(ids.shape, jnp.int32),
             pltpu.VMEM(dims, f32),
             pltpu.VMEM((2 * QUERY_HEADS, HEAD_SIZE), f32),
-            pltpu.SemaphoreType.DMA((2 + len(weights),)),
+            pltpu.SemaphoreType.DMA((1 + len(weights),)),
         ],
-        suffix, stats, parts, ids, *weights, hbm=range(2, 4 + len(weights)),
+        parts, suffix, stats, ids, *weights, hbm=range(3, 4 + len(weights)),
     )
 
 
@@ -514,15 +505,14 @@
     for s in range(1, SPREAD):
         ring = [(h, (h + s * near) % heads) for h in range(heads)]
         pieces[s] = lax.ppermute(pieces[s], "head", ring)
-        pieces[s] = pltpu.with_memory_space_constraint(pieces[s], pltpu.HBM)
     suffix, stats = fill_window(
         suffix_lengths,
         own,
         row_suffix_keys.reshape(-1, row_suffix_keys.shape[-1]),
         row_suffix_values.reshape(-1, row_suffix_values.shape[-1]),
     )
-    attn, router, up = merge_parts(
-        suffix, stats, arrived, expert_ids[0], router_weight.T, up_weights
+    attn, router, up, *pieces = merge_parts(
+        arrived, suffix, stats, expert_ids[0], router_weight.T, up_weights, *pieces
     )
     attn = exchange(attn.reshape(heads, DEST_ROWS, HEAD_SIZE), "head")
     parts, chosen, residual_lines = project(

time: 138 us -> 129 us (0.935)
  waiting for transfers between devices: 26.9 us -> 9.1 us
  Pallas kernels: 14.6 us -> 29.3 us
  starting transfers between devices: 43.5 us -> 30.9 us
  blocking collectives: 46.1 us -> 58.4 us
  local copies, waits for them, and re-layouts: 6.51 us -> 0.66 us
    all_to_all x2 -> x1, waiting for transfers between devices: 18.2 us -> 0.01 us  [exchange(): lax.all_to_all(x, axis, split_axis=0, concat_axis=0, tiled=True, axis_ind...]
    pallas_call x8, Pallas kernels: 14.6 us -> 29.3 us  [kernel_call(): pl.pallas_call(body, out_shape=outs, in_specs=specs, out_specs=tuple((raw...]
    all_to_all x3 -> x4, blocking collectives: 46.1 us -> 58.4 us  [exchange(): lax.all_to_all(x, axis, split_axis=0, concat_axis=0, tiled=True, axis_ind...]
    all_to_all x2 -> x1, starting transfers between devices: 28.9 us -> 16.9 us  [exchange(): lax.all_to_all(x, axis, split_axis=0, concat_axis=0, tiled=True, axis_ind...]
    unnamed x18 -> x10, local copies, waits for them, and re-layouts: 6.51 us -> 0.66 us
  transfers between devices with their start and end apart: 5 -> 4, of which waited for: 3 -> 2; matrix products, arithmetic and copies ran while one was open for 0% -> 0% of each run, Pallas kernels for 2% -> 14%
where the time goes in v6:
time: 129 us; the launch traced here: 128 us
  blocking collectives  58.4 us (45%)
  starting transfers between devices  30.9 us (24%)
  Pallas kernels  29.3 us (23%)
  waiting for transfers between devices  9.1 us (7%)
    all_to_all x4, blocking collectives, exchange(): lax.all_to_all(x, axis, split_axis=0, concat_axis=0, tiled=True, axis_ind...  58.4 us
    pallas_call x8, Pallas kernels, kernel_call(): pl.pallas_call(body, out_shape=outs, in_specs=specs, out_specs=tuple((raw...  29.3 us
    all_to_all x1, starting transfers between devices, exchange(): lax.all_to_all(x, axis, split_axis=0, concat_axis=0, tiled=True, axis_ind...  16.9 us
    ppermute x3, starting transfers between devices, layer(): pieces[s] = lax.ppermute(pieces[s], 'head', ring)  13.9 us
    ppermute x3, waiting for transfers between devices, layer(): pieces[s] = lax.ppermute(pieces[s], 'head', ring)  9.1 us
  transfers between devices with their start and end apart: 4, of which 2 were waited for; matrix products, arithmetic and copies ran while one was open for 0% of the time, Pallas kernels for 14%

profile of v6, /device:TPU:1, one launch (start us, length us, event | category | flops | bytes accessed | tf_op | source)
XLA Modules:
  0.0 128.4 jit_solution(2769791156788834474)
XLA Ops:
  0.0 3.7 %shard_map.136 = (bf16[24,72,128]{2,1,0:T(8,128)(2,1)}, f32[64,128]{1,0:T(8,128)S(1)}, f32[8,128]{1,0:T(8,128)S(1)}) custom-call(bf16[48,4096]{1,0:T(8,128)(2,1)} %bitcast.15, bf16[128,512]{1,0:T(8,128)(2,1)} %bitcast.17, bf16[128,512]{1,0:T(8,128)(2,1)} %bitcast.18), custom_call_target="tpu_custom_call" | custom-call | tf_op jit(solution)/shard_map/pallas_call | solution.py:44
  3.7 16.9 %all-to-all-start = ((bf16[24,72,128]{2,1,0:T(8,128)(2,1)}), bf16[24,72,128]{2,1,0:T(8,128)(2,1)S(1)}, u32[]{:S(2)}, u32[]{:S(2)}) async-start(bf16[24,72,128]{2,1,0:T(8,128)(2,1)} %get-tuple-element.26), calls=%async_computation | async-start | bytes 884736 | tf_op jit(solution)/shard_map/all_to_all | solution.py:31
  20.6 17.1 %shard_map.138 = (bf16[136,512]{1,0:T(8,128)(2,1)}, bf16[136,512]{1,0:T(8,128)(2,1)}, bf16[136,512]{1,0:T(8,128)(2,1)}, bf16[136,512]{1,0:T(8,128)(2,1)}) custom-call(bf16[128,2048]{1,0:T(8,128)(2,1)} %weight_hbm.1, bf16[2,2048]{1,0:T(2,128)(2,1)} %bitcast.21), custom_call_target="tpu_custom_call" | custom-call | tf_op jit(solution)/shard_map/pallas_call | solution.py:44
  37.7 4.2 %collective-permute-start = (bf16[136,512]{1,0:T(8,128)(2,1)}, bf16[136,512]{1,0:T(8,128)(2,1)S(1)}, u32[]{:S(2)}, u32[]{:S(2)}) collective-permute-start(bf16[136,512]{1,0:T(8,128)(2,1)} %get-tuple-element.31), channel_id=1, source_target_pairs={{0,8},{1,9},{2,10},{3,11},{4,12},{5,13},{6,14},{7,15},{8,16},{9,17... | collective-permute-start | bytes 417800 | tf_op jit(solution)/shard_map/ppermute | solution.py:507
  42.0 4.8 %collective-permute-start.1 = (bf16[136,512]{1,0:T(8,128)(2,1)}, bf16[136,512]{1,0:T(8,128)(2,1)S(1)}, u32[]{:S(2)}, u32[]{:S(2)}) collective-permute-start(bf16[136,512]{1,0:T(8,128)(2,1)} %get-tuple-element.32), channel_id=1, source_target_pairs={{0,16},{1,17},{2,18},{3,19},{4,20},{5,21},{6,22},{7,23},{8,24},{9,... | collective-permute-start | bytes 417800 | tf_op jit(solution)/shard_map/ppermute | solution.py:507
  46.7 5.0 %collective-permute-start.2 = (bf16[136,512]{1,0:T(8,128)(2,1)}, bf16[136,512]{1,0:T(8,128)(2,1)S(1)}, u32[]{:S(2)}, u32[]{:S(2)}) collective-permute-start(bf16[136,512]{1,0:T(8,128)(2,1)} %get-tuple-element.33), channel_id=1, source_target_pairs={{0,24},{1,25},{2,26},{3,27},{4,28},{5,29},{6,30},{7,31},{8,0},{9,1... | collective-permute-start | bytes 417800 | tf_op jit(solution)/shard_map/ppermute | solution.py:507
  51.7 1.1 shard_map.137
  52.9 0.0 collective-permute-done.refs_4_
  52.9 0.0 copy-start.2
  52.9 3.2 %collective-permute-done.1.refs_5_ = bf16[136,512]{1,0:T(8,128)(2,1)S(1)} collective-permute-done((bf16[136,512]{1,0:T(8,128)(2,1)}, bf16[136,512]{1,0:T(8,128)(2,1)S(1)}, u32[]{:S(2)}, u32[]{:S(2)}) %collective-permute-start.1) | collective-permute-done | bytes 139296 | tf_op jit(solution)/shard_map/ppermute | solution.py:507
  56.1 0.0 copy-start.3
  56.1 5.9 %collective-permute-done.2.refs_6_ = bf16[136,512]{1,0:T(8,128)(2,1)S(1)} collective-permute-done((bf16[136,512]{1,0:T(8,128)(2,1)}, bf16[136,512]{1,0:T(8,128)(2,1)S(1)}, u32[]{:S(2)}, u32[]{:S(2)}) %collective-permute-start.2) | collective-permute-done | bytes 139296 | tf_op jit(solution)/shard_map/ppermute | solution.py:507
  62.0 0.0 copy-start.4
  62.0 0.0 all-to-all-done.part_ref
  62.0 0.0 copy-done.2
  62.0 0.0 copy-done.3
  62.0 0.6 copy-done.4
  62.6 0.0 copy-start
  62.6 0.0 copy-start.1
  62.7 2.9 %shard_map.139 = (bf16[512,128]{1,0:T(8,128)(2,1)S(1)}, bf16[64,2048]{1,0:T(8,128)(2,1)S(1)}, bf16[2,2048,384]{2,1,0:T(8,128)(2,1)S(1)}, bf16[136,512]{1,0:T(8,1...) custom-call(bf16[24,72,128]{2,1,0:T(8,128)(2,1)S(1)} %all-to-all-done.part_re, ...), custom_call_target="tpu_custom_call" | custom-call | tf_op jit(solution)/shard_map/pallas_call | solution.py:44
  65.6 19.2 %all_to_all.25 = bf16[32,16,128]{2,1,0:T(8,128)(2,1)S(1)} all-to-all(bf16[32,16,128]{2,1,0:T(8,128)(2,1)S(1)} %bitcast.13), channel_id=1, replica_groups=mesh['grp'=24,'head'=32] {'head'}, dimensions={0} | all-to-all | bytes 262144 | tf_op jit(solution)/shard_map/all_to_all | solution.py:31
  84.8 0.3 shard_map.140
  85.1 7.5 %all_to_all.26.part_ref = bf16[8,32,128]{2,1,0:T(8,128)(2,1)S(1)} all-to-all(bf16[8,32,128]{2,1,0:T(8,128)(2,1)S(1)} %get-tuple-element.39), channel_id=1, replica_groups={{0,1,2,3,4,5,6,7},{8,9,10,11,12,13,14,15},{16,17,18,19,20,21,22,23},{24..., dimensions={0} | all-to-all | bytes 131072 | tf_op jit(solution)/shard_map/all_to_all | solution.py:31
  92.6 16.1 %all_to_all.27.x_ref = bf16[32,32,128]{2,1,0:T(8,128)(2,1)S(1)} all-to-all(bf16[32,32,128]{2,1,0:T(8,128)(2,1)S(1)} %shard_map.141), channel_id=1, replica_groups=mesh['grp'=24,'head'=32] {'head'}, dimensions={0} | all-to-all | bytes 524288 | tf_op jit(solution)/shard_map/all_to_all | solution.py:31
  108.7 0.0 copy-done
  108.7 0.0 copy-done.1
  108.7 3.5 %shard_map.142 = (bf16[32,32,128]{2,1,0:T(8,128)(2,1)S(1)}, f32[32,128]{1,0:T(8,128)S(1)}) custom-call(bf16[32,32,128]{2,1,0:T(8,128)(2,1)S(1)} %all_to_all.27.x_ref, f32[64,128]{1,0:T(8,128)S(1)} %get-tuple-element.41.chosen_ref, f32[8,128]{1,0:T(8,128)S(1)} %get-tuple-element.42.mark_ref, f32[1,2048]{1,0:T(1,128)S(1)} %bitcast.14, ...), custom_call_target="tpu_custom_call" | custom-call | tf_op jit(solution)/shard_map/pallas_call | solution.py:44
  112.2 15.5 %all_to_all.28.part_ref = bf16[32,32,128]{2,1,0:T(8,128)(2,1)S(1)} all-to-all(bf16[32,32,128]{2,1,0:T(8,128)(2,1)S(1)} %get-tuple-element.45), channel_id=1, replica_groups=mesh['grp'=24,'head'=32] {'head'}, dimensions={0} | all-to-all | bytes 524288 | tf_op jit(solution)/shard_map/all_to_all | solution.py:31
  127.8 0.7 shard_map.143
  (1 shorter events, 0.0 us)
Async XLA Ops:
  3.7 58.3 %all-to-all-start = ((bf16[24,72,128]{2,1,0:T(8,128)(2,1)}), bf16[24,72,128]{2,1,0:T(8,128)(2,1)S(1)}, u32[]{:S(2)}, u32[]{:S(2)}) async-start(bf16[24,72,128]{2,1,0:T(8,128)(2,1)} %get-tuple-element.26), calls=%async_computation | async-start | bytes 884736 | tf_op jit(solution)/shard_map/all_to_all | solution.py:31
  37.7 15.1 %collective-permute-start = (bf16[136,512]{1,0:T(8,128)(2,1)}, bf16[136,512]{1,0:T(8,128)(2,1)S(1)}, u32[]{:S(2)}, u32[]{:S(2)}) collective-permute-start(bf16[136,512]{1,0:T(8,128)(2,1)} %get-tuple-element.31), channel_id=1, source_target_pairs={{0,8},{1,9},{2,10},{3,11},{4,12},{5,13},{6,14},{7,15},{8,16},{9,17... | collective-permute-start | bytes 417800 | tf_op jit(solution)/shard_map/ppermute | solution.py:507
  42.0 14.1 %collective-permute-start.1 = (bf16[136,512]{1,0:T(8,128)(2,1)}, bf16[136,512]{1,0:T(8,128)(2,1)S(1)}, u32[]{:S(2)}, u32[]{:S(2)}) collective-permute-start(bf16[136,512]{1,0:T(8,128)(2,1)} %get-tuple-element.32), channel_id=1, source_target_pairs={{0,16},{1,17},{2,18},{3,19},{4,20},{5,21},{6,22},{7,23},{8,24},{9,... | collective-permute-start | bytes 417800 | tf_op jit(solution)/shard_map/ppermute | solution.py:507
  46.7 15.3 %collective-permute-start.2 = (bf16[136,512]{1,0:T(8,128)(2,1)}, bf16[136,512]{1,0:T(8,128)(2,1)S(1)}, u32[]{:S(2)}, u32[]{:S(2)}) collective-permute-start(bf16[136,512]{1,0:T(8,128)(2,1)} %get-tuple-element.33), channel_id=1, source_target_pairs={{0,24},{1,25},{2,26},{3,27},{4,28},{5,29},{6,30},{7,31},{8,0},{9,1... | collective-permute-start | bytes 417800 | tf_op jit(solution)/shard_map/ppermute | solution.py:507
  52.9 9.1 %copy-start.2 = (bf16[136,512]{1,0:T(8,128)(2,1)}, bf16[136,512]{1,0:T(8,128)(2,1)S(1)}, u32[]{:S(2)}) copy-start(bf16[136,512]{1,0:T(8,128)(2,1)S(1)} %collective-permute-done.refs_4_) | copy-start | bytes 417796
  56.1 5.9 %copy-start.3 = (bf16[136,512]{1,0:T(8,128)(2,1)}, bf16[136,512]{1,0:T(8,128)(2,1)S(1)}, u32[]{:S(2)}) copy-start(bf16[136,512]{1,0:T(8,128)(2,1)S(1)} %collective-permute-done.1.refs_5_) | copy-start | bytes 417796
  62.0 0.7 copy-start.4
  62.6 46.1 %copy-start = (bf16[2,2048,384]{2,1,0:T(8,128)(2,1)S(1)}, bf16[2,2048,384]{2,1,0:T(8,128)(2,1)}, u32[]{:S(2)}) copy-start(bf16[2,2048,384]{2,1,0:T(8,128)(2,1)} %gate.1) | copy-start | bytes 9437188
  62.6 46.1 %copy-start.1 = (f32[2048]{0:T(1024)S(1)}, f32[2048]{0:T(1024)}, u32[]{:S(2)}) copy-start(f32[2048]{0:T(1024)} %param.22) | copy-start | bytes 24580

commit v7 on v5

--- a/solution.py
+++ b/solution.py
@@ -75,9 +75,11 @@
 
 
 def prefix_body(
-    q_hbm, k_hbm, v_hbm, out_hbm, own_ref, mark_ref,
-    q_in, k_in, v_in, q_rows, stats, rests, made, in_sems, out_sems,
+    q_hbm, k_hbm, v_hbm, weight_hbm, residual_hbm, out_hbm, own_ref, mark_ref, *refs
 ):
+    pieces, refs = refs[:SPREAD], refs[SPREAD:]
+    q_in, k_in, v_in, q_rows, stats, rests, made, in_sems, out_sems = refs[:9]
+    weight, residual, extra, extras, pack_sems = refs[9:]
     rows = q_hbm.shape[0]
     dests = out_hbm.shape[0]
     per_dest = rows * GROUP // dests
@@ -89,6 +91,7 @@
         for k in range(KEY_VALUE_HEADS)
     ]
     values = start_copy(v_hbm, v_in, in_sems.at[KEY_VALUE_HEADS + 1])
+    loads = start_packing(weight_hbm, residual_hbm, weight, residual, pack_sems)
     stats[...] = jnp.zeros(stats.shape, f32)
     rests[...] = jnp.zeros(rests.shape, f32)
     lane = lax.broadcasted_iota(jnp.int32, mark_ref.shape, 1)
@@ -131,6 +134,7 @@
     departures.append(
         start_copy(made.at[:, last, :], out_hbm.at[:, last, :], out_sems.at[KEY_VALUE_HEADS])
     )
+    departures += finish_packing(loads, pieces, weight, residual, extra, extras, pack_sems)
     for copy in departures:
         copy.wait()
 
@@ -139,30 +143,28 @@
     return lax.axis_index("head") // (heads // SPREAD)
 
 
-def pack_body(weight_hbm, residual_hbm, *refs):
-    outs, (weight, residual, extra, extras, sems) = refs[:SPREAD], refs[SPREAD:]
+def start_packing(weight_hbm, residual_hbm, weight, residual, sems):
+    load = start_copy(weight_hbm, weight, sems.at[0])
+    return load, start_copy(residual_hbm, residual, sems.at[1])
+
+
+def finish_packing(loads, outs, weight, residual, extra, extras, sems):
     depth, width = weight.shape[0], outs[0].shape[1]
-    place = place_of(QUERY_HEADS)
-    load = start_copy(weight_hbm, weight, sems.at[0])
-    small = start_copy(residual_hbm, residual, sems.at[1])
-    small.wait()
+    for load in loads:
+        load.wait()
     copies = []
-    starts = []
     for s in range(SPREAD):
-        start = pl.multiple_of(((place + s) & (SPREAD - 1)) * width, width)
-        starts.append(start)
+        start = (place_of(QUERY_HEADS) + s) & (SPREAD - 1)
+        start = pl.multiple_of(start * width, width)
         extra[...] = jnp.zeros(extra.shape, f32)
         extra[0:2, :] = residual[:, pl.ds(start, width)].astype(f32)
         extras[s] = extra[...].astype(bf16)
-        copies.append(
-            start_copy(extras.at[s], outs[s].at[depth : depth + EXTRA_ROWS, :], sems.at[2 + s])
+        pairs = (
+            (extras.at[s], outs[s].at[depth : depth + EXTRA_ROWS, :]),
+            (weight.at[:, pl.ds(start, width)], outs[s].at[0:depth, :]),
         )
-    load.wait()
-    for s in range(SPREAD):
-        piece = weight.at[:, pl.ds(starts[s], width)]
-        copies.append(start_copy(piece, outs[s].at[0:depth, :], sems.at[2 + SPREAD + s]))
-    for copy in copies:
-        copy.wait()
+        copies += [start_copy(a, b, sems.at[2 + 2 * s + n]) for n, (a, b) in enumerate(pairs)]
+    return copies
 
 
 def window_body(
@@ -365,17 +367,19 @@
         out_ref[:, c * LANES : (c + 1) * LANES] = lines[pl.ds(c, 2, stride=blocks), :]
 
 
-def prefix_attention(q, k, v, dests):
+def prefix_attention(q, k, v, weight, residual, dests):
     rows = q.shape[0]
     per_dest = rows * GROUP // dests
     send = (dests, KEY_VALUE_HEADS * per_dest + STAT_ROWS, HEAD_SIZE)
     padded = (rows * GROUP // LANES + 1) * LANES
-    made, own, marks = kernel_call(
+    piece = (weight.shape[0] + EXTRA_ROWS, weight.shape[1] // SPREAD)
+    made, own, marks, *pieces = kernel_call(
         prefix_body,
         (
             pltpu.HBM(send, bf16),
             shape((KEY_VALUE_HEADS * per_dest, HEAD_SIZE), f32),
             shape((8, LANES), f32),
+            *(pltpu.HBM(piece, bf16) for _ in range(SPREAD)),
         ),
         [
             pltpu.VMEM((KEY_VALUE_HEADS, rows, GROUP * HEAD_SIZE), bf16),
@@ -387,27 +391,15 @@
             pltpu.VMEM(send, bf16),
             pltpu.SemaphoreType.DMA((KEY_VALUE_HEADS + 2,)),
             pltpu.SemaphoreType.DMA((KEY_VALUE_HEADS + 1,)),
-        ],
-        q, k, v, hbm=(0, 1, 2), hbm_outs=(0,),
-    )
-    return made, own, marks
-
-
-def pack_weights(weight, residual):
-    width = weight.shape[1] // SPREAD
-    dims = (weight.shape[0] + EXTRA_ROWS, width)
-    return kernel_call(
-        pack_body,
-        tuple(pltpu.HBM(dims, bf16) for _ in range(SPREAD)),
-        [
             pltpu.VMEM(weight.shape, bf16),
             pltpu.VMEM(residual.shape, bf16),
-            pltpu.VMEM((EXTRA_ROWS, width), f32),
-            pltpu.VMEM((SPREAD, EXTRA_ROWS, width), bf16),
+            pltpu.VMEM((EXTRA_ROWS, piece[1]), f32),
+            pltpu.VMEM((SPREAD, EXTRA_ROWS, piece[1]), bf16),
             pltpu.SemaphoreType.DMA((2 + 2 * SPREAD,)),
         ],
-        weight, residual, hbm=(0, 1), hbm_outs=range(SPREAD),
-    )
+        q, k, v, weight, residual, hbm=range(5), hbm_outs=(0, *range(3, 3 + SPREAD)),
+    )
+    return made, own, marks, pieces
 
 
 def fill_window(lengths, own, k, v):
@@ -505,12 +497,16 @@
 ):
     heads = lax.axis_size("head")
     dests = lax.axis_size("grp")
-    send, own, marks = prefix_attention(
-        queries[0], shared_prefix_keys[0], shared_prefix_values[0], dests
+    send, own, marks, pieces = prefix_attention(
+        queries[0],
+        shared_prefix_keys[0],
+        shared_prefix_values[0],
+        out_weight,
+        residual[0],
+        dests,
     )
     arrived = exchange(send, "grp")
     near = heads // SPREAD
-    pieces = list(pack_weights(out_weight, residual[0]))
     for s in range(1, SPREAD):
         ring = [(h, (h + s * near) % heads) for h in range(heads)]
         pieces[s] = lax.ppermute(pieces[s], "head", ring)

time: 138 us -> 136 us (0.986)
  Pallas kernels: 14.6 us -> 13 us
    pallas_call x8 -> x7, Pallas kernels: 14.6 us -> 13 us  [kernel_call(): pl.pallas_call(body, out_shape=outs, in_specs=specs, out_specs=tuple((raw...]
    unnamed x18 -> x16, local copies, waits for them, and re-layouts: 6.51 us -> 5.75 us
  transfers between devices with their start and end apart: 5 -> 5, of which waited for: 3 -> 3; matrix products, arithmetic and copies ran while one was open for 0% -> 0% of each run, Pallas kernels for 2% -> 1%
where the time goes in v7:
time: 136 us; the launch traced here: 135 us
  blocking collectives  46.1 us (34%)
  starting transfers between devices  43.5 us (32%)
  waiting for transfers between devices  26.8 us (20%)
  Pallas kernels  13 us (10%)
  local copies, waits for them, and re-layouts  5.75 us (4%)
    all_to_all x3, blocking collectives, exchange(): lax.all_to_all(x, axis, split_axis=0, concat_axis=0, tiled=True, axis_ind...  46.1 us
    all_to_all x2, starting transfers between devices, exchange(): lax.all_to_all(x, axis, split_axis=0, concat_axis=0, tiled=True, axis_ind...  29 us
    all_to_all x2, waiting for transfers between devices, exchange(): lax.all_to_all(x, axis, split_axis=0, concat_axis=0, tiled=True, axis_ind...  18.1 us
    ppermute x3, starting transfers between devices, layer(): pieces[s] = lax.ppermute(pieces[s], 'head', ring)  14.6 us
    pallas_call x7, Pallas kernels, kernel_call(): pl.pallas_call(body, out_shape=outs, in_specs=specs, out_specs=tuple((raw...  13 us
    ppermute x3, waiting for transfers between devices, layer(): pieces[s] = lax.ppermute(pieces[s], 'head', ring)  8.71 us
    unnamed x16, local copies, waits for them, and re-layouts  5.75 us
  transfers between devices with their start and end apart: 5, of which 3 were waited for; matrix products, arithmetic and copies ran while one was open for 0% of the time, Pallas kernels for 1%

profile of v7, /device:TPU:1, one launch (start us, length us, event | category | flops | bytes accessed | tf_op | source)
XLA Modules:
  0.0 135.3 jit_solution(13110695628783191806)
XLA Ops:
  0.0 4.0 %shard_map.136 = (bf16[24,72,128]{2,1,0:T(8,128)(2,1)}, f32[64,128]{1,0:T(8,128)S(1)}, f32[8,128]{1,0:T(8,128)S(1)}, bf16[136,512]{1,0:T(8,128)(2,1)}, bf16[136,...) custom-call(bf16[48,4096]{1,0:T(8,128)(2,1)} %bitcast.15, bf16[128,512]{1,0:T(8,128)(2,1)} %bitcast.17, ...), custom_call_target="tpu_custom_call" | custom-call | tf_op jit(solution)/shard_map/pallas_call | solution.py:44
  4.1 17.0 %all-to-all-start = ((bf16[24,72,128]{2,1,0:T(8,128)(2,1)}), bf16[24,72,128]{2,1,0:T(8,128)(2,1)}, u32[]{:S(2)}, u32[]{:S(2)}) async-start(bf16[24,72,128]{2,1,0:T(8,128)(2,1)} %get-tuple-element.25), calls=%async_computation | async-start | bytes 884736 | tf_op jit(solution)/shard_map/all_to_all | solution.py:31
  21.1 0.0 copy-start
  21.1 0.0 copy-start.5
  21.1 1.3 shard_map.137
  22.4 18.1 %all-to-all-done.part_hbm = bf16[24,72,128]{2,1,0:T(8,128)(2,1)} async-done(((bf16[24,72,128]{2,1,0:T(8,128)(2,1)}), bf16[24,72,128]{2,1,0:T(8,128)(2,1)}, u32[]{:S(2)}, u32[]{:S(2)}) %all-to-all-start) | async-done | bytes 442400 | tf_op jit(solution)/shard_map/all_to_all | solution.py:31
  40.5 2.2 %shard_map.138 = (bf16[512,128]{1,0:T(8,128)(2,1)S(1)}, bf16[64,2048]{1,0:T(8,128)(2,1)S(1)}, bf16[2,2048,384]{2,1,0:T(8,128)(2,1)S(1)}) custom-call(f32[64,128]{1,0:T(8,128)S(1)} %get-tuple-element.23.suffix_ref, f32[8,128]{1,0:T(8,128)S(1)} %get-tuple-element.24.stat_ref, bf16[24,72,128]{2,1,0:T(8,128)(2,1)} %all-to-all-done.part_hbm, s32[2,8]{1,0:T(2,128)} %bitcast.22, ...), custom_call_target="tpu_custom_call" | custom-call | tf_op jit(solution)/shard_map/pallas_call | solution.py:44
  42.6 0.0 copy-start.1
  42.7 1.6 %copy-done.1 = bf16[2,2048,384]{2,1,0:T(8,128)(2,1)} copy-done((bf16[2,2048,384]{2,1,0:T(8,128)(2,1)}, bf16[2,2048,384]{2,1,0:T(8,128)(2,1)S(1)}, u32[]{:S(2)}) %copy-start.1) | copy-done | bytes 3145752
  44.3 0.0 copy-start.4
  44.3 0.7 copy-done.4
  44.9 12.0 %all-to-all-start.1 = ((bf16[32,16,128]{2,1,0:T(8,128)(2,1)}), bf16[32,16,128]{2,1,0:T(8,128)(2,1)S(1)}, u32[]{:S(2)}, u32[]{:S(2)}) async-start(bf16[32,16,128]{2,1,0:T(8,128)(2,1)} %bitcast.13), calls=%async_computation.1 | async-start | bytes 262144 | tf_op jit(solution)/shard_map/all_to_all | solution.py:31
  56.9 4.2 %collective-permute-start = (bf16[136,512]{1,0:T(8,128)(2,1)}, bf16[136,512]{1,0:T(8,128)(2,1)S(1)}, u32[]{:S(2)}, u32[]{:S(2)}) collective-permute-start(bf16[136,512]{1,0:T(8,128)(2,1)} %get-tuple-element.28), channel_id=1, source_target_pairs={{0,8},{1,9},{2,10},{3,11},{4,12},{5,13},{6,14},{7,15},{8,16},{9,17... | collective-permute-start | bytes 417800 | tf_op jit(solution)/shard_map/ppermute | solution.py:512
  61.1 5.2 %collective-permute-start.1 = (bf16[136,512]{1,0:T(8,128)(2,1)}, bf16[136,512]{1,0:T(8,128)(2,1)S(1)}, u32[]{:S(2)}, u32[]{:S(2)}) collective-permute-start(bf16[136,512]{1,0:T(8,128)(2,1)} %get-tuple-element.29), channel_id=1, source_target_pairs={{0,16},{1,17},{2,18},{3,19},{4,20},{5,21},{6,22},{7,23},{8,24},{9,... | collective-permute-start | bytes 417800 | tf_op jit(solution)/shard_map/ppermute | solution.py:512
  66.3 5.2 %collective-permute-start.2 = (bf16[136,512]{1,0:T(8,128)(2,1)}, bf16[136,512]{1,0:T(8,128)(2,1)}, u32[]{:S(2)}, u32[]{:S(2)}) collective-permute-start(bf16[136,512]{1,0:T(8,128)(2,1)} %get-tuple-element.30), channel_id=1, source_target_pairs={{0,24},{1,25},{2,26},{3,27},{4,28},{5,29},{6,30},{7,31},{8,0},{9,1... | collective-permute-start | bytes 417800 | tf_op jit(solution)/shard_map/ppermute | solution.py:512
  71.5 0.0 collective-permute-done.refs_1_
  71.5 0.0 copy-start.6
  71.5 4.1 %collective-permute-done.1.refs_2_ = bf16[136,512]{1,0:T(8,128)(2,1)S(1)} collective-permute-done((bf16[136,512]{1,0:T(8,128)(2,1)}, bf16[136,512]{1,0:T(8,128)(2,1)S(1)}, u32[]{:S(2)}, u32[]{:S(2)}) %collective-permute-start.1) | collective-permute-done | bytes 139296 | tf_op jit(solution)/shard_map/ppermute | solution.py:512
  75.6 0.0 copy-done.6
  75.6 0.0 copy-start.7
  75.6 0.6 copy-done.7
  76.3 4.6 %collective-permute-done.2.refs_3_ = bf16[136,512]{1,0:T(8,128)(2,1)} collective-permute-done((bf16[136,512]{1,0:T(8,128)(2,1)}, bf16[136,512]{1,0:T(8,128)(2,1)}, u32[]{:S(2)}, u32[]{:S(2)}) %collective-permute-start.2) | collective-permute-done | bytes 139296 | tf_op jit(solution)/shard_map/ppermute | solution.py:512
  80.9 0.0 all-to-all-done.1
  80.9 0.0 copy-start.3
  80.9 0.9 copy-done.3
  81.8 1.3 shard_map.139
  83.1 9.6 %all_to_all.25.part_ref = bf16[8,32,128]{2,1,0:T(8,128)(2,1)S(1)} all-to-all(bf16[8,32,128]{2,1,0:T(8,128)(2,1)S(1)} %get-tuple-element.31), channel_id=1, replica_groups={{0,1,2,3,4,5,6,7},{8,9,10,11,12,13,14,15},{16,17,18,19,20,21,22,23},{24..., dimensions={0} | all-to-all | bytes 131072 | tf_op jit(solution)/shard_map/all_to_all | solution.py:31
  92.8 20.6 %all_to_all.26.x_ref = bf16[32,32,128]{2,1,0:T(8,128)(2,1)S(1)} all-to-all(bf16[32,32,128]{2,1,0:T(8,128)(2,1)S(1)} %shard_map.140), channel_id=1, replica_groups=mesh['grp'=24,'head'=32] {'head'}, dimensions={0} | all-to-all | bytes 524288 | tf_op jit(solution)/shard_map/all_to_all | solution.py:31
  113.4 0.0 copy-done
  113.4 0.0 copy-done.5
  113.4 0.0 copy-start.2
  113.4 1.9 %copy-done.2 = bf16[2,2048,384]{2,1,0:T(8,128)(2,1)S(1)} copy-done((bf16[2,2048,384]{2,1,0:T(8,128)(2,1)S(1)}, bf16[2,2048,384]{2,1,0:T(8,128)(2,1)}, u32[]{:S(2)}) %copy-start.2) | copy-done | bytes 3145752
  115.3 3.5 %shard_map.141 = (bf16[32,32,128]{2,1,0:T(8,128)(2,1)S(1)}, f32[32,128]{1,0:T(8,128)S(1)}) custom-call(bf16[32,32,128]{2,1,0:T(8,128)(2,1)S(1)} %all_to_all.26.x_ref, f32[64,128]{1,0:T(8,128)S(1)} %get-tuple-element.33.chosen_ref, f32[8,128]{1,0:T(8,128)S(1)} %get-tuple-element.34.mark_ref, f32[1,2048]{1,0:T(1,128)S(1)} %bitcast.14, ...), custom_call_target="tpu_custom_call" | custom-call | tf_op jit(solution)/shard_map/pallas_call | solution.py:44
  118.8 15.8 %all_to_all.27.part_ref = bf16[32,32,128]{2,1,0:T(8,128)(2,1)S(1)} all-to-all(bf16[32,32,128]{2,1,0:T(8,128)(2,1)S(1)} %get-tuple-element.37), channel_id=1, replica_groups=mesh['grp'=24,'head'=32] {'head'}, dimensions={0} | all-to-all | bytes 524288 | tf_op jit(solution)/shard_map/all_to_all | solution.py:31
  134.6 0.7 shard_map.142
  (1 shorter events, 0.0 us)
Async XLA Ops:
  4.1 36.4 %all-to-all-start = ((bf16[24,72,128]{2,1,0:T(8,128)(2,1)}), bf16[24,72,128]{2,1,0:T(8,128)(2,1)}, u32[]{:S(2)}, u32[]{:S(2)}) async-start(bf16[24,72,128]{2,1,0:T(8,128)(2,1)} %get-tuple-element.25), calls=%async_computation | async-start | bytes 884736 | tf_op jit(solution)/shard_map/all_to_all | solution.py:31
  21.1 92.3 %copy-start = (bf16[2,2048,384]{2,1,0:T(8,128)(2,1)S(1)}, bf16[2,2048,384]{2,1,0:T(8,128)(2,1)}, u32[]{:S(2)}) copy-start(bf16[2,2048,384]{2,1,0:T(8,128)(2,1)} %gate.1) | copy-start | bytes 9437188
  21.1 92.3 %copy-start.5 = (f32[2048]{0:T(1024)S(1)}, f32[2048]{0:T(1024)}, u32[]{:S(2)}) copy-start(f32[2048]{0:T(1024)} %param.22) | copy-start | bytes 24580
  42.6 1.6 %copy-start.1 = (bf16[2,2048,384]{2,1,0:T(8,128)(2,1)}, bf16[2,2048,384]{2,1,0:T(8,128)(2,1)S(1)}, u32[]{:S(2)}) copy-start(bf16[2,2048,384]{2,1,0:T(8,128)(2,1)S(1)} %get-tuple-element.36.up) | copy-start | bytes 9437188
  44.3 0.7 copy-start.4
  44.9 35.9 %all-to-all-start.1 = ((bf16[32,16,128]{2,1,0:T(8,128)(2,1)}), bf16[32,16,128]{2,1,0:T(8,128)(2,1)S(1)}, u32[]{:S(2)}, u32[]{:S(2)}) async-start(bf16[32,16,128]{2,1,0:T(8,128)(2,1)} %bitcast.13), calls=%async_computation.1 | async-start | bytes 262144 | tf_op jit(solution)/shard_map/all_to_all | solution.py:31
  56.9 14.6 %collective-permute-start = (bf16[136,512]{1,0:T(8,128)(2,1)}, bf16[136,512]{1,0:T(8,128)(2,1)S(1)}, u32[]{:S(2)}, u32[]{:S(2)}) collective-permute-start(bf16[136,512]{1,0:T(8,128)(2,1)} %get-tuple-element.28), channel_id=1, source_target_pairs={{0,8},{1,9},{2,10},{3,11},{4,12},{5,13},{6,14},{7,15},{8,16},{9,17... | collective-permute-start | bytes 417800 | tf_op jit(solution)/shard_map/ppermute | solution.py:512
  61.1 14.6 %collective-permute-start.1 = (bf16[136,512]{1,0:T(8,128)(2,1)}, bf16[136,512]{1,0:T(8,128)(2,1)S(1)}, u32[]{:S(2)}, u32[]{:S(2)}) collective-permute-start(bf16[136,512]{1,0:T(8,128)(2,1)} %get-tuple-element.29), channel_id=1, source_target_pairs={{0,16},{1,17},{2,18},{3,19},{4,20},{5,21},{6,22},{7,23},{8,24},{9,... | collective-permute-start | bytes 417800 | tf_op jit(solution)/shard_map/ppermute | solution.py:512
  66.3 14.5 %collective-permute-start.2 = (bf16[136,512]{1,0:T(8,128)(2,1)}, bf16[136,512]{1,0:T(8,128)(2,1)}, u32[]{:S(2)}, u32[]{:S(2)}) collective-permute-start(bf16[136,512]{1,0:T(8,128)(2,1)} %get-tuple-element.30), channel_id=1, source_target_pairs={{0,24},{1,25},{2,26},{3,27},{4,28},{5,29},{6,30},{7,31},{8,0},{9,1... | collective-permute-start | bytes 417800 | tf_op jit(solution)/shard_map/ppermute | solution.py:512
  71.5 4.1 %copy-start.6 = (bf16[136,512]{1,0:T(8,128)(2,1)}, bf16[136,512]{1,0:T(8,128)(2,1)S(1)}, u32[]{:S(2)}) copy-start(bf16[136,512]{1,0:T(8,128)(2,1)S(1)} %collective-permute-done.refs_1_) | copy-start | bytes 417796
  75.6 0.7 copy-start.7
  80.9 0.9 copy-start.3
  113.4 1.9 %copy-start.2 = (bf16[2,2048,384]{2,1,0:T(8,128)(2,1)S(1)}, bf16[2,2048,384]{2,1,0:T(8,128)(2,1)}, u32[]{:S(2)}) copy-start(bf16[2,2048,384]{2,1,0:T(8,128)(2,1)} %copy-done.1) | copy-start | bytes 9437188
